TPU v7x, 32 devices: a whole 2x2x4 slice. The times are simulated.
32 devices in a mesh: dp: 2 (over x), sp: 4 (over y, core), ctx: 4 (over z).
Axes of the slice: x: 2, y: 2, z: 4, core: 2. Of those that a mesh axis runs over, the one named last changes fastest.
Arguments:
- tokens: bfloat16 [2, 2048, 768], P('dp', ('sp', 'ctx')), may hold values from -6 to 6
- cotangent: bfloat16 [2, 2048, 768], P('dp', ('sp', 'ctx')), may hold values from -6 to 6
- lengths: int32 [2], P('dp'), may hold values from 512 to 2048, as said below
- kept_keys: int32 [2, 4, 512, 12, 64], P('dp', None, 'ctx', 'sp'), may hold values from 0 to 1983, as said below
- first_gain: bfloat16 [768], P('dp'), may hold values from 0.5 to 1.5
- qkv_weight: bfloat16 [768, 2304], P('dp'), may hold values from -0.21875 to 0.21875
- score_weight: bfloat16 [768, 12], P('dp'), may hold values from -0.4375 to 0.4375
- out_weight: bfloat16 [768, 768], P('dp'), may hold values from -1.25 to 1.25
- second_gain: bfloat16 [768], P('dp'), may hold values from 0.5 to 1.5
- fc_weight: bfloat16 [768, 3072], P('dp'), may hold values from -0.21875 to 0.21875
- proj_weight: bfloat16 [3072, 768], P('dp'), may hold values from -0.15625 to 0.15625
Outputs:
- output: bfloat16 [2, 2048, 768], P('dp', ('sp', 'ctx'))
- input_grad: bfloat16 [2, 2048, 768], P('dp', ('sp', 'ctx'))
- first_gain_grad: float32 [768], P('dp')
- qkv_grad: float32 [768, 2304], P('dp')
- score_grad: float32 [768, 12], P('dp')
- out_grad: float32 [768, 768], P('dp')
- second_gain_grad: float32 [768], P('dp')
- fc_grad: float32 [768, 3072], P('dp')
- proj_grad: float32 [3072, 768], P('dp')
Inputs may be any that keep to these rules, and one draw needn't show every extreme that they name: `lengths`: the valid tokens of a slot stand at its start; in every draw some slot is full. `kept_keys`: an entry for the query at position t names a key position of the same slot at most t - 64; where t < 64 the entries are 0 and unused. Positions may repeat.
All inputs are finite; a program needn't handle non-finite values.
Results may differ from a plain program's by a relative error of at most 0.02.
Values may be sent and summed in bfloat16 or wider, within the bound.
No kernel may reach another device: no remote copies, remote signals or barrier semaphores. Data moves between devices by JAX's collectives and lax.ppermute only.
A program may use at most 256 MiB of HBM per device.

v0:
```python
import functools

import jax
import jax.numpy as jnp
from jax import lax
from jax.experimental import pallas as pl
from jax.experimental.pallas import tpu as pltpu
from jax.sharding import PartitionSpec as P

H = 12
HD = 64
WIN = 64
LANES = 128
SLOT = 2048


EPSILON = 1e-05


def layer_norm(values, gain):
    mean_value = jnp.mean(values, axis=-1, keepdims=True)
    centred = values - mean_value
    variance = jnp.mean(centred * centred, axis=-1, keepdims=True)
    return centred * lax.rsqrt(variance + EPSILON) * gain


def tanh_gelu(values):
    return jax.nn.gelu(values, approximate=True)


def contract_rows(left, right):
    return lax.dot_general(
        left, right, (((0,), (0,)), ((), ())), preferred_element_type=jnp.float32
    )


def contract_cols(left, right):
    return lax.dot_general(
        left, right, (((1,), (1,)), ((), ())), preferred_element_type=jnp.float32
    )


NT = (((1,), (1,)), ((), ()))


PAD_ROWS = 16


def slot_order(src_ref, kv_ref):
    count, height, _ = src_ref.shape
    for tile in range(kv_ref.shape[0] // LANES):
        part, at = divmod(tile, count)
        kv_ref[tile * LANES : (tile + 1) * LANES, :] = src_ref[at, part * LANES : (part + 1) * LANES, :]


def slot_gates(src_ref, gate_ref):
    count, height, _ = src_ref.shape
    for at in range(count):
        scores = src_ref[at, height - PAD_ROWS :, :].astype(jnp.float32)
        gates = -jnp.log1p(jnp.exp(-scores))
        for part in range(gate_ref.shape[1] // LANES // count):
            tile = part * count + at
            gate_ref[:, tile * LANES : (tile + 1) * LANES] = jnp.broadcast_to(gates[part : part + 1, :], (8, LANES))


def attend_body(first, tiles, base, idx_ref, q_ref, src_ref, out_ref, prob_ref, score_ref, pair_ref, kv_ref, gate_ref):
    rows = q_ref.shape[0]
    if first:
        slot_order(src_ref, kv_ref)
        slot_gates(src_ref, gate_ref)
    span = tiles * LANES
    f32, bf16 = jnp.float32, jnp.bfloat16
    score_ref[:, :span] = (
        lax.dot_general(q_ref[...], kv_ref[:span, :], NT, preferred_element_type=f32) * HD ** (-0.5)
        + gate_ref[0:1, :span]
    )
    kept = idx_ref[0, 0]
    pair_ref[...] = jnp.concatenate([kept, kept], axis=1)
    wide = 8 * HD
    sub = lax.broadcasted_iota(jnp.int32, (8, wide), 0)
    lane = lax.broadcasted_iota(jnp.int32, (8, wide), 1)
    own = (lane // HD) == sub
    subf = sub.astype(f32)
    ahead = lax.broadcasted_iota(jnp.int32, (8, LANES), 0) - lax.broadcasted_iota(jnp.int32, (8, LANES), 1)
    near_from = max(0, tiles - 5)

    def eight(start):
        four = pair_ref[pl.ds(start, 8), :]
        index = jnp.concatenate([four] * 4, axis=1)
        pos = base + start + sub
        high = jnp.where(own & (pos >= WIN), index >> 7, -2).astype(f32)
        low = jnp.sum(jnp.where(own, (index & 127).astype(f32), 0.0), axis=0, keepdims=True) - subf
        high_pair = jnp.concatenate([high, high - 1.0], axis=0).astype(bf16)
        low_pair = jnp.concatenate([low, low - 8.0], axis=0).astype(bf16)
        one, zero = jnp.ones((), bf16), jnp.zeros((), bf16)
        left = jnp.concatenate(
            [jnp.where(high_pair == jnp.array(2 * p, bf16), one, zero) for p in range(tiles // 2)], axis=0
        )
        right = jnp.concatenate(
            [jnp.where(low_pair == jnp.array(16 * p, bf16), one, zero) for p in range(8)], axis=0
        )
        count = lax.dot_general(left, right, NT, preferred_element_type=f32)
        gap = ahead + (base + start)
        masked, counts = [], []
        largest = None
        for tile in range(tiles):
            number = count[8 * tile : 8 * tile + 8, :]
            if tile >= near_from:
                far = gap - tile * LANES
                number = number + jnp.where((far >= 0) & (far < WIN), 1.0, 0.0)
            value = jnp.where(number > 0.0, score_ref[pl.ds(start, 8), tile * LANES : (tile + 1) * LANES], -1e30)
            counts.append(number)
            masked.append(value)
            largest = value if largest is None else jnp.maximum(largest, value)
        top = jnp.max(largest, axis=1, keepdims=True)
        total = None
        expos = []
        for number, value in zip(counts, masked):
            expo = jnp.exp(value - top) * number
            expos.append(expo)
            total = expo if total is None else total + expo
        inverse = 1.0 / jnp.sum(total, axis=1, keepdims=True)
        return [expo * inverse for expo in expos]

    def step(index, carry):
        start = pl.multiple_of(index * 16, 16)
        first, second = eight(start), eight(start + 8)
        for tile in range(tiles):
            prob_ref[0, 0, pl.ds(start, 16), tile * LANES : (tile + 1) * LANES] = jnp.concatenate(
                [first[tile], second[tile]], axis=0
            ).astype(bf16)
        return carry

    lax.fori_loop(0, rows // 16, step, 0)
    both = jnp.dot(prob_ref[0, 0, :, :span], kv_ref[:span, :], preferred_element_type=f32)
    out_ref[0] = both[:, HD:].astype(bf16)


def attend_kernel(parts, chunk, base_ref, *refs):
    part = pl.program_id(1)
    base = base_ref[0] + part * chunk
    for at in range(parts):
        pl.when(part == at)(
            functools.partial(attend_body, at == 0, (at + 1) * chunk // LANES, base, *refs)
        )


def attend(base, kept, query, pairs):
    heads, parts, block, keep = kept.shape
    count, height, _ = pairs.shape
    slot = count * (height - PAD_ROWS)
    chunk = slot // parts
    grid_spec = pltpu.PrefetchScalarGridSpec(
        num_scalar_prefetch=1,
        grid=(heads, parts),
        in_specs=[
            pl.BlockSpec((1, 1, block, keep), lambda h, r, b: (h, r, 0, 0)),
            pl.BlockSpec((block, LANES), lambda h, r, b: (r, h)),
            pl.BlockSpec((count, height, LANES), lambda h, r, b: (0, 0, h)),
        ],
        out_specs=[
            pl.BlockSpec((1, block, HD), lambda h, r, b: (h, r, 0)),
            pl.BlockSpec((1, 1, block, slot), lambda h, r, b: (h, r, 0, 0)),
        ],
        scratch_shapes=[
            pltpu.VMEM((block, slot), jnp.float32),
            pltpu.VMEM((block, 2 * keep), jnp.int32),
            pltpu.VMEM((slot, LANES), jnp.bfloat16),
            pltpu.VMEM((8, slot), jnp.float32),
        ],
    )
    return pl.pallas_call(
        functools.partial(attend_kernel, parts, chunk),
        grid_spec=grid_spec,
        out_shape=[
            jax.ShapeDtypeStruct((heads, parts * block, HD), jnp.bfloat16),
            jax.ShapeDtypeStruct((heads, parts, block, slot), jnp.bfloat16),
        ],
        name="attend",
    )(base, kept, query, pairs)


def attend_back_body(first, last, tiles, chunk, q_ref, grad_ref, src_ref, prob_ref, dq_ref, out_ref, raw_ref, kv_ref, dkv_ref, gate_ref):
    f32, bf16 = jnp.float32, jnp.bfloat16
    rows = q_ref.shape[0]
    steps = tiles * LANES // chunk
    if first:
        slot_order(src_ref, kv_ref)
        dkv_ref[...] = jnp.zeros_like(dkv_ref)
        gate_ref[...] = jnp.zeros_like(gate_ref)
    dot_sum = None
    for at in range(steps):
        cols = slice(at * chunk, (at + 1) * chunk)
        raw = lax.dot_general(grad_ref[...], kv_ref[cols, :], NT, preferred_element_type=f32)
        raw_ref[:, cols] = raw
        part = jnp.sum(raw * prob_ref[0, 0, :, cols].astype(f32), axis=1, keepdims=True)
        dot_sum = part if dot_sum is None else dot_sum + part
    lane = lax.broadcasted_iota(jnp.int32, (rows, LANES), 1)
    scaled = jnp.where(lane == HD, 1.0, q_ref[...].astype(f32) * HD ** (-0.5))
    query_t = jnp.transpose(scaled)[: HD + 16].astype(bf16)
    grad_t = jnp.transpose(grad_ref[...].astype(f32))[HD:].astype(bf16)
    dq = None
    for at in range(steps):
        cols = slice(at * chunk, (at + 1) * chunk)
        prob = prob_ref[0, 0, :, cols]
        grad_score = (prob.astype(f32) * (raw_ref[:, cols] - dot_sum)).astype(bf16)
        piece = jnp.dot(grad_score, kv_ref[cols, :], preferred_element_type=f32)
        dq = piece if dq is None else dq + piece
        keys = jnp.dot(query_t, grad_score, preferred_element_type=f32)
        dkv_ref[:HD, cols] += keys[:HD]
        gate_ref[:, cols] += keys[HD : HD + 8]
        dkv_ref[HD:, cols] += jnp.dot(grad_t, prob, preferred_element_type=f32)
    dq_ref[...] = (dq * HD ** (-0.5)).astype(dq_ref.dtype)
    if last:
        count, height, _ = out_ref.shape
        parts = (height - PAD_ROWS) // LANES
        for at in range(count):
            rows_of = []
            for part in range(parts):
                cols = slice((part * count + at) * LANES, (part * count + at + 1) * LANES)
                out_ref[at, part * LANES : (part + 1) * LANES, :] = jnp.transpose(dkv_ref[:, cols]).astype(bf16)
                rows_of.append(gate_ref[0:1, cols])
            rows_of.append(jnp.zeros((PAD_ROWS - parts, LANES), f32))
            out_ref[at, height - PAD_ROWS :, :] = jnp.concatenate(rows_of, axis=0).astype(bf16)


def attend_back_kernel(parts, chunk, *refs):
    part = pl.program_id(1)
    for at in range(parts):
        pl.when(part == at)(
            functools.partial(attend_back_body, at == 0, at == parts - 1, (at + 1) * chunk // LANES, chunk, *refs)
        )


def attend_back(query, grad, pairs, prob):
    heads, parts, block, slot = prob.shape
    count, height, width = pairs.shape
    chunk = slot // parts
    return pl.pallas_call(
        functools.partial(attend_back_kernel, parts, chunk),
        grid=(heads, parts),
        in_specs=[
            pl.BlockSpec((block, LANES), lambda h, r: (r, h)),
            pl.BlockSpec((block, LANES), lambda h, r: (r, h)),
            pl.BlockSpec((count, height, LANES), lambda h, r: (0, 0, h)),
            pl.BlockSpec((1, 1, block, slot), lambda h, r: (h, r, 0, 0)),
        ],
        out_specs=[
            pl.BlockSpec((block, LANES), lambda h, r: (r, h)),
            pl.BlockSpec((count, height, LANES), lambda h, r: (0, 0, h)),
        ],
        out_shape=[
            jax.ShapeDtypeStruct((parts * block, heads * LANES), jnp.bfloat16),
            jax.ShapeDtypeStruct((count, height, width), jnp.bfloat16),
        ],
        scratch_shapes=[
            pltpu.VMEM((block, slot), jnp.float32),
            pltpu.VMEM((slot, LANES), jnp.bfloat16),
            pltpu.VMEM((LANES, slot), jnp.float32),
            pltpu.VMEM((8, slot), jnp.float32),
        ],
        name="attend_back",
    )(query, grad, pairs, prob)


def finish_kernel(heads, norm_ref, pair_ref, dq_ref, score_ref, in_ref, gain_ref, small_ref, grad_ref):
    f32, bf16 = jnp.float32, jnp.bfloat16
    group = norm_ref.shape[1]
    parts = group // LANES
    wide = in_ref.shape[1]
    gates = pair_ref[group:, :].astype(f32)
    total = jnp.concatenate(
        [
            jnp.concatenate([gates[at : at + 1, head * LANES : (head + 1) * LANES] for at in range(parts)], axis=1)
            for head in range(heads)
        ],
        axis=0,
    )
    total = total * jax.nn.sigmoid(-score_ref[...].astype(f32))
    scores = jnp.transpose(jnp.concatenate([total, jnp.zeros((LANES - heads, group), f32)], axis=0))
    rest = wide - heads * 3 * HD
    columns = jnp.concatenate(
        [pair_ref[:group, :].astype(f32)]
        + [dq_ref[:, head * LANES : head * LANES + HD].astype(f32) for head in range(heads)]
        + [scores[:, :rest]],
        axis=1,
    ).astype(bf16)
    small = jnp.dot(norm_ref[...], columns, preferred_element_type=f32)
    gain_grad = jnp.sum(small * in_ref[...].astype(f32), axis=1, keepdims=True) / gain_ref[:, 0:1]
    lane = lax.broadcasted_iota(jnp.int32, small.shape, 1)
    at = heads * 3 * HD + heads
    small = jnp.where(lane == at, gain_grad, jnp.where(lane == at + 1, gain_ref[:, 1:2], small))
    small_ref[...] = small.astype(bf16)
    grad_ref[...] = lax.dot_general(columns, in_ref[...], NT, preferred_element_type=f32).astype(bf16)


def finish(norm_t, pair, dq, score, weights, gains):
    width, group = norm_t.shape
    heads = score.shape[0]
    return pl.pallas_call(
        functools.partial(finish_kernel, heads),
        out_shape=[
            jax.ShapeDtypeStruct(weights.shape, jnp.bfloat16),
            jax.ShapeDtypeStruct((group, width), jnp.bfloat16),
        ],
        name="finish",
    )(norm_t, pair, dq, score, weights, gains)


def unpack_kernel(groups, heads, small_ref, qkv_ref, score_ref):
    keys = heads * 2 * HD
    for at in range(groups):
        values = small_ref[at].astype(jnp.float32)
        for head in range(heads):
            start = (at * heads + head) * 3 * HD
            qkv_ref[:, start : start + HD] = values[:, keys + head * HD : keys + (head + 1) * HD]
            qkv_ref[:, start + HD : start + 3 * HD] = values[:, head * 2 * HD : (head + 1) * 2 * HD]
        score_ref[:, at * heads : (at + 1) * heads] = values[:, keys + heads * HD : keys + heads * HD + heads]


def unpack(small, heads):
    groups, rows, width = small.shape
    block = 96 if rows % 96 == 0 else rows
    return pl.pallas_call(
        functools.partial(unpack_kernel, groups, heads),
        grid=(rows // block,),
        in_specs=[pl.BlockSpec((groups, block, width), lambda r: (0, r, 0))],
        out_specs=[
            pl.BlockSpec((block, groups * heads * 3 * HD), lambda r: (r, 0)),
            pl.BlockSpec((block, groups * heads), lambda r: (r, 0)),
        ],
        out_shape=[
            jax.ShapeDtypeStruct((rows, groups * heads * 3 * HD), jnp.float32),
            jax.ShapeDtypeStruct((rows, groups * heads), jnp.float32),
        ],
        name="unpack",
    )(small)


def arrange_kernel(heads, rows, qkv_ref, score_ref, gains_ref, out_ref):
    f32 = jnp.float32
    values = qkv_ref[...].astype(f32)
    keys = heads * 2 * HD
    width = out_ref.shape[1]
    pieces = [values[:, (3 * head + 1) * HD : (3 * head + 3) * HD] for head in range(heads)]
    pieces += [values[:, 3 * head * HD : (3 * head + 1) * HD] for head in range(heads)]
    pieces += [score_ref[...].astype(f32), jnp.zeros((rows, width - heads * 3 * HD - heads), f32)]
    out_ref[:rows, :] = jnp.concatenate(pieces, axis=1).astype(out_ref.dtype)
    out_ref[rows:, :] = jnp.concatenate(
        [gains_ref[...].astype(f32), jnp.zeros((gains_ref.shape[0], width - rows), f32)], axis=1
    ).astype(out_ref.dtype)


def arrange(qkv, score, gains, width):
    rows, heads = score.shape
    return pl.pallas_call(
        functools.partial(arrange_kernel, heads, rows),
        out_shape=jax.ShapeDtypeStruct((rows + PAD_ROWS, width), qkv.dtype),
        name="arrange",
    )(qkv, score, gains)


def dp_send(mine):
    if lax.axis_size("dp") != 2:
        return lax.all_gather(mine, "dp", axis=0, tiled=True)
    return lax.ppermute(mine, "dp", [(0, 1), (1, 0)])


def dp_join(mine, came):
    if lax.axis_size("dp") != 2:
        return came
    return jnp.where(
        lax.axis_index("dp") == 0, jnp.concatenate([mine, came]), jnp.concatenate([came, mine])
    )


def dp_scatter(parts):
    if lax.axis_size("dp") != 2:
        return lax.psum_scatter(parts, "dp", scatter_dimension=0, tiled=False)
    at = lax.axis_index("dp")
    mine = lax.dynamic_index_in_dim(parts, at, 0, keepdims=False)
    sent = lax.dynamic_index_in_dim(parts, 1 - at, 0, keepdims=False)
    other = lax.ppermute(sent, "dp", [(0, 1), (1, 0)])
    return (mine.astype(jnp.float32) + other.astype(jnp.float32)).astype(parts.dtype)


def group_rows_of(mine, group, count):
    height = mine.shape[0]
    if lax.axis_size("dp") != 2 or height % count != 0:
        whole = lax.all_gather(mine, "dp", axis=0, tiled=True)
        return lax.dynamic_slice_in_dim(whole, group * count, count, 0)
    near = lax.dynamic_slice_in_dim(mine, group * count % height, count, 0)
    far = lax.ppermute(near, "dp", [(0, 1), (1, 0)])
    return jnp.where(lax.axis_index("dp") == group * count // height, near, far)


def dp_sum(mine):
    if lax.axis_size("dp") != 2:
        return lax.psum(mine, "dp")
    other = lax.ppermute(mine, "dp", [(0, 1), (1, 0)])
    return (mine.astype(jnp.float32) + other.astype(jnp.float32)).astype(mine.dtype)


def exchange_sum(parts, axis):
    came = lax.all_to_all(parts, axis, split_axis=0, concat_axis=0, tiled=True)
    return jnp.sum(came.astype(jnp.float32), axis=0)


def per_device(
    tokens,
    cotangent,
    lengths,
    kept_keys,
    first_gain,
    qkv_weight,
    score_weight,
    out_weight,
    second_gain,
    fc_weight,
    proj_weight,
):
    f32, bf16 = jnp.float32, jnp.bfloat16
    dp_count = lax.axis_size("dp")
    seg_count = lax.axis_size("sp")
    ctx_count = lax.axis_size("ctx")
    dp_at = lax.axis_index("dp")
    sp_at = lax.axis_index("sp")
    ctx_at = lax.axis_index("ctx")
    rows = tokens.shape[1]
    width = tokens.shape[2]
    group_rows = seg_count * rows
    heads = H // seg_count
    head_cols = heads * 3 * HD
    hidden = fc_weight.shape[1]
    hidden_part = hidden // (dp_count * seg_count)
    piece = width // (dp_count * ctx_count)

    keys = heads * 2 * HD
    wide = -(-(head_cols + heads + 2) // LANES) * LANES
    weight_rows = width // dp_count
    own_in = arrange(
        lax.dynamic_slice_in_dim(qkv_weight, sp_at * head_cols, head_cols, 1),
        lax.dynamic_slice_in_dim(score_weight, sp_at * heads, heads, 1),
        jnp.pad(jnp.stack([first_gain, second_gain]), ((0, PAD_ROWS - 2), (0, 0))),
        wide,
    )
    if dp_count == 2:
        other_in = lax.ppermute(own_in, "dp", [(0, 1), (1, 0)])
        parts_in = [
            jnp.where(dp_at == at, own_in, other_in) for at in range(dp_count)
        ]
    else:
        parts_in = list(lax.all_gather(own_in, "dp", axis=0, tiled=False))
    tokens_group = lax.all_gather(tokens[0], "sp", axis=0, tiled=True)
    all_in = jnp.concatenate([part[:weight_rows] for part in parts_in])
    gain_one = jnp.concatenate([part[weight_rows, :weight_rows] for part in parts_in]).astype(f32)
    gain_two = jnp.concatenate([part[weight_rows + 1, :weight_rows] for part in parts_in]).astype(f32)

    fc_own = jnp.concatenate(
        [
            lax.dynamic_slice_in_dim(fc_weight, (at * seg_count + sp_at) * hidden_part, hidden_part, 1)
            for at in range(dp_count)
        ],
        axis=1,
    )
    proj_own = lax.dynamic_slice_in_dim(proj_weight, sp_at * hidden_part, hidden_part, 0)
    all_in, out_own, fc_own, proj_own = lax.optimization_barrier((all_in, out_weight, fc_own, proj_own))
    out_part = group_rows_of(out_own, sp_at, heads * HD)
    fc_came = dp_send(fc_own)
    proj_came = dp_send(proj_own)

    inputs = tokens[0].astype(f32)
    inputs_group = tokens_group.astype(f32)
    norm_one = layer_norm(inputs_group, gain_one).astype(bf16)
    qkv_rows = jnp.dot(norm_one, all_in, preferred_element_type=f32).astype(bf16)
    score_weight_part = all_in[:, head_cols : head_cols + heads]
    key_score = lax.dot_general(
        score_weight_part, norm_one, (((0,), (1,)), ((), ())), preferred_element_type=f32
    ).astype(bf16)
    score_rows = jnp.transpose(key_score.reshape(heads, seg_count, rows), (1, 0, 2)).reshape(
        seg_count, heads * rows
    )
    pairs_own = jnp.concatenate(
        [qkv_rows[:, :keys], jnp.pad(score_rows, ((0, PAD_ROWS - seg_count), (0, 0)))], axis=0
    )
    query_wide = jnp.pad(
        qkv_rows[:, keys:head_cols].reshape(group_rows, heads, HD), ((0, 0), (0, 0), (0, HD))
    ).reshape(group_rows, heads * LANES)
    kept = jnp.transpose(kept_keys[0], (2, 0, 1, 3))
    base = (ctx_at * rows).astype(jnp.int32)[None]
    cot_own, pairs_own = lax.optimization_barrier((cotangent[0], pairs_own))
    cot_group = lax.all_gather(cot_own, "sp", axis=0, tiled=True)
    pairs = lax.all_gather(pairs_own, "ctx", axis=0, tiled=False)
    query_wide, cot_group, out_part, fc_came, proj_came = lax.optimization_barrier(
        (query_wide, cot_group, out_part, fc_came, proj_came)
    )
    head_outs, prob = attend(base, kept, query_wide, pairs)
    attended = jnp.transpose(head_outs, (1, 0, 2)).reshape(group_rows, heads * HD)
    fc_part = dp_join(fc_own, fc_came)
    proj_part = dp_join(proj_own, proj_came)

    group_at = jnp.arange(group_rows, dtype=jnp.int32)
    group_positions = (group_at // rows) * (ctx_count * rows) + ctx_at * rows + group_at % rows
    grad_out_group = jnp.where((group_positions < lengths[0])[:, None], cot_group, jnp.zeros_like(cot_group))
    positions = (sp_at * ctx_count + ctx_at) * rows + jnp.arange(rows, dtype=jnp.int32)
    is_valid = (positions < lengths[0])[:, None]

    branch = jnp.dot(attended, out_part, preferred_element_type=f32).astype(bf16)
    mixed = inputs + exchange_sum(branch.reshape(seg_count, rows, width), "sp")
    norm_two_own = layer_norm(mixed, gain_two).astype(bf16)
    norm_two = lax.all_gather(norm_two_own, "sp", axis=0, tiled=True)
    hidden_pre = jnp.dot(norm_two, fc_part, preferred_element_type=f32)
    active = tanh_gelu(hidden_pre).astype(bf16)
    grad_active = contract_cols(grad_out_group, proj_part)
    _, gelu_pull = jax.vjp(tanh_gelu, hidden_pre)
    grad_pre = gelu_pull(grad_active)[0].astype(bf16)
    fc_parts = contract_rows(norm_two, grad_pre).astype(bf16).reshape(dp_count, ctx_count, piece, width)
    proj_parts = contract_rows(active, grad_out_group).astype(bf16).reshape(dp_count, ctx_count, -1, width)
    grad_pre, fc_parts, proj_parts = lax.optimization_barrier((grad_pre, fc_parts, proj_parts))
    fc_dp = dp_scatter(fc_parts)
    proj_dp = dp_scatter(proj_parts)
    grad_norm_parts = contract_cols(grad_pre, fc_part).astype(bf16)
    grad_norm_two = exchange_sum(grad_norm_parts.reshape(seg_count, rows, width), "sp")
    _, second_pull = jax.vjp(layer_norm, mixed, gain_two)
    grad_mixed_norm, second_gain_grad = second_pull(grad_norm_two)
    grad_out = jnp.where(is_valid, cotangent[0], jnp.zeros_like(cotangent[0])).astype(f32)
    grad_mixed = grad_out + grad_mixed_norm
    grad_branch = lax.all_gather(grad_mixed.astype(bf16), "sp", axis=0, tiled=True)

    out_wide = jnp.pad(out_part.reshape(heads, HD, width), ((0, 0), (HD, 0), (0, 0))).reshape(heads * LANES, width)
    grad_wide = contract_cols(grad_branch, out_wide).astype(bf16)
    out_mine = contract_rows(attended, grad_branch).astype(bf16)
    grad_wide, fc_dp, out_mine = lax.optimization_barrier((grad_wide, fc_dp, out_mine))
    out_sum = dp_sum(out_mine)
    fc_came = lax.all_to_all(fc_dp, "ctx", split_axis=0, concat_axis=0, tiled=True)
    query_grads, pair_grads = attend_back(query_wide, grad_wide, pairs, prob)
    query_grads, pair_grads, fc_came, proj_dp, out_sum = lax.optimization_barrier(
        (query_grads, pair_grads, fc_came, proj_dp, out_sum)
    )
    pair_mine = lax.psum_scatter(pair_grads, "ctx", scatter_dimension=0, tiled=False)
    late = jnp.concatenate([proj_dp, out_sum.reshape(ctx_count, -1, width)], axis=1)

    def total(came):
        return jnp.sum(came.astype(f32), axis=0).astype(bf16)

    late, active_late = lax.optimization_barrier((late, active))
    late_came = lax.all_to_all(late, "ctx", split_axis=0, concat_axis=0, tiled=True)
    expanded = exchange_sum(
        jnp.dot(active_late, proj_part, preferred_element_type=f32).astype(bf16).reshape(seg_count, rows, width), "sp"
    )
    big = jnp.concatenate([total(fc_came), total(late_came)], axis=0)
    norm_t = jnp.transpose(norm_one)
    gain_cols = jnp.stack([gain_one, second_gain_grad], axis=1)
    pair_mine, big, expanded, norm_t, gain_cols = lax.optimization_barrier(
        (pair_mine, big, expanded, norm_t, gain_cols)
    )
    output = jnp.where(is_valid, mixed + expanded, 0.0).astype(bf16)[None]
    big_all = lax.all_gather(big, ("sp", "ctx"), axis=0, tiled=False).reshape(seg_count, ctx_count, -1, width)
    proj_piece = hidden // (seg_count * dp_count * ctx_count)
    both = piece + proj_piece

    small, grad_norm_part = finish(norm_t, pair_mine, query_grads, key_score, all_in, gain_cols)
    small_own = exchange_sum(
        dp_scatter(small.reshape(dp_count, ctx_count, piece, wide)), "ctx"
    ).astype(bf16)
    small_own, big_all, grad_norm_part = lax.optimization_barrier((small_own, big_all, grad_norm_part))
    grad_norm_one = exchange_sum(grad_norm_part.reshape(seg_count, rows, width), "sp")
    _, first_pull = jax.vjp(lambda values: layer_norm(values, gain_one), inputs)
    grad_input_norm = first_pull(grad_norm_one)[0]
    input_grad = (grad_mixed + grad_input_norm).astype(bf16)[None]

    small_all = lax.all_gather(small_own, ("sp", "ctx"), axis=0, tiled=False).reshape(
        seg_count, ctx_count * piece, wide
    )
    groups = range(seg_count)
    fc_grad = jnp.concatenate(
        [
            big_all[at, :, :piece, part * hidden_part : (part + 1) * hidden_part].reshape(-1, hidden_part)
            for part in range(dp_count)
            for at in groups
        ],
        axis=1,
    ).astype(f32)
    proj_grad = big_all[:, :, piece:both].reshape(hidden // dp_count, width).astype(f32)
    out_grad = lax.dynamic_slice_in_dim(
        big_all[:, :, both:].reshape(width, width), dp_at * (width // dp_count), width // dp_count, 0
    ).astype(f32)
    qkv_grad, score_grad = unpack(small_all, heads)
    gains = jnp.sum(small_all[:, :, head_cols + heads : head_cols + heads + 2].astype(f32), axis=0)
    return (output, input_grad, gains[:, 0], qkv_grad, score_grad, out_grad, gains[:, 1], fc_grad, proj_grad)


def solution(mesh):
    placed = (
        P("dp", ("sp", "ctx"), None),
        P("dp", ("sp", "ctx"), None),
        P("dp"),
        P("dp", None, "ctx", "sp", None),
        P("dp"),
        P("dp", None),
        P("dp", None),
        P("dp", None),
        P("dp"),
        P("dp", None),
        P("dp", None),
    )
    return jax.shard_map(
        per_device,
        mesh=mesh,
        in_specs=placed,
        out_specs=(
            P("dp", ("sp", "ctx"), None),
            P("dp", ("sp", "ctx"), None),
            P("dp"),
            P("dp", None),
            P("dp", None),
            P("dp", None),
            P("dp"),
            P("dp", None),
            P("dp", None),
        ),
        check_vma=False,
    )
```

profile of v0, /device:TPU:0, one launch (start us, length us, event | category | flops | bytes accessed | tf_op | source)
XLA Modules:
  0.0 390.7 jit_solution(5543292407045158778)
XLA Ops:
  14.0 3.0 collective-permute-start
  17.1 8.6 %all-gather = bf16[1,512,768]{1,2,0:T(8,128)(2,1)S(1)} all-gather(bf16[1,128,768]{1,2,0:T(8,128)(2,1)S(1)} %copy.36), channel_id=2, replica_groups=mesh['dp'=2,'sp'=4,'ctx'=4] {'sp'}, dimensions={1}, use_global_device_ids=true | all-gather | bytes 983040 | tf_op jit(solution)/shard_map/all_gather | solution.py:454
  38.5 9.1 %all_gather.31 = bf16[512,768]{1,0:T(8,128)(2,1)} all-gather(bf16[128,768]{1,0:T(8,128)(2,1)S(1)} %bitcast.143), channel_id=1, replica_groups=mesh['dp'=2,'sp'=4,'ctx'=4] {'sp'}, dimensions={0}, use_global_device_ids=true | all-gather | bytes 983040 | tf_op jit(solution)/shard_map/all_gather | solution.py:492
  47.5 22.4 %collective-permute-done.1 = bf16[192,768]{1,0:T(8,128)(2,1)S(1)} collective-permute-done((bf16[192,768]{1,0:T(8,128)(2,1)S(1)}, bf16[192,768]{1,0:T(8,128)(2,1)S(1)}, u32[]{:S(2)}, u32[]{:S(2)}) %collective-permute-start.1) | collective-permute-done | bytes 294944 | tf_op jit(solution)/shard_map/ppermute | solution.py:393
  72.0 48.8 %attend.1 = (bf16[3,512,64]{2,1,0:T(8,128)(2,1)}, bf16[3,4,128,2048]{3,2,1,0:T(8,128)(2,1)}) custom-call(s32[1]{0:T(128)} %bitcast.2.base_ref, s32[3,4,128,64]{3,2,1,0:T(8,128)} %bitcast.136, bf16[512,384]{1,0:T(8,128)(2,1)} %copy.39.refs_1_.refs_0_, bf16[4,528,384]{2,1,0:T(8,128)(2,1)} %bitcast.131), custom_call_target="tpu_custom_call" | custom-call | tf_op jit(solution)/shard_map/attend/pallas_call | solution.py:172
  123.2 3.5 all-to-all-start
  127.4 10.9 %all-to-all-done = bf16[4,128,768]{2,1,0:T(8,128)(2,1)S(1)} async-done(((bf16[4,128,768]{2,1,0:T(8,128)(2,1)}), bf16[4,128,768]{2,1,0:T(8,128)(2,1)S(1)}, u32[]{:S(2)}, u32[]{:S(2)}) %all-to-all-start) | async-done | bytes 786464 | tf_op jit(solution)/shard_map/all_to_all | solution.py:405
  138.9 8.1 %all_gather.34 = bf16[512,768]{1,0:T(8,128)(2,1)S(1)} all-gather(bf16[128,768]{1,0:T(8,128)(2,1)S(1)} %multiply_convert_fusion.1), channel_id=1, replica_groups=mesh['dp'=2,'sp'=4,'ctx'=4] {'sp'}, dimensions={0}, use_global_device_ids=true | all-gather | bytes 983040 | tf_op jit(solution)/shard_map/all_gather | solution.py:511
  147.0 2.8 multiply_convert_fusion
  149.8 3.5 fusion.12
  157.1 3.5 convolution_convert_fusion.3
  160.5 3.5 all-to-all-start.1
  170.2 5.4 %all-to-all-done.1 = bf16[4,128,768]{2,1,0:T(8,128)(2,1)S(1)} async-done(((bf16[4,128,768]{2,1,0:T(8,128)(2,1)}), bf16[4,128,768]{2,1,0:T(8,128)(2,1)S(1)}, u32[]{:S(2)}, u32[]{:S(2)}) %all-to-all-start.1) | async-done | bytes 786464 | tf_op jit(solution)/shard_map/all_to_all | solution.py:405
  177.8 8.0 %all_gather.35 = bf16[512,768]{1,0:T(8,128)(2,1)S(1)} all-gather(bf16[128,768]{1,0:T(8,128)(2,1)S(1)} %add_convert_fusion.1), channel_id=1, replica_groups=mesh['dp'=2,'sp'=4,'ctx'=4] {'sp'}, dimensions={0}, use_global_device_ids=true | all-gather | bytes 983040 | tf_op jit(solution)/shard_map/all_gather | solution.py:528
  190.3 4.9 %all-to-all-start.2 = ((bf16[4,96,768]{2,1,0:T(8,128)(2,1)}), bf16[4,96,768]{2,1,0:T(8,128)(2,1)S(1)}, u32[]{:S(2)}, u32[]{:S(2)}) async-start(bf16[4,96,768]{2,1,0:T(8,128)(2,1)} %fusion.14), calls=%async_computation.2 | async-start | bytes 1179648 | tf_op jit(solution)/shard_map/all_to_all | solution.py:535
  195.7 13.7 %attend_back.1 = (bf16[512,384]{1,0:T(8,128)(2,1)}, bf16[4,528,384]{2,1,0:T(8,128)(2,1)}) custom-call(bf16[512,384]{1,0:T(8,128)(2,1)} %copy.39.refs_1_.refs_0_, bf16[512,384]{1,0:T(8,128)(2,1)} %convolution_convert_fusion.6.refs_1_, bf16[4,528,384]{2,1,0:T(8,128)(2,1)} %bitcast.132, bf16[3,4,128,2048]{3,2,1,0:T(8,128)(2,1)} %get-tuple-element.64.refs_3_), custom_call_target="tpu_custom_call" | custom-call | tf_op jit(solution)/shard_map/attend_back/pallas_call | solution.py:239
  214.9 2.6 convolution_convert_fusion.2
  217.5 14.9 %all_to_all.35 = bf16[4,128,768]{2,1,0:T(8,128)(2,1)} all-to-all(bf16[4,128,768]{2,1,0:T(8,128)(2,1)S(1)} %bitcast.162), channel_id=1, replica_groups=mesh['dp'=2,'sp'=4,'ctx'=4] {'sp'}, dimensions={0} | all-to-all | bytes 1572864 | tf_op jit(solution)/shard_map/all_to_all | solution.py:405
  232.3 5.1 %all-to-all-start.3 = ((bf16[4,144,768]{2,1,0:T(8,128)(2,1)}), bf16[4,144,768]{2,1,0:T(8,128)(2,1)S(1)}, u32[]{:S(2)}, u32[]{:S(2)}) async-start(bf16[4,144,768]{2,1,0:T(8,128)(2,1)} %pad_maximum_fusion.1), calls=%async_computation.4 | async-start | bytes 1769472 | tf_op jit(solution)/shard_map/all_to_all | solution.py:547
  241.8 26.2 %all-to-all-done.3 = bf16[4,144,768]{2,1,0:T(8,128)(2,1)S(1)} async-done(((bf16[4,144,768]{2,1,0:T(8,128)(2,1)}), bf16[4,144,768]{2,1,0:T(8,128)(2,1)S(1)}, u32[]{:S(2)}, u32[]{:S(2)}) %all-to-all-start.3) | async-done | bytes 884768 | tf_op jit(solution)/shard_map/all_to_all | solution.py:547
  269.9 4.4 %finish.1 = (bf16[768,640]{1,0:T(8,128)(2,1)}, bf16[512,768]{1,0:T(8,128)(2,1)}) custom-call(bf16[768,512]{1,0:T(8,128)(2,1)} %fusion.62.norm_ref, bf16[528,384]{1,0:T(8,128)(2,1)} %bitcast.165, bf16[512,384]{1,0:T(8,128)(2,1)} %get-tuple-element.79.dq_ref, bf16[3,512]{1,0:T(4,128)(2,1)} %copy-done.16, bf16[768,640]{1,0:T(8,128)(2,1)} %copy-done.3, ...), custom_call_target="tpu_custom_call" | custom-call | tf_op jit(solution)/shard_map/finish/pallas_call | solution.py:300
  276.9 11.6 %collective-permute-done.7 = bf16[4,96,640]{2,1,0:T(8,128)(2,1)S(1)} collective-permute-done((bf16[4,96,640]{2,1,0:T(8,128)(2,1)S(1)}, bf16[4,96,640]{2,1,0:T(8,128)(2,1)S(1)}, u32[]{:S(2)}, u32[]{:S(2)}) %collective-permute-start.7) | collective-permute-done | bytes 491552 | tf_op jit(solution)/shard_map/ppermute | solution.py:383
  290.4 3.5 all-to-all-start.5
  294.1 24.9 %all-to-all-done.5 = bf16[4,96,640]{2,1,0:T(8,128)(2,1)S(1)} async-done(((bf16[4,96,640]{2,1,0:T(8,128)(2,1)}), bf16[4,96,640]{2,1,0:T(8,128)(2,1)S(1)}, u32[]{:S(2)}, u32[]{:S(2)}) %all-to-all-start.5) | async-done | bytes 491552 | tf_op jit(solution)/shard_map/all_to_all | solution.py:405
  319.7 13.1 %all-gather.10.cloned.1.call-done = bf16[3840,768]{1,0:T(8,128)(2,1)} async-done(((bf16[240,768]{1,0:T(8,128)(2,1)}), bf16[3840,768]{1,0:T(8,128)(2,1)}) %all-gather.10.cloned.1.call-update) | async-done | bytes 5898256 | tf_op jit(solution)/shard_map/all_gather | solution.py:558
  333.6 2.4 slice.77
  337.8 4.2 %all-to-all-start.6 = ((bf16[4,128,768]{2,1,0:T(8,128)(2,1)}), bf16[4,128,768]{2,1,0:T(8,128)(2,1)}, u32[]{:S(2)}, u32[]{:S(2)}) async-start(bf16[4,128,768]{2,1,0:T(8,128)(2,1)} %bitcast.160), calls=%async_computation.7 | async-start | bytes 1572864 | tf_op jit(solution)/shard_map/all_to_all | solution.py:405
  344.5 2.8 convert_element_type.218
  348.4 2.7 bitcast_convert_fusion
  351.1 3.2 all-to-all-done.6
  357.2 18.9 %all-gather.12.cloned.1.call-done = bf16[1536,640]{1,0:T(8,128)(2,1)} async-done(((bf16[96,640]{1,0:T(8,128)(2,1)}), bf16[1536,640]{1,0:T(8,128)(2,1)}) %all-gather.12.cloned.1.call-update) | async-done | bytes 1966096 | tf_op jit(solution)/shard_map/all_gather | solution.py:572
  377.4 4.2 %unpack.1 = (f32[384,2304]{1,0:T(8,128)}, f32[384,12]{1,0:T(8,128)}) custom-call(bf16[4,384,640]{2,1,0:T(8,128)(2,1)} %bitcast.138), custom_call_target="tpu_custom_call" | custom-call | tf_op jit(solution)/shard_map/unpack/pallas_call | solution.py:324
  (183 shorter events, 71.4 us)
Async XLA Ops:
  7.2 9.7 %copy-start.2 = (bf16[1,128,768]{2,1,0:T(8,128)(2,1)S(1)}, bf16[1,128,768]{2,1,0:T(8,128)(2,1)}, u32[]{:S(2)}) copy-start(bf16[1,128,768]{2,1,0:T(8,128)(2,1)} %param.11) | copy-start | bytes 589828
  7.2 64.8 %all-gather.8.cloned.1.call-start = ((), (), s32[]{:S(2)}) async-start(), calls=%async_computation.9 | async-start | bytes 2027520 | tf_op jit(solution)/shard_map/all_gather | solution.py:493
  14.0 15.6 %collective-permute-start = (bf16[400,640]{1,0:T(8,128)(2,1)}, bf16[400,640]{1,0:T(8,128)(2,1)S(1)}, u32[]{:S(2)}, u32[]{:S(2)}) collective-permute-start(bf16[400,640]{1,0:T(8,128)(2,1)} %arrange.1), channel_id=1, source_target_pairs={{0,16},{16,0},{1,17},{17,1},{2,18},{18,2},{3,19},{19,3},{4,20},{20... | collective-permute-start | bytes 1536008 | tf_op jit(solution)/shard_map/ppermute | solution.py:448
  32.1 5.1 %copy-start.15 = (bf16[384,768]{1,0:T(8,128)(2,1)S(1)}, bf16[384,768]{1,0:T(8,128)(2,1)}, u32[]{:S(2)}) copy-start(bf16[384,768]{1,0:T(8,128)(2,1)} %param.18) | copy-start | bytes 1769476
  33.0 5.5 %copy-start.7 = (bf16[1,128,768]{2,1,0:T(8,128)(2,1)S(1)}, bf16[1,128,768]{2,1,0:T(8,128)(2,1)}, u32[]{:S(2)}) copy-start(bf16[1,128,768]{2,1,0:T(8,128)(2,1)} %param.12) | copy-start | bytes 589828
  35.2 35.8 %collective-permute-start.2 = (bf16[384,768]{1,0:T(8,128)(2,1)}, bf16[384,768]{1,0:T(8,128)(2,1)}, u32[]{:S(2)}, u32[]{:S(2)}) collective-permute-start(bf16[384,768]{1,0:T(8,128)(2,1)} %get-tuple-element.52), channel_id=1, source_target_pairs={{0,16},{16,0},{1,17},{17,1},{2,18},{18,2},{3,19},{19,3},{4,20},{20... | collective-permute-start | bytes 1769480 | tf_op jit(solution)/shard_map/ppermute | solution.py:366
  36.1 34.9 %collective-permute-start.3 = (bf16[384,768]{1,0:T(8,128)(2,1)}, bf16[384,768]{1,0:T(8,128)(2,1)}, u32[]{:S(2)}, u32[]{:S(2)}) collective-permute-start(bf16[384,768]{1,0:T(8,128)(2,1)} %get-tuple-element.53), channel_id=1, source_target_pairs={{0,16},{16,0},{1,17},{17,1},{2,18},{18,2},{3,19},{19,3},{4,20},{20... | collective-permute-start | bytes 1769480 | tf_op jit(solution)/shard_map/ppermute | solution.py:366
  37.4 32.5 %collective-permute-start.1 = (bf16[192,768]{1,0:T(8,128)(2,1)S(1)}, bf16[192,768]{1,0:T(8,128)(2,1)S(1)}, u32[]{:S(2)}, u32[]{:S(2)}) collective-permute-start(bf16[192,768]{1,0:T(8,128)(2,1)S(1)} %constant_dynamic-slice_fusion), channel_id=1, source_target_pairs={{0,16},{16,0},{1,17},{17,1},{2,18},{18,2},{3,19},{19,3},{4,20},{20... | collective-permute-start | bytes 884744 | tf_op jit(solution)/shard_map/ppermute | solution.py:393
  123.2 15.1 %all-to-all-start = ((bf16[4,128,768]{2,1,0:T(8,128)(2,1)}), bf16[4,128,768]{2,1,0:T(8,128)(2,1)S(1)}, u32[]{:S(2)}, u32[]{:S(2)}) async-start(bf16[4,128,768]{2,1,0:T(8,128)(2,1)} %bitcast.14), calls=%async_computation | async-start | bytes 1572864 | tf_op jit(solution)/shard_map/all_to_all | solution.py:405
  138.5 37.4 %copy-start.17 = (f32[128]{0:T(128)}, f32[128]{0:T(128)S(1)}, u32[]{:S(2)}) copy-start(f32[128]{0:T(128)S(1)} %broadcast_multiply_fusion.2) | copy-start | bytes 1540
  138.8 37.2 %copy-start.21 = (f32[128]{0:T(128)}, f32[128]{0:T(128)S(1)}, u32[]{:S(2)}) copy-start(f32[128]{0:T(128)S(1)} %fusion.54) | copy-start | bytes 1540
  149.8 5.4 %copy-start.30 = (bf16[512,768]{1,0:T(8,128)(2,1)}, bf16[512,768]{1,0:T(8,128)(2,1)S(1)}, u32[]{:S(2)}) copy-start(bf16[512,768]{1,0:T(8,128)(2,1)S(1)} %get-tuple-element.75) | copy-start | bytes 2359300
  160.5 15.1 %all-to-all-start.1 = ((bf16[4,128,768]{2,1,0:T(8,128)(2,1)}), bf16[4,128,768]{2,1,0:T(8,128)(2,1)S(1)}, u32[]{:S(2)}, u32[]{:S(2)}) async-start(bf16[4,128,768]{2,1,0:T(8,128)(2,1)} %bitcast.161), calls=%async_computation.1 | async-start | bytes 1572864 | tf_op jit(solution)/shard_map/all_to_all | solution.py:405
  167.3 20.9 %collective-permute-start.4 = (bf16[4,96,768]{2,1,0:T(8,128)(2,1)}, bf16[4,96,768]{2,1,0:T(8,128)(2,1)}, u32[]{:S(2)}, u32[]{:S(2)}) collective-permute-start(bf16[4,96,768]{2,1,0:T(8,128)(2,1)} %dynamic-slice_bitcast_fusion.1), channel_id=1, source_target_pairs={{0,16},{16,0},{1,17},{17,1},{2,18},{18,2},{3,19},{19,3},{4,20},{20... | collective-permute-start | bytes 1769480 | tf_op jit(solution)/shard_map/ppermute | solution.py:383
  169.3 7.7 %copy-start.8 = (bf16[1,128,768]{2,1,0:T(8,128)(2,1)S(1)}, bf16[1,128,768]{2,1,0:T(8,128)(2,1)}, u32[]{:S(2)}) copy-start(bf16[1,128,768]{2,1,0:T(8,128)(2,1)} %param.12) | copy-start | bytes 589828
  169.3 40.1 %collective-permute-start.5 = (bf16[4,96,768]{2,1,0:T(8,128)(2,1)}, bf16[4,96,768]{2,1,0:T(8,128)(2,1)}, u32[]{:S(2)}, u32[]{:S(2)}) collective-permute-start(bf16[4,96,768]{2,1,0:T(8,128)(2,1)} %dynamic-slice_bitcast_fusion), channel_id=1, source_target_pairs={{0,16},{16,0},{1,17},{17,1},{2,18},{18,2},{3,19},{19,3},{4,20},{20... | collective-permute-start | bytes 1769480 | tf_op jit(solution)/shard_map/ppermute | solution.py:383
  176.2 10.6 %copy-start.14 = (bf16[3,128,768]{2,1,0:T(8,128)(2,1)S(1)}, bf16[3,128,768]{2,1,0:T(8,128)(2,1)}, u32[]{:S(2)}) copy-start(bf16[3,128,768]{2,1,0:T(8,128)(2,1)} %pad.19) | copy-start | bytes 1769476
  190.3 22.4 %all-to-all-start.2 = ((bf16[4,96,768]{2,1,0:T(8,128)(2,1)}), bf16[4,96,768]{2,1,0:T(8,128)(2,1)S(1)}, u32[]{:S(2)}, u32[]{:S(2)}) async-start(bf16[4,96,768]{2,1,0:T(8,128)(2,1)} %fusion.14), calls=%async_computation.2 | async-start | bytes 1179648 | tf_op jit(solution)/shard_map/all_to_all | solution.py:535
  195.2 73.7 %reduce-scatter.2.cloned.1.call-start = ((), (), s32[]{:S(2)}) async-start(), calls=%async_computation.8 | async-start | bytes 2027520 | tf_op jit(solution)/shard_map/reduce_scatter | solution.py:540
  195.2 15.6 %collective-permute-start.6 = (bf16[192,768]{1,0:T(8,128)(2,1)}, bf16[192,768]{1,0:T(8,128)(2,1)}, u32[]{:S(2)}, u32[]{:S(2)}) collective-permute-start(bf16[192,768]{1,0:T(8,128)(2,1)} %convolution_convert_fusion.7), channel_id=1, source_target_pairs={{0,16},{16,0},{1,17},{17,1},{2,18},{18,2},{3,19},{19,3},{4,20},{20... | collective-permute-start | bytes 884744 | tf_op jit(solution)/shard_map/ppermute | solution.py:400
  217.4 20.0 %copy-start.23 = (bf16[384,1]{0,1:T(2,128)(2,1)S(1)}, bf16[384,1]{0,1:T(2,128)(2,1)}, u32[]{:S(2)}) copy-start(bf16[384,1]{0,1:T(2,128)(2,1)} %get-tuple-element.143) | copy-start | bytes 2308
  217.4 20.0 %copy-start.24 = (bf16[384,1]{0,1:T(2,128)(2,1)S(1)}, bf16[384,1]{0,1:T(2,128)(2,1)}, u32[]{:S(2)}) copy-start(bf16[384,1]{0,1:T(2,128)(2,1)} %get-tuple-element.148) | copy-start | bytes 2308
  217.5 20.0 %copy-start.20 = (f32[512]{0:T(512)S(1)}, f32[512]{0:T(512)}, u32[]{:S(2)}) copy-start(f32[512]{0:T(512)} %copy-done.19) | copy-start | bytes 6148
  232.3 35.6 %all-to-all-start.3 = ((bf16[4,144,768]{2,1,0:T(8,128)(2,1)}), bf16[4,144,768]{2,1,0:T(8,128)(2,1)S(1)}, u32[]{:S(2)}, u32[]{:S(2)}) async-start(bf16[4,144,768]{2,1,0:T(8,128)(2,1)} %pad_maximum_fusion.1), calls=%async_computation.4 | async-start | bytes 1769472 | tf_op jit(solution)/shard_map/all_to_all | solution.py:547
  237.4 95.4 %all-gather.10.cloned.1.call-start = ((), (), s32[]{:S(2)}) async-start(), calls=%async_computation.10 | async-start | bytes 6266880 | tf_op jit(solution)/shard_map/all_gather | solution.py:558
  275.3 57.5 %copy-start.10 = (f32[128,768]{1,0:T(8,128)S(1)}, f32[128,768]{1,0:T(8,128)}, u32[]{:S(2)}) copy-start(f32[128,768]{1,0:T(8,128)} %convert_reduce_fusion.2) | copy-start | bytes 1179652
  275.3 57.5 %copy-start.25 = (pred[128]{0:T(512)(128)(4,1)S(1)}, pred[128]{0:T(512)(128)(4,1)}, u32[]{:S(2)}) copy-start(pred[128]{0:T(512)(128)(4,1)} %add_compare_fusion) | copy-start | bytes 388
  275.4 13.1 %collective-permute-start.7 = (bf16[4,96,640]{2,1,0:T(8,128)(2,1)S(1)}, bf16[4,96,640]{2,1,0:T(8,128)(2,1)S(1)}, u32[]{:S(2)}, u32[]{:S(2)}) collective-permute-start(bf16[4,96,640]{2,1,0:T(8,128)(2,1)S(1)} %dynamic-slice_bitcast_fusion.2), channel_id=1, source_target_pairs={{0,16},{16,0},{1,17},{17,1},{2,18},{18,2},{3,19},{19,3},{4,20},{20... | collective-permute-start | bytes 1474568 | tf_op jit(solution)/shard_map/ppermute | solution.py:383
  290.4 28.5 %all-to-all-start.5 = ((bf16[4,96,640]{2,1,0:T(8,128)(2,1)}), bf16[4,96,640]{2,1,0:T(8,128)(2,1)S(1)}, u32[]{:S(2)}, u32[]{:S(2)}) async-start(bf16[4,96,640]{2,1,0:T(8,128)(2,1)} %fusion.15), calls=%async_computation.6 | async-start | bytes 983040 | tf_op jit(solution)/shard_map/all_to_all | solution.py:405
  293.9 82.2 %all-gather.12.cloned.1.call-start = ((), (), s32[]{:S(2)}) async-start(), calls=%async_computation.11 | async-start | bytes 2088960 | tf_op jit(solution)/shard_map/all_gather | solution.py:572
  337.8 16.6 %all-to-all-start.6 = ((bf16[4,128,768]{2,1,0:T(8,128)(2,1)}), bf16[4,128,768]{2,1,0:T(8,128)(2,1)}, u32[]{:S(2)}, u32[]{:S(2)}) async-start(bf16[4,128,768]{2,1,0:T(8,128)(2,1)} %bitcast.160), calls=%async_computation.7 | async-start | bytes 1572864 | tf_op jit(solution)/shard_map/all_to_all | solution.py:405
  376.1 8.1 %copy-start.1 = (bf16[384,2304]{1,0:T(8,128)(2,1)S(1)}, bf16[384,2304]{1,0:T(8,128)(2,1)}, u32[]{:S(2)}) copy-start(bf16[384,2304]{1,0:T(8,128)(2,1)} %param.16) | copy-start | bytes 5308420
  (18 other events, 57.3 us)
Sparse Core Ops, SparseCore 0:
  33.1 38.4 all-gather.7
  212.8 44.6 reduce-scatter.1
  269.0 63.7 all-gather.9
  334.9 41.1 all-gather.11
where the time goes:
time: 393 us; the launch traced here: 391 us
  waiting for transfers between devices  137 us (35%)
  Pallas kernels  73.2 us (19%)
  blocking collectives  48.7 us (12%)
  starting transfers between devices  34.7 us (9%)
  other arithmetic  34.7 us (9%)
  local copies, waits for them, and re-layouts  26.2 us (7%)
  matrix products  21.3 us (5%)
  between operations  15.1 us (4%)
    pallas_call x1, Pallas kernels, attend(): pl.pallas_call(functools.partial(attend_kernel, parts, chunk), grid_spec=...  48.8 us
    all_to_all x4, waiting for transfers between devices, exchange_sum(): came = lax.all_to_all(parts, axis, split_axis=0, concat_axis=0, tiled=True)  44.4 us
    all_to_all x1, waiting for transfers between devices, per_device(): lax.all_to_all(late, 'ctx', split_axis=0, concat_axis=0, tiled=True)  26.2 us
    ppermute x1, waiting for transfers between devices, group_rows_of(): far = lax.ppermute(near, 'dp', [(0, 1), (1, 0)])  22.4 us
    all_gather x1, waiting for transfers between devices, per_device(): lax.all_gather(small_own, ('sp', 'ctx'), axis=0, tiled=False)  18.9 us
    all_to_all x1, blocking collectives, exchange_sum(): came = lax.all_to_all(parts, axis, split_axis=0, concat_axis=0, tiled=True)  14.9 us
    all_to_all x4, starting transfers between devices, exchange_sum(): came = lax.all_to_all(parts, axis, split_axis=0, concat_axis=0, tiled=True)  14.7 us
    pallas_call x1, Pallas kernels, attend_back(): pl.pallas_call(functools.partial(attend_back_kernel, parts, chunk), grid=...  13.7 us
  transfers between devices with their start and end apart: 18, of which 9 were waited for; matrix products, arithmetic and copies ran while one was open for 14% of the time, Pallas kernels for 5%

commit v1 on v0

--- a/solution.py
+++ b/solution.py
@@ -133,7 +133,7 @@
 
     lax.fori_loop(0, rows // 16, step, 0)
     both = jnp.dot(prob_ref[0, 0, :, :span], kv_ref[:span, :], preferred_element_type=f32)
-    out_ref[0] = both[:, HD:].astype(bf16)
+    out_ref[0] = jnp.transpose(both)[HD:, :].astype(bf16)
 
 
 def attend_kernel(parts, chunk, base_ref, *refs):
@@ -159,7 +159,7 @@
             pl.BlockSpec((count, height, LANES), lambda h, r, b: (0, 0, h)),
         ],
         out_specs=[
-            pl.BlockSpec((1, block, HD), lambda h, r, b: (h, r, 0)),
+            pl.BlockSpec((1, HD, block), lambda h, r, b: (h, 0, r)),
             pl.BlockSpec((1, 1, block, slot), lambda h, r, b: (h, r, 0, 0)),
         ],
         scratch_shapes=[
@@ -173,14 +173,14 @@
         functools.partial(attend_kernel, parts, chunk),
         grid_spec=grid_spec,
         out_shape=[
-            jax.ShapeDtypeStruct((heads, parts * block, HD), jnp.bfloat16),
+            jax.ShapeDtypeStruct((heads, HD, parts * block), jnp.bfloat16),
             jax.ShapeDtypeStruct((heads, parts, block, slot), jnp.bfloat16),
         ],
         name="attend",
     )(base, kept, query, pairs)
 
 
-def attend_back_body(first, last, tiles, chunk, q_ref, grad_ref, src_ref, prob_ref, dq_ref, out_ref, raw_ref, kv_ref, dkv_ref, gate_ref):
+def attend_back_body(first, last, tiles, chunk, q_ref, grad_ref, src_ref, prob_ref, dq_ref, out_ref, turned_ref, dq_turned_ref, gates_ref, raw_ref, kv_ref, dkv_ref, gate_ref):
     f32, bf16 = jnp.float32, jnp.bfloat16
     rows = q_ref.shape[0]
     steps = tiles * LANES // chunk
@@ -210,8 +210,12 @@
         dkv_ref[:HD, cols] += keys[:HD]
         gate_ref[:, cols] += keys[HD : HD + 8]
         dkv_ref[HD:, cols] += jnp.dot(grad_t, prob, preferred_element_type=f32)
-    dq_ref[...] = (dq * HD ** (-0.5)).astype(dq_ref.dtype)
+    dq = dq * HD ** (-0.5)
+    dq_ref[...] = dq.astype(dq_ref.dtype)
+    dq_turned_ref[0] = jnp.transpose(dq)[:HD, :].astype(bf16)
     if last:
+        turned_ref[0] = dkv_ref[...].astype(bf16)
+        gates_ref[0] = gate_ref[...]
         count, height, _ = out_ref.shape
         parts = (height - PAD_ROWS) // LANES
         for at in range(count):
@@ -248,10 +252,16 @@
         out_specs=[
             pl.BlockSpec((block, LANES), lambda h, r: (r, h)),
             pl.BlockSpec((count, height, LANES), lambda h, r: (0, 0, h)),
+            pl.BlockSpec((1, LANES, slot), lambda h, r: (h, 0, 0)),
+            pl.BlockSpec((1, HD, block), lambda h, r: (h, 0, r)),
+            pl.BlockSpec((1, 8, slot), lambda h, r: (h, 0, 0)),
         ],
         out_shape=[
             jax.ShapeDtypeStruct((parts * block, heads * LANES), jnp.bfloat16),
             jax.ShapeDtypeStruct((count, height, width), jnp.bfloat16),
+            jax.ShapeDtypeStruct((heads, LANES, slot), jnp.bfloat16),
+            jax.ShapeDtypeStruct((heads, HD, parts * block), jnp.bfloat16),
+            jax.ShapeDtypeStruct((heads, 8, slot), jnp.float32),
         ],
         scratch_shapes=[
             pltpu.VMEM((block, slot), jnp.float32),
@@ -263,9 +273,41 @@
     )(query, grad, pairs, prob)
 
 
-def finish_kernel(heads, norm_ref, pair_ref, dq_ref, score_ref, in_ref, gain_ref, small_ref, grad_ref):
+def weight_kernel(turned_ref, dq_ref, gates_ref, score_ref, slot_ref, norm_ref, in_ref, gain_ref, out_ref):
     f32, bf16 = jnp.float32, jnp.bfloat16
-    group = norm_ref.shape[1]
+    heads, _, slot = turned_ref.shape
+    wide = in_ref.shape[1]
+    width = slot_ref.shape[1]
+    total = jnp.concatenate([gates_ref[head, 0:1, :] for head in range(heads)], axis=0)
+    total = total * jax.nn.sigmoid(-score_ref[...].astype(f32))
+    total = jnp.concatenate([total, jnp.zeros((PAD_ROWS - heads, slot), f32)], axis=0).astype(bf16)
+    turned = [
+        jnp.dot(turned_ref[...].reshape(heads * LANES, slot), slot_ref[...], preferred_element_type=f32),
+        jnp.dot(dq_ref[...].reshape(heads * HD, -1), norm_ref[...], preferred_element_type=f32),
+        jnp.dot(total, slot_ref[...], preferred_element_type=f32),
+        jnp.zeros((wide - heads * 3 * HD - PAD_ROWS, width), f32),
+    ]
+    small = jnp.transpose(jnp.concatenate(turned, axis=0))
+    gain_grad = jnp.sum(small * in_ref[...].astype(f32), axis=1, keepdims=True) / gain_ref[:, 0:1]
+    lane = lax.broadcasted_iota(jnp.int32, small.shape, 1)
+    at = heads * 3 * HD + heads
+    small = jnp.where(lane == at, gain_grad, jnp.where(lane == at + 1, gain_ref[:, 1:2], small))
+    out_ref[:, :wide] = small.astype(bf16)
+    out_ref[:, wide:] = jnp.zeros((width, width - wide), bf16)
+
+
+def weight_grad(turned, dq, gates, score, norm_slot, norm_one, weights, gains):
+    width = norm_one.shape[1]
+    return pl.pallas_call(
+        weight_kernel,
+        out_shape=jax.ShapeDtypeStruct((width, width), jnp.bfloat16),
+        name="weight_grad",
+    )(turned, dq, gates, score, norm_slot, norm_one, weights, gains)
+
+
+def finish_kernel(heads, pair_ref, dq_ref, score_ref, in_ref, grad_ref):
+    f32, bf16 = jnp.float32, jnp.bfloat16
+    group = dq_ref.shape[0]
     parts = group // LANES
     wide = in_ref.shape[1]
     gates = pair_ref[group:, :].astype(f32)
@@ -285,56 +327,58 @@
         + [scores[:, :rest]],
         axis=1,
     ).astype(bf16)
-    small = jnp.dot(norm_ref[...], columns, preferred_element_type=f32)
-    gain_grad = jnp.sum(small * in_ref[...].astype(f32), axis=1, keepdims=True) / gain_ref[:, 0:1]
-    lane = lax.broadcasted_iota(jnp.int32, small.shape, 1)
-    at = heads * 3 * HD + heads
-    small = jnp.where(lane == at, gain_grad, jnp.where(lane == at + 1, gain_ref[:, 1:2], small))
-    small_ref[...] = small.astype(bf16)
     grad_ref[...] = lax.dot_general(columns, in_ref[...], NT, preferred_element_type=f32).astype(bf16)
 
 
-def finish(norm_t, pair, dq, score, weights, gains):
-    width, group = norm_t.shape
-    heads = score.shape[0]
+def finish(pair, dq, score, weights):
     return pl.pallas_call(
-        functools.partial(finish_kernel, heads),
+        functools.partial(finish_kernel, score.shape[0]),
+        out_shape=jax.ShapeDtypeStruct((dq.shape[0], weights.shape[0]), jnp.bfloat16),
+        name="finish",
+    )(pair, dq, score, weights)
+
+
+def unpack_kernel(groups, heads, piece, parts, all_ref, qkv_ref, score_ref, fc_ref, proj_ref):
+    f32 = jnp.float32
+    keys = heads * 2 * HD
+    part_cols = fc_ref.shape[1] // (groups * parts)
+    for step in range(all_ref.shape[1]):
+        rows = slice(step * piece, (step + 1) * piece)
+        for at in range(groups):
+            values = all_ref[at, step, :piece, :].astype(f32)
+            for head in range(heads):
+                start = (at * heads + head) * 3 * HD
+                qkv_ref[rows, start : start + HD] = values[:, keys + head * HD : keys + (head + 1) * HD]
+                qkv_ref[rows, start + HD : start + 3 * HD] = values[:, head * 2 * HD : (head + 1) * 2 * HD]
+            score_ref[rows, at * heads : (at + 1) * heads] = values[:, keys + heads * HD : keys + heads * HD + heads]
+            values = all_ref[at, step, piece : 2 * piece, :].astype(f32)
+            for part in range(parts):
+                start = (part * groups + at) * part_cols
+                fc_ref[rows, start : start + part_cols] = values[:, part * part_cols : (part + 1) * part_cols]
+            proj_ref[at, step] = all_ref[at, step, 2 * piece : 2 * piece + proj_ref.shape[2], :].astype(f32)
+
+
+def unpack(gathered, heads, piece, proj_piece, parts, hidden):
+    groups, count, rows, width = gathered.shape
+    step = 1 if piece % 16 == 0 else count
+    return pl.pallas_call(
+        functools.partial(unpack_kernel, groups, heads, piece, parts),
+        grid=(count // step,),
+        in_specs=[pl.BlockSpec((groups, step, rows, width), lambda c: (0, c, 0, 0))],
+        out_specs=[
+            pl.BlockSpec((step * piece, groups * heads * 3 * HD), lambda c: (c, 0)),
+            pl.BlockSpec((step * piece, groups * heads), lambda c: (c, 0)),
+            pl.BlockSpec((step * piece, hidden), lambda c: (c, 0)),
+            pl.BlockSpec((groups, step, proj_piece, width), lambda c: (0, c, 0, 0)),
+        ],
         out_shape=[
-            jax.ShapeDtypeStruct(weights.shape, jnp.bfloat16),
-            jax.ShapeDtypeStruct((group, width), jnp.bfloat16),
-        ],
-        name="finish",
-    )(norm_t, pair, dq, score, weights, gains)
-
-
-def unpack_kernel(groups, heads, small_ref, qkv_ref, score_ref):
-    keys = heads * 2 * HD
-    for at in range(groups):
-        values = small_ref[at].astype(jnp.float32)
-        for head in range(heads):
-            start = (at * heads + head) * 3 * HD
-            qkv_ref[:, start : start + HD] = values[:, keys + head * HD : keys + (head + 1) * HD]
-            qkv_ref[:, start + HD : start + 3 * HD] = values[:, head * 2 * HD : (head + 1) * 2 * HD]
-        score_ref[:, at * heads : (at + 1) * heads] = values[:, keys + heads * HD : keys + heads * HD + heads]
-
-
-def unpack(small, heads):
-    groups, rows, width = small.shape
-    block = 96 if rows % 96 == 0 else rows
-    return pl.pallas_call(
-        functools.partial(unpack_kernel, groups, heads),
-        grid=(rows // block,),
-        in_specs=[pl.BlockSpec((groups, block, width), lambda r: (0, r, 0))],
-        out_specs=[
-            pl.BlockSpec((block, groups * heads * 3 * HD), lambda r: (r, 0)),
-            pl.BlockSpec((block, groups * heads), lambda r: (r, 0)),
-        ],
-        out_shape=[
-            jax.ShapeDtypeStruct((rows, groups * heads * 3 * HD), jnp.float32),
-            jax.ShapeDtypeStruct((rows, groups * heads), jnp.float32),
+            jax.ShapeDtypeStruct((count * piece, groups * heads * 3 * HD), jnp.float32),
+            jax.ShapeDtypeStruct((count * piece, groups * heads), jnp.float32),
+            jax.ShapeDtypeStruct((count * piece, hidden), jnp.float32),
+            jax.ShapeDtypeStruct((groups, count, proj_piece, width), jnp.float32),
         ],
         name="unpack",
-    )(small)
+    )(gathered)
 
 
 def arrange_kernel(heads, rows, qkv_ref, score_ref, gains_ref, out_ref):
@@ -465,7 +509,7 @@
     )
     proj_own = lax.dynamic_slice_in_dim(proj_weight, sp_at * hidden_part, hidden_part, 0)
     all_in, out_own, fc_own, proj_own = lax.optimization_barrier((all_in, out_weight, fc_own, proj_own))
-    out_part = group_rows_of(out_own, sp_at, heads * HD)
+    out_came = dp_send(out_own)
     fc_came = dp_send(fc_own)
     proj_came = dp_send(proj_own)
 
@@ -491,11 +535,17 @@
     cot_own, pairs_own = lax.optimization_barrier((cotangent[0], pairs_own))
     cot_group = lax.all_gather(cot_own, "sp", axis=0, tiled=True)
     pairs = lax.all_gather(pairs_own, "ctx", axis=0, tiled=False)
-    query_wide, cot_group, out_part, fc_came, proj_came = lax.optimization_barrier(
-        (query_wide, cot_group, out_part, fc_came, proj_came)
-    )
+    norm_own = lax.dynamic_slice_in_dim(norm_one, sp_at * rows, rows, 0)
+    query_wide, cot_group, out_came, fc_came, proj_came, norm_own, pairs = lax.optimization_barrier(
+        (query_wide, cot_group, out_came, fc_came, proj_came, norm_own, pairs)
+    )
+    norm_slot = lax.all_gather(norm_own, ("sp", "ctx"), axis=0, tiled=True)
     head_outs, prob = attend(base, kept, query_wide, pairs)
-    attended = jnp.transpose(head_outs, (1, 0, 2)).reshape(group_rows, heads * HD)
+    head_outs, norm_slot = lax.optimization_barrier((head_outs, norm_slot))
+    attended = head_outs.reshape(heads * HD, group_rows)
+    attended_all = lax.all_gather(attended, "sp", axis=0, tiled=True)
+    out_full = dp_join(out_own, out_came)
+    out_part = lax.dynamic_slice_in_dim(out_full, sp_at * heads * HD, heads * HD, 0)
     fc_part = dp_join(fc_own, fc_came)
     proj_part = dp_join(proj_own, proj_came)
 
@@ -505,10 +555,9 @@
     positions = (sp_at * ctx_count + ctx_at) * rows + jnp.arange(rows, dtype=jnp.int32)
     is_valid = (positions < lengths[0])[:, None]
 
-    branch = jnp.dot(attended, out_part, preferred_element_type=f32).astype(bf16)
-    mixed = inputs + exchange_sum(branch.reshape(seg_count, rows, width), "sp")
-    norm_two_own = layer_norm(mixed, gain_two).astype(bf16)
-    norm_two = lax.all_gather(norm_two_own, "sp", axis=0, tiled=True)
+    mixed_group = inputs_group + contract_rows(attended_all, out_full)
+    norm_two = layer_norm(mixed_group, gain_two).astype(bf16)
+    mixed = lax.dynamic_slice_in_dim(mixed_group, sp_at * rows, rows, 0)
     hidden_pre = jnp.dot(norm_two, fc_part, preferred_element_type=f32)
     active = tanh_gelu(hidden_pre).astype(bf16)
     grad_active = contract_cols(grad_out_group, proj_part)
@@ -517,8 +566,7 @@
     fc_parts = contract_rows(norm_two, grad_pre).astype(bf16).reshape(dp_count, ctx_count, piece, width)
     proj_parts = contract_rows(active, grad_out_group).astype(bf16).reshape(dp_count, ctx_count, -1, width)
     grad_pre, fc_parts, proj_parts = lax.optimization_barrier((grad_pre, fc_parts, proj_parts))
-    fc_dp = dp_scatter(fc_parts)
-    proj_dp = dp_scatter(proj_parts)
+    mlp_dp = dp_scatter(jnp.concatenate([fc_parts, proj_parts], axis=2))
     grad_norm_parts = contract_cols(grad_pre, fc_part).astype(bf16)
     grad_norm_two = exchange_sum(grad_norm_parts.reshape(seg_count, rows, width), "sp")
     _, second_pull = jax.vjp(layer_norm, mixed, gain_two)
@@ -529,64 +577,47 @@
 
     out_wide = jnp.pad(out_part.reshape(heads, HD, width), ((0, 0), (HD, 0), (0, 0))).reshape(heads * LANES, width)
     grad_wide = contract_cols(grad_branch, out_wide).astype(bf16)
-    out_mine = contract_rows(attended, grad_branch).astype(bf16)
-    grad_wide, fc_dp, out_mine = lax.optimization_barrier((grad_wide, fc_dp, out_mine))
+    out_mine = jnp.dot(attended, grad_branch, preferred_element_type=f32).astype(bf16)
+    grad_wide, mlp_dp, out_mine = lax.optimization_barrier((grad_wide, mlp_dp, out_mine))
     out_sum = dp_sum(out_mine)
-    fc_came = lax.all_to_all(fc_dp, "ctx", split_axis=0, concat_axis=0, tiled=True)
-    query_grads, pair_grads = attend_back(query_wide, grad_wide, pairs, prob)
-    query_grads, pair_grads, fc_came, proj_dp, out_sum = lax.optimization_barrier(
-        (query_grads, pair_grads, fc_came, proj_dp, out_sum)
-    )
+    mlp_came = lax.all_to_all(mlp_dp, "ctx", split_axis=0, concat_axis=0, tiled=True)
+    score_slot = jnp.transpose(
+        pairs[:, group_rows : group_rows + seg_count].reshape(ctx_count, seg_count, heads, rows), (2, 1, 0, 3)
+    ).reshape(heads, -1)
+    gain_cols = jnp.stack([gain_one, second_gain_grad], axis=1)
+    grad_wide, score_slot, gain_cols = lax.optimization_barrier((grad_wide, score_slot, gain_cols))
+    query_grads, pair_grads, turned, query_turned, gates = attend_back(query_wide, grad_wide, pairs, prob)
     pair_mine = lax.psum_scatter(pair_grads, "ctx", scatter_dimension=0, tiled=False)
-    late = jnp.concatenate([proj_dp, out_sum.reshape(ctx_count, -1, width)], axis=1)
-
-    def total(came):
-        return jnp.sum(came.astype(f32), axis=0).astype(bf16)
-
-    late, active_late = lax.optimization_barrier((late, active))
-    late_came = lax.all_to_all(late, "ctx", split_axis=0, concat_axis=0, tiled=True)
+    small = weight_grad(turned, query_turned, gates, score_slot, norm_slot, norm_one, all_in, gain_cols)
+    small, mlp_came, out_sum = lax.optimization_barrier((small, mlp_came, out_sum))
+    late = jnp.concatenate(
+        [dp_scatter(small.reshape(dp_count, ctx_count, piece, width)), out_sum.reshape(ctx_count, -1, width)], axis=1
+    )
+    late_sum = exchange_sum(late, "ctx").astype(bf16)
+    mlp_sum = jnp.sum(mlp_came.astype(f32), axis=0).astype(bf16)
+    gradients = jnp.concatenate([late_sum[:piece], mlp_sum, late_sum[piece:]], axis=0)
+    pair_mine, gradients, active_late = lax.optimization_barrier((pair_mine, gradients, active))
+    gathered = lax.all_gather(gradients, ("sp", "ctx"), axis=0, tiled=False).reshape(seg_count, ctx_count, -1, width)
+    proj_piece = hidden // (seg_count * dp_count * ctx_count)
+
+    grad_norm_part = finish(pair_mine, query_grads, key_score, all_in)
     expanded = exchange_sum(
         jnp.dot(active_late, proj_part, preferred_element_type=f32).astype(bf16).reshape(seg_count, rows, width), "sp"
     )
-    big = jnp.concatenate([total(fc_came), total(late_came)], axis=0)
-    norm_t = jnp.transpose(norm_one)
-    gain_cols = jnp.stack([gain_one, second_gain_grad], axis=1)
-    pair_mine, big, expanded, norm_t, gain_cols = lax.optimization_barrier(
-        (pair_mine, big, expanded, norm_t, gain_cols)
-    )
     output = jnp.where(is_valid, mixed + expanded, 0.0).astype(bf16)[None]
-    big_all = lax.all_gather(big, ("sp", "ctx"), axis=0, tiled=False).reshape(seg_count, ctx_count, -1, width)
-    proj_piece = hidden // (seg_count * dp_count * ctx_count)
-    both = piece + proj_piece
-
-    small, grad_norm_part = finish(norm_t, pair_mine, query_grads, key_score, all_in, gain_cols)
-    small_own = exchange_sum(
-        dp_scatter(small.reshape(dp_count, ctx_count, piece, wide)), "ctx"
-    ).astype(bf16)
-    small_own, big_all, grad_norm_part = lax.optimization_barrier((small_own, big_all, grad_norm_part))
     grad_norm_one = exchange_sum(grad_norm_part.reshape(seg_count, rows, width), "sp")
     _, first_pull = jax.vjp(lambda values: layer_norm(values, gain_one), inputs)
     grad_input_norm = first_pull(grad_norm_one)[0]
     input_grad = (grad_mixed + grad_input_norm).astype(bf16)[None]
 
-    small_all = lax.all_gather(small_own, ("sp", "ctx"), axis=0, tiled=False).reshape(
-        seg_count, ctx_count * piece, wide
-    )
-    groups = range(seg_count)
-    fc_grad = jnp.concatenate(
-        [
-            big_all[at, :, :piece, part * hidden_part : (part + 1) * hidden_part].reshape(-1, hidden_part)
-            for part in range(dp_count)
-            for at in groups
-        ],
-        axis=1,
+    qkv_grad, score_grad, fc_grad, proj_grad = unpack(gathered, heads, piece, proj_piece, dp_count, hidden)
+    proj_grad = proj_grad.reshape(-1, width)
+    out_grad = lax.dynamic_slice_in_dim(
+        gathered[:, :, 2 * piece + proj_piece :].reshape(width, width), dp_at * weight_rows, weight_rows, 0
     ).astype(f32)
-    proj_grad = big_all[:, :, piece:both].reshape(hidden // dp_count, width).astype(f32)
-    out_grad = lax.dynamic_slice_in_dim(
-        big_all[:, :, both:].reshape(width, width), dp_at * (width // dp_count), width // dp_count, 0
-    ).astype(f32)
-    qkv_grad, score_grad = unpack(small_all, heads)
-    gains = jnp.sum(small_all[:, :, head_cols + heads : head_cols + heads + 2].astype(f32), axis=0)
+    gains = jnp.sum(
+        gathered[:, :, :piece, head_cols + heads : head_cols + heads + 2].astype(f32), axis=0
+    ).reshape(weight_rows, 2)
     return (output, input_grad, gains[:, 0], qkv_grad, score_grad, out_grad, gains[:, 1], fc_grad, proj_grad)
 
 

time: 393 us -> 370 us (0.941)
  blocking collectives: 48.7 us -> 33.5 us
  Pallas kernels: 73.2 us -> 83.4 us
  other arithmetic: 34.7 us -> 24.7 us
  starting transfers between devices: 34.7 us -> 27.7 us
    ppermute x2 -> x3, waiting for transfers between devices: 0.01 us -> 28.6 us  [dp_send(): return lax.ppermute(mine, 'dp', [(0, 1), (1, 0)])]
    all_to_all x2 -> x1, waiting for transfers between devices: 26.2 us -> 3.71 us  [per_device(): lax.all_to_all(mlp_dp, 'ctx', split_axis=0, concat_axis=0, tiled=True)]
    ppermute x1 -> x0, waiting for transfers between devices: 22.4 us -> none  [group_rows_of(): far = lax.ppermute(near, 'dp', [(0, 1), (1, 0)])]
    all_to_all x1 -> x0, blocking collectives: 14.9 us -> none  [exchange_sum(): came = lax.all_to_all(parts, axis, split_axis=0, concat_axis=0, tiled=True)]
    all_to_all x4, waiting for transfers between devices: 44.4 us -> 57.5 us  [exchange_sum(): came = lax.all_to_all(parts, axis, split_axis=0, concat_axis=0, tiled=True)]
    pallas_call x2 -> x3, Pallas kernels: 8.63 us -> 18.1 us  [the longest x1 8.44 us: unpack(): pl.pallas_call(functools.partial(unpack_kernel, groups, heads, piece, par...]
    ppermute x3 -> x2, waiting for transfers between devices: 11.6 us -> 19 us  [dp_scatter(): other = lax.ppermute(sent, 'dp', [(0, 1), (1, 0)])]
    convert_element_type x5 -> x2, other arithmetic: 7.69 us -> 1.39 us  [the longest x1 1.09 us: per_device(): out_grad = lax.dynamic_slice_in_dim(gathered[:, :, 2 * piece + proj_piece...]
  transfers between devices with their start and end apart: 18 -> 16, of which waited for: 9 -> 12; matrix products, arithmetic and copies ran while one was open for 14% -> 10% of each run, Pallas kernels for 5% -> 20%
where the time goes in v1:
time: 370 us; the launch traced here: 369 us
  waiting for transfers between devices  140 us (38%)
  Pallas kernels  83.4 us (23%)
  blocking collectives  33.5 us (9%)
  starting transfers between devices  27.7 us (7%)
  other arithmetic  24.7 us (7%)
  local copies, waits for them, and re-layouts  22.6 us (6%)
  matrix products  21.8 us (6%)
  between operations  15 us (4%)
    all_to_all x4, waiting for transfers between devices, exchange_sum(): came = lax.all_to_all(parts, axis, split_axis=0, concat_axis=0, tiled=True)  57.5 us
    pallas_call x1, Pallas kernels, attend(): pl.pallas_call(functools.partial(attend_kernel, parts, chunk), grid_spec=...  48.8 us
    all_gather x1, waiting for transfers between devices, per_device(): lax.all_gather(gradients, ('sp', 'ctx'), axis=0, tiled=False)  30.6 us
    ppermute x3, waiting for transfers between devices, dp_send(): return lax.ppermute(mine, 'dp', [(0, 1), (1, 0)])  28.6 us
    ppermute x2, waiting for transfers between devices, dp_scatter(): other = lax.ppermute(sent, 'dp', [(0, 1), (1, 0)])  19 us
    all_to_all x4, starting transfers between devices, exchange_sum(): came = lax.all_to_all(parts, axis, split_axis=0, concat_axis=0, tiled=True)  15.5 us
    pallas_call x1, Pallas kernels, attend_back(): pl.pallas_call(functools.partial(attend_back_kernel, parts, chunk), grid=...  14.4 us
    all_gather x1, blocking collectives, per_device(): tokens_group = lax.all_gather(tokens[0], 'sp', axis=0, tiled=True)  8.61 us
  transfers between devices with their start and end apart: 16, of which 12 were waited for; matrix products, arithmetic and copies ran while one was open for 10% of the time, Pallas kernels for 20%

profile of v1, /device:TPU:0, one launch (start us, length us, event | category | flops | bytes accessed | tf_op | source)
XLA Modules:
  0.0 368.9 jit_solution(10700179280103846581)
XLA Ops:
  14.0 3.0 collective-permute-start
  16.9 8.6 %all-gather = bf16[1,512,768]{2,1,0:T(8,128)(2,1)S(1)} all-gather(bf16[1,128,768]{2,1,0:T(8,128)(2,1)S(1)} %copy-done.6), channel_id=2, replica_groups=mesh['dp'=2,'sp'=4,'ctx'=4] {'sp'}, dimensions={1}, use_global_device_ids=true | all-gather | bytes 983040 | tf_op jit(solution)/shard_map/all_gather | solution.py:498
  26.9 2.2 pad_maximum_fusion.2
  37.1 8.6 %all_gather.28 = bf16[512,768]{1,0:T(8,128)(2,1)S(1)} all-gather(bf16[128,768]{1,0:T(8,128)(2,1)S(1)} %bitcast.114), channel_id=1, replica_groups=mesh['dp'=2,'sp'=4,'ctx'=4] {'sp'}, dimensions={0}, use_global_device_ids=true | all-gather | bytes 983040 | tf_op jit(solution)/shard_map/all_gather | solution.py:536
  45.7 3.9 %collective-permute-done.1 = bf16[384,768]{1,0:T(8,128)(2,1)} collective-permute-done((bf16[384,768]{1,0:T(8,128)(2,1)}, bf16[384,768]{1,0:T(8,128)(2,1)}, u32[]{:S(2)}, u32[]{:S(2)}) %collective-permute-start.1) | collective-permute-done | bytes 589856 | tf_op jit(solution)/shard_map/ppermute | solution.py:410
  49.6 12.6 %collective-permute-done.2 = bf16[384,768]{1,0:T(8,128)(2,1)} collective-permute-done((bf16[384,768]{1,0:T(8,128)(2,1)}, bf16[384,768]{1,0:T(8,128)(2,1)}, u32[]{:S(2)}, u32[]{:S(2)}) %collective-permute-start.2) | collective-permute-done | bytes 589856 | tf_op jit(solution)/shard_map/ppermute | solution.py:410
  62.3 12.0 %collective-permute-done.3 = bf16[384,768]{1,0:T(8,128)(2,1)} collective-permute-done((bf16[384,768]{1,0:T(8,128)(2,1)}, bf16[384,768]{1,0:T(8,128)(2,1)}, u32[]{:S(2)}, u32[]{:S(2)}) %collective-permute-start.3) | collective-permute-done | bytes 589856 | tf_op jit(solution)/shard_map/ppermute | solution.py:410
  82.0 48.8 %attend.1 = (bf16[3,64,512]{2,1,0:T(8,128)(2,1)}, bf16[3,4,128,2048]{3,2,1,0:T(8,128)(2,1)}) custom-call(s32[1]{0:T(128)} %bitcast.2.base_ref, s32[3,4,128,64]{3,2,1,0:T(8,128)} %bitcast.110, bf16[512,384]{1,0:T(8,128)(2,1)} %copy.37.refs_1_.refs_0_, bf16[4,528,384]{2,1,0:T(8,128)(2,1)} %bitcast.105), custom_call_target="tpu_custom_call" | custom-call | tf_op jit(solution)/shard_map/attend/pallas_call | solution.py:172
  130.8 8.3 %all_gather.32 = bf16[768,512]{1,0:T(8,128)(2,1)S(1)} all-gather(bf16[192,512]{1,0:T(8,128)(2,1)} %bitcast.122), channel_id=1, replica_groups=mesh['dp'=2,'sp'=4,'ctx'=4] {'sp'}, dimensions={0}, use_global_device_ids=true | all-gather | bytes 983040 | tf_op jit(solution)/shard_map/all_gather | solution.py:546
  142.4 2.5 multiply_convert_fusion
  146.8 2.9 fusion.14
  151.7 3.0 convolution_convert_fusion.3
  154.6 3.5 all-to-all-start
  161.9 7.8 %all-to-all-done = bf16[4,128,768]{2,1,0:T(8,128)(2,1)S(1)} async-done(((bf16[4,128,768]{2,1,0:T(8,128)(2,1)}), bf16[4,128,768]{2,1,0:T(8,128)(2,1)S(1)}, u32[]{:S(2)}, u32[]{:S(2)}) %all-to-all-start) | async-done | bytes 786464 | tf_op jit(solution)/shard_map/all_to_all | solution.py:449
  171.0 8.0 %all_gather.33 = bf16[512,768]{1,0:T(8,128)(2,1)S(1)} all-gather(bf16[128,768]{1,0:T(8,128)(2,1)S(1)} %fusion.25), channel_id=1, replica_groups=mesh['dp'=2,'sp'=4,'ctx'=4] {'sp'}, dimensions={0}, use_global_device_ids=true | all-gather | bytes 983040 | tf_op jit(solution)/shard_map/all_gather | solution.py:576
  181.4 8.3 %collective-permute-done.4 = bf16[4,192,768]{2,1,0:T(8,128)(2,1)} collective-permute-done((bf16[4,192,768]{2,1,0:T(8,128)(2,1)}, bf16[4,192,768]{2,1,0:T(8,128)(2,1)}, u32[]{:S(2)}, u32[]{:S(2)}) %collective-permute-start.4) | collective-permute-done | bytes 1179680 | tf_op jit(solution)/shard_map/ppermute | solution.py:427
  189.7 2.6 fusion
  192.3 4.9 %all-to-all-start.1 = ((bf16[4,192,768]{2,1,0:T(8,128)(2,1)}), bf16[4,192,768]{2,1,0:T(8,128)(2,1)S(1)}, u32[]{:S(2)}, u32[]{:S(2)}) async-start(bf16[4,192,768]{2,1,0:T(8,128)(2,1)} %fusion), calls=%async_computation.2 | async-start | bytes 2359296 | tf_op jit(solution)/shard_map/all_to_all | solution.py:583
  200.5 14.4 %attend_back.1 = (bf16[512,384]{1,0:T(8,128)(2,1)}, bf16[4,528,384]{2,1,0:T(8,128)(2,1)}, bf16[3,128,2048]{2,1,0:T(8,128)(2,1)}, bf16[3,64,512]{2,1,0:T(8,128)(2,1)}, f32[3,8,2048]{2,1,0:T(8,128)}) custom-call(bf16[512,384]{1,0:T(8,128)(2,1)} %copy.37.refs_1_.refs_0_, bf16[512,384]{1,0:T(8,128)(2,1)} %convolution_convert_fusion.5.refs_1_, ...), custom_call_target="tpu_custom_call" | custom-call | tf_op jit(solution)/shard_map/attend_back/pallas_call | solution.py:243
  216.5 6.4 %weight_grad.1 = bf16[768,768]{1,0:T(8,128)(2,1)} custom-call(bf16[3,128,2048]{2,1,0:T(8,128)(2,1)} %get-tuple-element.72.turned_ref, bf16[3,64,512]{2,1,0:T(8,128)(2,1)} %get-tuple-element.73.dq_ref, f32[3,8,2048]{2,1,0:T(8,128)} %get-tuple-element.74.gates_ref, bf16[3,2048]{1,0:T(4,128)(2,1)} %reshape.259.score_ref, ...), custom_call_target="tpu_custom_call" | custom-call | tf_op jit(solution)/shard_map/weight_grad/pallas_call | solution.py:301
  225.4 3.7 %all-to-all-done.1 = bf16[4,192,768]{2,1,0:T(8,128)(2,1)S(1)} async-done(((bf16[4,192,768]{2,1,0:T(8,128)(2,1)}), bf16[4,192,768]{2,1,0:T(8,128)(2,1)S(1)}, u32[]{:S(2)}, u32[]{:S(2)}) %all-to-all-start.1) | async-done | bytes 1179680 | tf_op jit(solution)/shard_map/all_to_all | solution.py:583
  230.5 10.7 %collective-permute-done.6 = bf16[4,96,768]{2,1,0:T(8,128)(2,1)S(1)} collective-permute-done((bf16[4,96,768]{2,1,0:T(8,128)(2,1)S(1)}, bf16[4,96,768]{2,1,0:T(8,128)(2,1)S(1)}, u32[]{:S(2)}, u32[]{:S(2)}) %collective-permute-start.6) | collective-permute-done | bytes 589856 | tf_op jit(solution)/shard_map/ppermute | solution.py:427
  242.3 4.2 %all-to-all-start.2 = ((bf16[4,144,768]{2,1,0:T(8,128)(2,1)}), bf16[4,144,768]{2,1,0:T(8,128)(2,1)}, u32[]{:S(2)}, u32[]{:S(2)}) async-start(bf16[4,144,768]{2,1,0:T(8,128)(2,1)} %pad_maximum_fusion.1), calls=%async_computation.3 | async-start | bytes 1769472 | tf_op jit(solution)/shard_map/all_to_all | solution.py:449
  247.5 23.3 %all-to-all-done.2 = bf16[4,144,768]{2,1,0:T(8,128)(2,1)} async-done(((bf16[4,144,768]{2,1,0:T(8,128)(2,1)}), bf16[4,144,768]{2,1,0:T(8,128)(2,1)}, u32[]{:S(2)}, u32[]{:S(2)}) %all-to-all-start.2) | async-done | bytes 884768 | tf_op jit(solution)/shard_map/all_to_all | solution.py:449
  273.0 3.3 finish.1
  276.3 3.5 all-to-all-start.4
  279.9 3.6 convolution_convert_fusion.2
  283.6 12.5 %all-to-all-done.4 = bf16[4,128,768]{2,1,0:T(8,128)(2,1)S(1)} async-done(((bf16[4,128,768]{2,1,0:T(8,128)(2,1)}), bf16[4,128,768]{2,1,0:T(8,128)(2,1)S(1)}, u32[]{:S(2)}, u32[]{:S(2)}) %all-to-all-start.4) | async-done | bytes 786464 | tf_op jit(solution)/shard_map/all_to_all | solution.py:449
  296.1 4.2 %all-to-all-start.3 = ((bf16[4,128,768]{2,1,0:T(8,128)(2,1)}), bf16[4,128,768]{2,1,0:T(8,128)(2,1)}, u32[]{:S(2)}, u32[]{:S(2)}) async-start(bf16[4,128,768]{2,1,0:T(8,128)(2,1)} %bitcast.120), calls=%async_computation.4 | async-start | bytes 1572864 | tf_op jit(solution)/shard_map/all_to_all | solution.py:449
  300.9 13.9 %all-to-all-done.3 = bf16[4,128,768]{2,1,0:T(8,128)(2,1)} async-done(((bf16[4,128,768]{2,1,0:T(8,128)(2,1)}), bf16[4,128,768]{2,1,0:T(8,128)(2,1)}, u32[]{:S(2)}, u32[]{:S(2)}) %all-to-all-start.3) | async-done | bytes 786464 | tf_op jit(solution)/shard_map/all_to_all | solution.py:449
  317.1 30.6 %all-gather.11.cloned.1.call-done = bf16[5376,768]{1,0:T(8,128)(2,1)} async-done(((bf16[336,768]{1,0:T(8,128)(2,1)}), bf16[5376,768]{1,0:T(8,128)(2,1)}) %all-gather.11.cloned.1.call-update) | async-done | bytes 8257552 | tf_op jit(solution)/shard_map/all_gather | solution.py:600
  350.3 8.4 %unpack.1 = (f32[384,2304]{1,0:T(8,128)}, f32[384,12]{1,0:T(8,128)}, f32[384,3072]{1,0:T(8,128)}, f32[4,4,96,768]{3,2,1,0:T(8,128)}) custom-call(bf16[4,4,336,768]{3,2,1,0:T(8,128)(2,1)} %bitcast.104), custom_call_target="tpu_custom_call" | custom-call | tf_op jit(solution)/shard_map/unpack/pallas_call | solution.py:364
  (160 shorter events, 59.5 us)
Async XLA Ops:
  7.2 9.7 %copy-start.6 = (bf16[1,128,768]{2,1,0:T(8,128)(2,1)S(1)}, bf16[1,128,768]{2,1,0:T(8,128)(2,1)}, u32[]{:S(2)}) copy-start(bf16[1,128,768]{2,1,0:T(8,128)(2,1)} %param.11) | copy-start | bytes 589828
  7.2 67.1 %all-gather.9.cloned.1.call-start = ((), (), s32[]{:S(2)}) async-start(), calls=%async_computation.8 | async-start | bytes 2027520 | tf_op jit(solution)/shard_map/all_gather | solution.py:537
  14.0 15.5 %collective-permute-start = (bf16[400,640]{1,0:T(8,128)(2,1)}, bf16[400,640]{1,0:T(8,128)(2,1)S(1)}, u32[]{:S(2)}, u32[]{:S(2)}) collective-permute-start(bf16[400,640]{1,0:T(8,128)(2,1)} %arrange.1), channel_id=1, source_target_pairs={{0,16},{16,0},{1,17},{17,1},{2,18},{18,2},{3,19},{19,3},{4,20},{20... | collective-permute-start | bytes 1536008 | tf_op jit(solution)/shard_map/ppermute | solution.py:492
  30.7 5.7 %copy-start.3 = (bf16[512,768]{1,0:T(8,128)(2,1)}, bf16[512,768]{1,0:T(8,128)(2,1)S(1)}, u32[]{:S(2)}) copy-start(bf16[512,768]{1,0:T(8,128)(2,1)S(1)} %fusion.7.norm_ref) | copy-start | bytes 2359300
  33.0 97.8 %all-gather.7.cloned.1.call-start = ((), (), s32[]{:S(2)}) async-start(), calls=%async_computation.6 | async-start | bytes 3342336 | tf_op jit(solution)/shard_map/all_gather | solution.py:542
  33.0 16.6 %collective-permute-start.1 = (bf16[384,768]{1,0:T(8,128)(2,1)}, bf16[384,768]{1,0:T(8,128)(2,1)}, u32[]{:S(2)}, u32[]{:S(2)}) collective-permute-start(bf16[384,768]{1,0:T(8,128)(2,1)} %param.18), channel_id=1, source_target_pairs={{0,16},{16,0},{1,17},{17,1},{2,18},{18,2},{3,19},{19,3},{4,20},{20... | collective-permute-start | bytes 1769480 | tf_op jit(solution)/shard_map/ppermute | solution.py:410
  34.1 28.1 %collective-permute-start.2 = (bf16[384,768]{1,0:T(8,128)(2,1)}, bf16[384,768]{1,0:T(8,128)(2,1)}, u32[]{:S(2)}, u32[]{:S(2)}) collective-permute-start(bf16[384,768]{1,0:T(8,128)(2,1)} %get-tuple-element.53), channel_id=1, source_target_pairs={{0,16},{16,0},{1,17},{17,1},{2,18},{18,2},{3,19},{19,3},{4,20},{20... | collective-permute-start | bytes 1769480 | tf_op jit(solution)/shard_map/ppermute | solution.py:410
  35.1 39.2 %collective-permute-start.3 = (bf16[384,768]{1,0:T(8,128)(2,1)}, bf16[384,768]{1,0:T(8,128)(2,1)}, u32[]{:S(2)}, u32[]{:S(2)}) collective-permute-start(bf16[384,768]{1,0:T(8,128)(2,1)} %get-tuple-element.54), channel_id=1, source_target_pairs={{0,16},{16,0},{1,17},{17,1},{2,18},{18,2},{3,19},{19,3},{4,20},{20... | collective-permute-start | bytes 1769480 | tf_op jit(solution)/shard_map/ppermute | solution.py:410
  36.3 41.9 %copy-start.19 = (bf16[384]{0:T(512)(128)(2,1)S(1)}, bf16[384]{0:T(512)(128)(2,1)}, u32[]{:S(2)}) copy-start(bf16[384]{0:T(512)(128)(2,1)} %get-tuple-element.122) | copy-start | bytes 2308
  36.3 41.9 %copy-start.20 = (bf16[384]{0:T(512)(128)(2,1)S(1)}, bf16[384]{0:T(512)(128)(2,1)}, u32[]{:S(2)}) copy-start(bf16[384]{0:T(512)(128)(2,1)} %get-tuple-element.146) | copy-start | bytes 2308
  81.0 49.8 %copy-start.9 = (bf16[768,768]{1,0:T(8,128)(2,1)}, bf16[768,768]{1,0:T(8,128)(2,1)S(1)}, u32[]{:S(2)}) copy-start(bf16[768,768]{1,0:T(8,128)(2,1)S(1)} %maximum_select_fusion) | copy-start | bytes 3538948
  154.6 15.1 %all-to-all-start = ((bf16[4,128,768]{2,1,0:T(8,128)(2,1)}), bf16[4,128,768]{2,1,0:T(8,128)(2,1)S(1)}, u32[]{:S(2)}, u32[]{:S(2)}) async-start(bf16[4,128,768]{2,1,0:T(8,128)(2,1)} %bitcast.14), calls=%async_computation | async-start | bytes 1572864 | tf_op jit(solution)/shard_map/all_to_all | solution.py:449
  161.1 28.7 %collective-permute-start.4 = (bf16[4,192,768]{2,1,0:T(8,128)(2,1)}, bf16[4,192,768]{2,1,0:T(8,128)(2,1)}, u32[]{:S(2)}, u32[]{:S(2)}) collective-permute-start(bf16[4,192,768]{2,1,0:T(8,128)(2,1)} %dynamic-slice_bitcast_fusion), channel_id=1, source_target_pairs={{0,16},{16,0},{1,17},{17,1},{2,18},{18,2},{3,19},{19,3},{4,20},{20... | collective-permute-start | bytes 3538952 | tf_op jit(solution)/shard_map/ppermute | solution.py:427
  161.9 9.0 %copy-start.21 = (pred[128]{0:T(512)(128)(4,1)S(1)}, pred[128]{0:T(512)(128)(4,1)}, u32[]{:S(2)}) copy-start(pred[128]{0:T(512)(128)(4,1)} %add_compare_fusion) | copy-start | bytes 388
  170.6 8.4 %copy-start.14 = (bf16[3,64,512]{2,1,0:T(8,128)(2,1)S(1)}, bf16[3,64,512]{2,1,0:T(8,128)(2,1)}, u32[]{:S(2)}) copy-start(bf16[3,64,512]{2,1,0:T(8,128)(2,1)} %get-tuple-element.60) | copy-start | bytes 589828
  170.8 9.2 %copy-start.17 = (bf16[3,128,768]{2,1,0:T(8,128)(2,1)S(1)}, bf16[3,128,768]{2,1,0:T(8,128)(2,1)}, u32[]{:S(2)}) copy-start(bf16[3,128,768]{2,1,0:T(8,128)(2,1)} %pad.19) | copy-start | bytes 1769476
  170.9 10.6 %copy-start.23 = (f32[128]{0:T(128)}, f32[128]{0:T(128)S(1)}, u32[]{:S(2)}) copy-start(f32[128]{0:T(128)S(1)} %negate_multiply_fusion.1) | copy-start | bytes 1540
  179.0 10.7 %copy-start.5 = (bf16[2,4,192,768]{3,2,1,0:T(8,128)(2,1)S(1)}, bf16[2,4,192,768]{3,2,1,0:T(8,128)(2,1)}, u32[]{:S(2)}) copy-start(bf16[2,4,192,768]{3,2,1,0:T(8,128)(2,1)} %copy-done.4) | copy-start | bytes 7077892
  192.3 36.8 %all-to-all-start.1 = ((bf16[4,192,768]{2,1,0:T(8,128)(2,1)}), bf16[4,192,768]{2,1,0:T(8,128)(2,1)S(1)}, u32[]{:S(2)}, u32[]{:S(2)}) async-start(bf16[4,192,768]{2,1,0:T(8,128)(2,1)} %fusion), calls=%async_computation.2 | async-start | bytes 2359296 | tf_op jit(solution)/shard_map/all_to_all | solution.py:583
  197.2 75.8 %reduce-scatter.2.cloned.1.call-start = ((), (), s32[]{:S(2)}) async-start(), calls=%async_computation.7 | async-start | bytes 2027520 | tf_op jit(solution)/shard_map/reduce_scatter | solution.py:590
  215.0 8.6 %collective-permute-start.5 = (bf16[192,768]{1,0:T(8,128)(2,1)}, bf16[192,768]{1,0:T(8,128)(2,1)}, u32[]{:S(2)}, u32[]{:S(2)}) collective-permute-start(bf16[192,768]{1,0:T(8,128)(2,1)} %convolution_convert_fusion.6), channel_id=1, source_target_pairs={{0,16},{16,0},{1,17},{17,1},{2,18},{18,2},{3,19},{19,3},{4,20},{20... | collective-permute-start | bytes 884744 | tf_op jit(solution)/shard_map/ppermute | solution.py:444
  229.2 12.0 %copy-start.7 = (bf16[768,768]{1,0:T(8,128)(2,1)S(1)}, bf16[768,768]{1,0:T(8,128)(2,1)}, u32[]{:S(2)}) copy-start(bf16[768,768]{1,0:T(8,128)(2,1)} %weight_grad.1) | copy-start | bytes 3538948
  229.2 12.1 %copy-start.11 = (bf16[192,768]{1,0:T(8,128)(2,1)S(1)}, bf16[192,768]{1,0:T(8,128)(2,1)}, u32[]{:S(2)}) copy-start(bf16[192,768]{1,0:T(8,128)(2,1)} %add_convert_fusion) | copy-start | bytes 884740
  230.4 10.8 %collective-permute-start.6 = (bf16[4,96,768]{2,1,0:T(8,128)(2,1)S(1)}, bf16[4,96,768]{2,1,0:T(8,128)(2,1)S(1)}, u32[]{:S(2)}, u32[]{:S(2)}) collective-permute-start(bf16[4,96,768]{2,1,0:T(8,128)(2,1)S(1)} %dynamic-slice_bitcast_fusion.1), channel_id=1, source_target_pairs={{0,16},{16,0},{1,17},{17,1},{2,18},{18,2},{3,19},{19,3},{4,20},{20... | collective-permute-start | bytes 1769480 | tf_op jit(solution)/shard_map/ppermute | solution.py:427
  242.3 28.5 %all-to-all-start.2 = ((bf16[4,144,768]{2,1,0:T(8,128)(2,1)}), bf16[4,144,768]{2,1,0:T(8,128)(2,1)}, u32[]{:S(2)}, u32[]{:S(2)}) async-start(bf16[4,144,768]{2,1,0:T(8,128)(2,1)} %pad_maximum_fusion.1), calls=%async_computation.3 | async-start | bytes 1769472 | tf_op jit(solution)/shard_map/all_to_all | solution.py:449
  246.5 101.3 %all-gather.11.cloned.1.call-start = ((), (), s32[]{:S(2)}) async-start(), calls=%async_computation.9 | async-start | bytes 8773632 | tf_op jit(solution)/shard_map/all_gather | solution.py:600
  247.5 24.7 %copy-start.13 = (bf16[192,768]{1,0:T(8,128)(2,1)S(1)}, bf16[192,768]{1,0:T(8,128)(2,1)}, u32[]{:S(2)}) copy-start(bf16[192,768]{1,0:T(8,128)(2,1)} %reduce_sum.208) | copy-start | bytes 884740
  276.3 19.8 %all-to-all-start.4 = ((bf16[4,128,768]{2,1,0:T(8,128)(2,1)}), bf16[4,128,768]{2,1,0:T(8,128)(2,1)S(1)}, u32[]{:S(2)}, u32[]{:S(2)}) async-start(bf16[4,128,768]{2,1,0:T(8,128)(2,1)} %bitcast.111), calls=%async_computation.5 | async-start | bytes 1572864 | tf_op jit(solution)/shard_map/all_to_all | solution.py:449
  296.1 18.7 %all-to-all-start.3 = ((bf16[4,128,768]{2,1,0:T(8,128)(2,1)}), bf16[4,128,768]{2,1,0:T(8,128)(2,1)}, u32[]{:S(2)}, u32[]{:S(2)}) async-start(bf16[4,128,768]{2,1,0:T(8,128)(2,1)} %bitcast.120), calls=%async_computation.4 | async-start | bytes 1572864 | tf_op jit(solution)/shard_map/all_to_all | solution.py:449
  300.3 15.8 %copy-start.22 = (pred[128]{0:T(512)(128)(4,1)S(1)}, pred[128]{0:T(512)(128)(4,1)}, u32[]{:S(2)}) copy-start(pred[128]{0:T(512)(128)(4,1)} %add_compare_fusion) | copy-start | bytes 388
  300.3 15.8 %copy-start.24 = (f32[128]{0:T(128)S(1)}, f32[128]{0:T(128)}, u32[]{:S(2)}) copy-start(f32[128]{0:T(128)} %copy-done.23) | copy-start | bytes 1540
  350.3 12.0 %copy-start.1 = (bf16[384,2304]{1,0:T(8,128)(2,1)S(1)}, bf16[384,2304]{1,0:T(8,128)(2,1)}, u32[]{:S(2)}) copy-start(bf16[384,2304]{1,0:T(8,128)(2,1)} %param.16) | copy-start | bytes 5308420
  (11 other events, 24.9 us)
Sparse Core Ops, SparseCore 0:
  33.1 38.6 all-gather.8
  74.6 44.8 all-gather.6
  215.1 44.8 reduce-scatter.1
  273.1 74.5 all-gather.10

commit v2 on v1

--- a/solution.py
+++ b/solution.py
@@ -44,30 +44,13 @@
 
 
 PAD_ROWS = 16
-
-
-def slot_order(src_ref, kv_ref):
-    count, height, _ = src_ref.shape
-    for tile in range(kv_ref.shape[0] // LANES):
-        part, at = divmod(tile, count)
-        kv_ref[tile * LANES : (tile + 1) * LANES, :] = src_ref[at, part * LANES : (part + 1) * LANES, :]
-
-
-def slot_gates(src_ref, gate_ref):
-    count, height, _ = src_ref.shape
-    for at in range(count):
-        scores = src_ref[at, height - PAD_ROWS :, :].astype(jnp.float32)
-        gates = -jnp.log1p(jnp.exp(-scores))
-        for part in range(gate_ref.shape[1] // LANES // count):
-            tile = part * count + at
-            gate_ref[:, tile * LANES : (tile + 1) * LANES] = jnp.broadcast_to(gates[part : part + 1, :], (8, LANES))
-
-
-def attend_body(first, tiles, base, idx_ref, q_ref, src_ref, out_ref, prob_ref, score_ref, pair_ref, kv_ref, gate_ref):
+STEP = 128
+
+
+def attend_body(first, tiles, base, idx_ref, q_ref, kv_ref, key_ref, out_ref, prob_ref, score_ref, pair_ref, gate_ref):
     rows = q_ref.shape[0]
     if first:
-        slot_order(src_ref, kv_ref)
-        slot_gates(src_ref, gate_ref)
+        gate_ref[...] = jnp.broadcast_to(-jnp.log1p(jnp.exp(-key_ref[0].astype(jnp.float32))), gate_ref.shape)
     span = tiles * LANES
     f32, bf16 = jnp.float32, jnp.bfloat16
     score_ref[:, :span] = (
@@ -123,15 +106,19 @@
         return [expo * inverse for expo in expos]
 
     def step(index, carry):
-        start = pl.multiple_of(index * 16, 16)
-        first, second = eight(start), eight(start + 8)
-        for tile in range(tiles):
-            prob_ref[0, 0, pl.ds(start, 16), tile * LANES : (tile + 1) * LANES] = jnp.concatenate(
-                [first[tile], second[tile]], axis=0
-            ).astype(bf16)
+        for at in range(0, STEP, 16):
+            start = pl.multiple_of(index * STEP + at, 16)
+            near, next_to = eight(start), eight(start + 8)
+            for tile in range(tiles):
+                prob_ref[0, 0, pl.ds(start, 16), tile * LANES : (tile + 1) * LANES] = jnp.concatenate(
+                    [near[tile], next_to[tile]], axis=0
+                ).astype(bf16)
         return carry
 
-    lax.fori_loop(0, rows // 16, step, 0)
+    if rows == STEP:
+        step(0, 0)
+    else:
+        lax.fori_loop(0, rows // STEP, step, 0)
     both = jnp.dot(prob_ref[0, 0, :, :span], kv_ref[:span, :], preferred_element_type=f32)
     out_ref[0] = jnp.transpose(both)[HD:, :].astype(bf16)
 
@@ -145,10 +132,9 @@
         )
 
 
-def attend(base, kept, query, pairs):
+def attend(base, kept, query, pairs, key_score):
     heads, parts, block, keep = kept.shape
-    count, height, _ = pairs.shape
-    slot = count * (height - PAD_ROWS)
+    slot = pairs.shape[0]
     chunk = slot // parts
     grid_spec = pltpu.PrefetchScalarGridSpec(
         num_scalar_prefetch=1,
@@ -156,7 +142,8 @@
         in_specs=[
             pl.BlockSpec((1, 1, block, keep), lambda h, r, b: (h, r, 0, 0)),
             pl.BlockSpec((block, LANES), lambda h, r, b: (r, h)),
-            pl.BlockSpec((count, height, LANES), lambda h, r, b: (0, 0, h)),
+            pl.BlockSpec((slot, LANES), lambda h, r, b: (0, h)),
+            pl.BlockSpec((1, 1, slot), lambda h, r, b: (h, 0, 0)),
         ],
         out_specs=[
             pl.BlockSpec((1, HD, block), lambda h, r, b: (h, 0, r)),
@@ -165,7 +152,6 @@
         scratch_shapes=[
             pltpu.VMEM((block, slot), jnp.float32),
             pltpu.VMEM((block, 2 * keep), jnp.int32),
-            pltpu.VMEM((slot, LANES), jnp.bfloat16),
             pltpu.VMEM((8, slot), jnp.float32),
         ],
     )
@@ -177,15 +163,14 @@
             jax.ShapeDtypeStruct((heads, parts, block, slot), jnp.bfloat16),
         ],
         name="attend",
-    )(base, kept, query, pairs)
-
-
-def attend_back_body(first, last, tiles, chunk, q_ref, grad_ref, src_ref, prob_ref, dq_ref, out_ref, turned_ref, dq_turned_ref, gates_ref, raw_ref, kv_ref, dkv_ref, gate_ref):
+    )(base, kept, query, pairs, key_score)
+
+
+def attend_back_body(first, last, tiles, chunk, q_ref, grad_ref, kv_ref, prob_ref, dq_ref, out_ref, turned_ref, dq_turned_ref, gates_ref, raw_ref, dkv_ref, gate_ref):
     f32, bf16 = jnp.float32, jnp.bfloat16
     rows = q_ref.shape[0]
     steps = tiles * LANES // chunk
     if first:
-        slot_order(src_ref, kv_ref)
         dkv_ref[...] = jnp.zeros_like(dkv_ref)
         gate_ref[...] = jnp.zeros_like(gate_ref)
     dot_sum = None
@@ -236,9 +221,10 @@
         )
 
 
-def attend_back(query, grad, pairs, prob):
+def attend_back(count, query, grad, pairs, prob):
     heads, parts, block, slot = prob.shape
-    count, height, width = pairs.shape
+    width = pairs.shape[1]
+    height = slot // count + PAD_ROWS
     chunk = slot // parts
     return pl.pallas_call(
         functools.partial(attend_back_kernel, parts, chunk),
@@ -246,7 +232,7 @@
         in_specs=[
             pl.BlockSpec((block, LANES), lambda h, r: (r, h)),
             pl.BlockSpec((block, LANES), lambda h, r: (r, h)),
-            pl.BlockSpec((count, height, LANES), lambda h, r: (0, 0, h)),
+            pl.BlockSpec((slot, LANES), lambda h, r: (0, h)),
             pl.BlockSpec((1, 1, block, slot), lambda h, r: (h, r, 0, 0)),
         ],
         out_specs=[
@@ -265,7 +251,6 @@
         ],
         scratch_shapes=[
             pltpu.VMEM((block, slot), jnp.float32),
-            pltpu.VMEM((slot, LANES), jnp.bfloat16),
             pltpu.VMEM((LANES, slot), jnp.float32),
             pltpu.VMEM((8, slot), jnp.float32),
         ],
@@ -495,7 +480,7 @@
         ]
     else:
         parts_in = list(lax.all_gather(own_in, "dp", axis=0, tiled=False))
-    tokens_group = lax.all_gather(tokens[0], "sp", axis=0, tiled=True)
+    tokens_slot = lax.all_gather(tokens[0], ("sp", "ctx"), axis=0, tiled=True)
     all_in = jnp.concatenate([part[:weight_rows] for part in parts_in])
     gain_one = jnp.concatenate([part[weight_rows, :weight_rows] for part in parts_in]).astype(f32)
     gain_two = jnp.concatenate([part[weight_rows + 1, :weight_rows] for part in parts_in]).astype(f32)
@@ -513,35 +498,34 @@
     fc_came = dp_send(fc_own)
     proj_came = dp_send(proj_own)
 
+    cot_group = lax.all_gather(cotangent[0], "sp", axis=0, tiled=True)
+    kept = jnp.transpose(kept_keys[0], (2, 0, 1, 3))
+    tokens_slot, cot_group, out_came, fc_came, kept = lax.optimization_barrier(
+        (tokens_slot, cot_group, out_came, fc_came, kept)
+    )
+
+    def group_of(values):
+        parts = values.reshape((seg_count, ctx_count, rows) + values.shape[1:])
+        return lax.dynamic_index_in_dim(parts, ctx_at, 1, keepdims=False).reshape((group_rows,) + values.shape[1:])
+
     inputs = tokens[0].astype(f32)
-    inputs_group = tokens_group.astype(f32)
-    norm_one = layer_norm(inputs_group, gain_one).astype(bf16)
-    qkv_rows = jnp.dot(norm_one, all_in, preferred_element_type=f32).astype(bf16)
-    score_weight_part = all_in[:, head_cols : head_cols + heads]
-    key_score = lax.dot_general(
-        score_weight_part, norm_one, (((0,), (1,)), ((), ())), preferred_element_type=f32
+    inputs_group = group_of(tokens_slot).astype(f32)
+    norm_slot = layer_norm(tokens_slot.astype(f32), gain_one).astype(bf16)
+    pairs = jnp.dot(norm_slot, all_in[:, :keys], preferred_element_type=f32).astype(bf16)
+    score_slot = lax.dot_general(
+        all_in[:, head_cols : head_cols + heads], norm_slot, (((0,), (1,)), ((), ())), preferred_element_type=f32
     ).astype(bf16)
-    score_rows = jnp.transpose(key_score.reshape(heads, seg_count, rows), (1, 0, 2)).reshape(
-        seg_count, heads * rows
-    )
-    pairs_own = jnp.concatenate(
-        [qkv_rows[:, :keys], jnp.pad(score_rows, ((0, PAD_ROWS - seg_count), (0, 0)))], axis=0
-    )
-    query_wide = jnp.pad(
-        qkv_rows[:, keys:head_cols].reshape(group_rows, heads, HD), ((0, 0), (0, 0), (0, HD))
-    ).reshape(group_rows, heads * LANES)
-    kept = jnp.transpose(kept_keys[0], (2, 0, 1, 3))
+    key_score = lax.dynamic_index_in_dim(
+        score_slot.reshape(heads, seg_count, ctx_count, rows), ctx_at, 2, keepdims=False
+    ).reshape(heads, group_rows)
+    norm_one = group_of(norm_slot)
+    query_weight = jnp.pad(
+        all_in[:, keys:head_cols].reshape(width, heads, HD), ((0, 0), (0, 0), (0, HD))
+    ).reshape(width, heads * LANES)
+    query_wide = jnp.dot(norm_one, query_weight, preferred_element_type=f32).astype(bf16)
     base = (ctx_at * rows).astype(jnp.int32)[None]
-    cot_own, pairs_own = lax.optimization_barrier((cotangent[0], pairs_own))
-    cot_group = lax.all_gather(cot_own, "sp", axis=0, tiled=True)
-    pairs = lax.all_gather(pairs_own, "ctx", axis=0, tiled=False)
-    norm_own = lax.dynamic_slice_in_dim(norm_one, sp_at * rows, rows, 0)
-    query_wide, cot_group, out_came, fc_came, proj_came, norm_own, pairs = lax.optimization_barrier(
-        (query_wide, cot_group, out_came, fc_came, proj_came, norm_own, pairs)
-    )
-    norm_slot = lax.all_gather(norm_own, ("sp", "ctx"), axis=0, tiled=True)
-    head_outs, prob = attend(base, kept, query_wide, pairs)
-    head_outs, norm_slot = lax.optimization_barrier((head_outs, norm_slot))
+    head_outs, prob = attend(base, kept, query_wide, pairs, score_slot[:, None])
+    head_outs, proj_came = lax.optimization_barrier((head_outs, proj_came))
     attended = head_outs.reshape(heads * HD, group_rows)
     attended_all = lax.all_gather(attended, "sp", axis=0, tiled=True)
     out_full = dp_join(out_own, out_came)
@@ -566,7 +550,10 @@
     fc_parts = contract_rows(norm_two, grad_pre).astype(bf16).reshape(dp_count, ctx_count, piece, width)
     proj_parts = contract_rows(active, grad_out_group).astype(bf16).reshape(dp_count, ctx_count, -1, width)
     grad_pre, fc_parts, proj_parts = lax.optimization_barrier((grad_pre, fc_parts, proj_parts))
-    mlp_dp = dp_scatter(jnp.concatenate([fc_parts, proj_parts], axis=2))
+    fc_came = lax.all_to_all(
+        jnp.transpose(fc_parts, (1, 0, 2, 3)), "ctx", split_axis=0, concat_axis=0, tiled=True
+    )
+    proj_dp = dp_scatter(proj_parts)
     grad_norm_parts = contract_cols(grad_pre, fc_part).astype(bf16)
     grad_norm_two = exchange_sum(grad_norm_parts.reshape(seg_count, rows, width), "sp")
     _, second_pull = jax.vjp(layer_norm, mixed, gain_two)
@@ -578,24 +565,24 @@
     out_wide = jnp.pad(out_part.reshape(heads, HD, width), ((0, 0), (HD, 0), (0, 0))).reshape(heads * LANES, width)
     grad_wide = contract_cols(grad_branch, out_wide).astype(bf16)
     out_mine = jnp.dot(attended, grad_branch, preferred_element_type=f32).astype(bf16)
-    grad_wide, mlp_dp, out_mine = lax.optimization_barrier((grad_wide, mlp_dp, out_mine))
+    grad_wide, fc_came, proj_dp, out_mine = lax.optimization_barrier((grad_wide, fc_came, proj_dp, out_mine))
     out_sum = dp_sum(out_mine)
-    mlp_came = lax.all_to_all(mlp_dp, "ctx", split_axis=0, concat_axis=0, tiled=True)
-    score_slot = jnp.transpose(
-        pairs[:, group_rows : group_rows + seg_count].reshape(ctx_count, seg_count, heads, rows), (2, 1, 0, 3)
-    ).reshape(heads, -1)
+    fc_own = dp_scatter(jnp.sum(fc_came.astype(f32), axis=0).astype(bf16))
+    proj_came = lax.all_to_all(proj_dp, "ctx", split_axis=0, concat_axis=0, tiled=True)
     gain_cols = jnp.stack([gain_one, second_gain_grad], axis=1)
-    grad_wide, score_slot, gain_cols = lax.optimization_barrier((grad_wide, score_slot, gain_cols))
-    query_grads, pair_grads, turned, query_turned, gates = attend_back(query_wide, grad_wide, pairs, prob)
+    grad_wide, gain_cols = lax.optimization_barrier((grad_wide, gain_cols))
+    query_grads, pair_grads, turned, query_turned, gates = attend_back(
+        ctx_count, query_wide, grad_wide, pairs, prob
+    )
     pair_mine = lax.psum_scatter(pair_grads, "ctx", scatter_dimension=0, tiled=False)
     small = weight_grad(turned, query_turned, gates, score_slot, norm_slot, norm_one, all_in, gain_cols)
-    small, mlp_came, out_sum = lax.optimization_barrier((small, mlp_came, out_sum))
+    small, fc_own, proj_came, out_sum = lax.optimization_barrier((small, fc_own, proj_came, out_sum))
     late = jnp.concatenate(
         [dp_scatter(small.reshape(dp_count, ctx_count, piece, width)), out_sum.reshape(ctx_count, -1, width)], axis=1
     )
     late_sum = exchange_sum(late, "ctx").astype(bf16)
-    mlp_sum = jnp.sum(mlp_came.astype(f32), axis=0).astype(bf16)
-    gradients = jnp.concatenate([late_sum[:piece], mlp_sum, late_sum[piece:]], axis=0)
+    proj_sum = jnp.sum(proj_came.astype(f32), axis=0).astype(bf16)
+    gradients = jnp.concatenate([late_sum[:piece], fc_own, proj_sum, late_sum[piece:]], axis=0)
     pair_mine, gradients, active_late = lax.optimization_barrier((pair_mine, gradients, active))
     gathered = lax.all_gather(gradients, ("sp", "ctx"), axis=0, tiled=False).reshape(seg_count, ctx_count, -1, width)
     proj_piece = hidden // (seg_count * dp_count * ctx_count)

time: 370 us -> 338 us (0.914)
  Pallas kernels: 83.4 us -> 54.3 us
  waiting for transfers between devices: 140 us -> 130 us
  starting transfers between devices: 27.7 us -> 37.4 us
  blocking collectives: 33.5 us -> 26.4 us
    pallas_call x1, Pallas kernels: 48.8 us -> 19.5 us  [attend(): pl.pallas_call(functools.partial(attend_kernel, parts, chunk), grid_spec=...]
    all_to_all x1 -> x2, waiting for transfers between devices: 3.71 us -> 12.4 us  [the longest x1 12.4 us: per_device(): lax.all_to_all(jnp.transpose(fc_parts, (1, 0, 2, 3)), 'ctx', split_axis=0...]
    all_to_all x4, waiting for transfers between devices: 57.5 us -> 49.2 us  [exchange_sum(): came = lax.all_to_all(parts, axis, split_axis=0, concat_axis=0, tiled=True)]
    all_gather x2 -> x1, blocking collectives: 17.2 us -> 9.75 us  [per_device(): cot_group = lax.all_gather(cotangent[0], 'sp', axis=0, tiled=True)]
    ppermute x3, waiting for transfers between devices: 28.6 us -> 22 us  [dp_send(): return lax.ppermute(mine, 'dp', [(0, 1), (1, 0)])]
    ppermute x2 -> x3, waiting for transfers between devices: 19 us -> 14.4 us  [dp_scatter(): other = lax.ppermute(sent, 'dp', [(0, 1), (1, 0)])]
    all_to_all x1 -> x2, starting transfers between devices: 4.87 us -> 9.08 us  [the longest x1 4.94 us: per_device(): lax.all_to_all(jnp.transpose(fc_parts, (1, 0, 2, 3)), 'ctx', split_axis=0...]
    dot_general x2 -> x3, matrix products: 1.34 us -> 5.5 us  [the longest x1 2.98 us: per_device(): jnp.dot(norm_slot, all_in[:, :keys], preferred_element_type=f32)]
  transfers between devices with their start and end apart: 16 -> 17, of which waited for: 12 -> 11; matrix products, arithmetic and copies ran while one was open for 10% -> 15% of each run, Pallas kernels for 20% -> 14%
where the time goes in v2:
time: 338 us; the launch traced here: 337 us
  waiting for transfers between devices  130 us (38%)
  Pallas kernels  54.3 us (16%)
  starting transfers between devices  37.4 us (11%)
  other arithmetic  27.8 us (8%)
  blocking collectives  26.4 us (8%)
  matrix products  24 us (7%)
  local copies, waits for them, and re-layouts  21.5 us (6%)
  between operations  15.1 us (4%)
    all_to_all x4, waiting for transfers between devices, exchange_sum(): came = lax.all_to_all(parts, axis, split_axis=0, concat_axis=0, tiled=True)  49.2 us
    all_gather x1, waiting for transfers between devices, per_device(): lax.all_gather(gradients, ('sp', 'ctx'), axis=0, tiled=False)  31.4 us
    ppermute x3, waiting for transfers between devices, dp_send(): return lax.ppermute(mine, 'dp', [(0, 1), (1, 0)])  22 us
    pallas_call x1, Pallas kernels, attend(): pl.pallas_call(functools.partial(attend_kernel, parts, chunk), grid_spec=...  19.5 us
    all_to_all x4, starting transfers between devices, exchange_sum(): came = lax.all_to_all(parts, axis, split_axis=0, concat_axis=0, tiled=True)  16.2 us
    ppermute x3, waiting for transfers between devices, dp_scatter(): other = lax.ppermute(sent, 'dp', [(0, 1), (1, 0)])  14.4 us
    pallas_call x1, Pallas kernels, attend_back(): pl.pallas_call(functools.partial(attend_back_kernel, parts, chunk), grid=...  14.4 us
    all_to_all x1, waiting for transfers between devices, per_device(): lax.all_to_all(jnp.transpose(fc_parts, (1, 0, 2, 3)), 'ctx', split_axis=0...  12.4 us
  transfers between devices with their start and end apart: 17, of which 11 were waited for; matrix products, arithmetic and copies ran while one was open for 15% of the time, Pallas kernels for 14%

profile of v2, /device:TPU:0, one launch (start us, length us, event | category | flops | bytes accessed | tf_op | source)
XLA Modules:
  0.0 336.8 jit_solution(865612076813680096)
XLA Ops:
  14.5 3.0 collective-permute-start
  19.3 2.2 pad_maximum_fusion.2
  21.6 9.7 %all-gather.1 = bf16[1,512,768]{2,1,0:T(8,128)(2,1)} all-gather(bf16[1,128,768]{2,1,0:T(8,128)(2,1)S(1)} %copy-done.11), channel_id=3, replica_groups=mesh['dp'=2,'sp'=4,'ctx'=4] {'sp'}, dimensions={1}, use_global_device_ids=true | all-gather | bytes 983040 | tf_op jit(solution)/shard_map/all_gather | solution.py:501
  39.5 9.4 %collective-permute-done.1 = bf16[384,768]{1,0:T(8,128)(2,1)} collective-permute-done((bf16[384,768]{1,0:T(8,128)(2,1)S(1)}, bf16[384,768]{1,0:T(8,128)(2,1)}, u32[]{:S(2)}, u32[]{:S(2)}) %collective-permute-start.1) | collective-permute-done | bytes 589856 | tf_op jit(solution)/shard_map/ppermute | solution.py:395
  48.9 12.6 %collective-permute-done.2 = bf16[384,768]{1,0:T(8,128)(2,1)} collective-permute-done((bf16[384,768]{1,0:T(8,128)(2,1)}, bf16[384,768]{1,0:T(8,128)(2,1)}, u32[]{:S(2)}, u32[]{:S(2)}) %collective-permute-start.2) | collective-permute-done | bytes 589856 | tf_op jit(solution)/shard_map/ppermute | solution.py:395
  61.5 2.5 convert_reduce_fusion
  70.8 3.0 convolution_convert_fusion.refs_2_
  73.8 19.5 %attend.1 = (bf16[3,64,512]{2,1,0:T(8,128)(2,1)}, bf16[3,4,128,2048]{3,2,1,0:T(8,128)(2,1)}) custom-call(s32[1]{0:T(128)} %bitcast.7.base_ref, s32[3,4,128,64]{3,2,1,0:T(8,128)} %bitcast.121, bf16[512,384]{1,0:T(8,128)(2,1)} %convolution_convert_fusion.7.refs_1_.refs_0_, bf16[2048,384]{1,0:T(8,128)(2,1)} %convolution_convert_fusion.refs_2_, ...), custom_call_target="tpu_custom_call" | custom-call | tf_op jit(solution)/shard_map/attend/pallas_call | solution.py:158
  93.3 7.8 %all_gather.20 = bf16[768,512]{1,0:T(8,128)(2,1)S(1)} all-gather(bf16[192,512]{1,0:T(8,128)(2,1)} %bitcast.136), channel_id=1, replica_groups=mesh['dp'=2,'sp'=4,'ctx'=4] {'sp'}, dimensions={0}, use_global_device_ids=true | all-gather | bytes 983040 | tf_op jit(solution)/shard_map/all_gather | solution.py:530
  104.3 2.9 multiply_convert_fusion
  107.3 3.2 fusion.11
  113.4 3.8 %convolution_convert_fusion.5 = bf16[512,768]{1,0:T(8,128)(2,1)} fusion(bf16[512,768]{1,0:T(8,128)(2,1)S(1)} %fusion.11, bf16[384,768]{1,0:T(8,128)(2,1)} %collective-permute-done.2, bf16[384,768]{1,0:T(8,128)(2,1)} %get-tuple-element.48, pred[]{:T(512)S(6)} %eq.5), kind=kOutput, calls=%fused_computation.28 | convolution fusion | flops 609681408 | bytes 2752513 | tf_op jit(solution)/shard_map/dot_general | solution.py:38
  117.2 3.5 %all-to-all-start = ((bf16[4,128,768]{2,1,0:T(8,128)(2,1)}), bf16[4,128,768]{2,1,0:T(8,128)(2,1)S(1)}, u32[]{:S(2)}, u32[]{:S(2)}) async-start(bf16[4,128,768]{2,1,0:T(8,128)(2,1)} %bitcast.132), calls=%async_computation | async-start | bytes 1572864 | tf_op jit(solution)/shard_map/all_to_all | solution.py:434
  126.5 5.7 %all-to-all-done = bf16[4,128,768]{2,1,0:T(8,128)(2,1)S(1)} async-done(((bf16[4,128,768]{2,1,0:T(8,128)(2,1)}), bf16[4,128,768]{2,1,0:T(8,128)(2,1)S(1)}, u32[]{:S(2)}, u32[]{:S(2)}) %all-to-all-start) | async-done | bytes 786464 | tf_op jit(solution)/shard_map/all_to_all | solution.py:434
  132.3 4.9 %all-to-all-start.1 = ((bf16[4,2,96,768]{3,2,1,0:T(8,128)(2,1)}), bf16[4,2,96,768]{3,2,1,0:T(8,128)(2,1)S(1)}, u32[]{:S(2)}, u32[]{:S(2)}) async-start(bf16[4,2,96,768]{3,2,1,0:T(8,128)(2,1)} %bitcast.116), calls=%async_computation.1 | async-start | bytes 2359296 | tf_op jit(solution)/shard_map/all_to_all | solution.py:553
  138.3 2.2 collective-permute-done.4
  142.5 8.9 %all_gather.21 = bf16[512,768]{1,0:T(8,128)(2,1)S(1)} all-gather(bf16[128,768]{1,0:T(8,128)(2,1)S(1)} %fusion.23), channel_id=1, replica_groups=mesh['dp'=2,'sp'=4,'ctx'=4] {'sp'}, dimensions={0}, use_global_device_ids=true | all-gather | bytes 983040 | tf_op jit(solution)/shard_map/all_gather | solution.py:563
  153.1 12.4 %all-to-all-done.1 = bf16[4,2,96,768]{3,2,1,0:T(8,128)(2,1)S(1)} async-done(((bf16[4,2,96,768]{3,2,1,0:T(8,128)(2,1)}), bf16[4,2,96,768]{3,2,1,0:T(8,128)(2,1)S(1)}, u32[]{:S(2)}, u32[]{:S(2)}) %all-to-all-start.1) | async-done | bytes 1179680 | tf_op jit(solution)/shard_map/all_to_all | solution.py:553
  165.5 4.1 %all-to-all-start.2 = ((bf16[4,96,768]{2,1,0:T(8,128)(2,1)}), bf16[4,96,768]{2,1,0:T(8,128)(2,1)}, u32[]{:S(2)}, u32[]{:S(2)}) async-start(bf16[4,96,768]{2,1,0:T(8,128)(2,1)} %fusion.13), calls=%async_computation.3 | async-start | bytes 1179648 | tf_op jit(solution)/shard_map/all_to_all | solution.py:571
  170.0 14.4 %attend_back.1 = (bf16[512,384]{1,0:T(8,128)(2,1)}, bf16[4,528,384]{2,1,0:T(8,128)(2,1)}, bf16[3,128,2048]{2,1,0:T(8,128)(2,1)}, bf16[3,64,512]{2,1,0:T(8,128)(2,1)}, f32[3,8,2048]{2,1,0:T(8,128)}) custom-call(bf16[512,384]{1,0:T(8,128)(2,1)} %convolution_convert_fusion.7.refs_1_.refs_0_, bf16[512,384]{1,0:T(8,128)(2,1)} %convolution_convert_fusion.6.refs_1_, ...), custom_call_target="tpu_custom_call" | custom-call | tf_op jit(solution)/shard_map/attend_back/pallas_call | solution.py:229
  189.9 6.7 %weight_grad.1 = bf16[768,768]{1,0:T(8,128)(2,1)} custom-call(bf16[3,128,2048]{2,1,0:T(8,128)(2,1)} %get-tuple-element.66.turned_ref, bf16[3,64,512]{2,1,0:T(8,128)(2,1)} %get-tuple-element.67.dq_ref, f32[3,8,2048]{2,1,0:T(8,128)} %get-tuple-element.68.gates_ref, bf16[3,2048]{1,0:T(4,128)(2,1)} %copy-done.27, bf16[2048,768]{1,0:T(8,128)(2,1)} %copy-done.3, ...), custom_call_target="tpu_custom_call" | custom-call | tf_op jit(solution)/shard_map/weight_grad/pallas_call | solution.py:286
  201.8 12.2 %collective-permute-done.7 = bf16[4,96,768]{2,1,0:T(8,128)(2,1)S(1)} collective-permute-done((bf16[4,96,768]{2,1,0:T(8,128)(2,1)S(1)}, bf16[4,96,768]{2,1,0:T(8,128)(2,1)S(1)}, u32[]{:S(2)}, u32[]{:S(2)}) %collective-permute-start.7) | collective-permute-done | bytes 589856 | tf_op jit(solution)/shard_map/ppermute | solution.py:412
  215.1 4.3 %all-to-all-start.3 = ((bf16[4,144,768]{2,1,0:T(8,128)(2,1)}), bf16[4,144,768]{2,1,0:T(8,128)(2,1)S(1)}, u32[]{:S(2)}, u32[]{:S(2)}) async-start(bf16[4,144,768]{2,1,0:T(8,128)(2,1)} %pad_maximum_fusion.1), calls=%async_computation.4 | async-start | bytes 1769472 | tf_op jit(solution)/shard_map/all_to_all | solution.py:434
  220.6 18.5 %all-to-all-done.3 = bf16[4,144,768]{2,1,0:T(8,128)(2,1)S(1)} async-done(((bf16[4,144,768]{2,1,0:T(8,128)(2,1)}), bf16[4,144,768]{2,1,0:T(8,128)(2,1)S(1)}, u32[]{:S(2)}, u32[]{:S(2)}) %all-to-all-start.3) | async-done | bytes 884768 | tf_op jit(solution)/shard_map/all_to_all | solution.py:434
  240.8 3.3 finish.1
  244.2 4.2 %all-to-all-start.5 = ((bf16[4,128,768]{2,1,0:T(8,128)(2,1)}), bf16[4,128,768]{2,1,0:T(8,128)(2,1)}, u32[]{:S(2)}, u32[]{:S(2)}) async-start(bf16[4,128,768]{2,1,0:T(8,128)(2,1)} %bitcast.122), calls=%async_computation.6 | async-start | bytes 1572864 | tf_op jit(solution)/shard_map/all_to_all | solution.py:434
  248.6 3.2 convolution_convert_fusion.4
  251.8 12.3 %all-to-all-done.5 = bf16[4,128,768]{2,1,0:T(8,128)(2,1)} async-done(((bf16[4,128,768]{2,1,0:T(8,128)(2,1)}), bf16[4,128,768]{2,1,0:T(8,128)(2,1)}, u32[]{:S(2)}, u32[]{:S(2)}) %all-to-all-start.5) | async-done | bytes 786464 | tf_op jit(solution)/shard_map/all_to_all | solution.py:434
  264.1 4.2 %all-to-all-start.4 = ((bf16[4,128,768]{2,1,0:T(8,128)(2,1)}), bf16[4,128,768]{2,1,0:T(8,128)(2,1)}, u32[]{:S(2)}, u32[]{:S(2)}) async-start(bf16[4,128,768]{2,1,0:T(8,128)(2,1)} %bitcast.131), calls=%async_computation.5 | async-start | bytes 1572864 | tf_op jit(solution)/shard_map/all_to_all | solution.py:434
  270.1 12.7 %all-to-all-done.4 = bf16[4,128,768]{2,1,0:T(8,128)(2,1)} async-done(((bf16[4,128,768]{2,1,0:T(8,128)(2,1)}), bf16[4,128,768]{2,1,0:T(8,128)(2,1)}, u32[]{:S(2)}, u32[]{:S(2)}) %all-to-all-start.4) | async-done | bytes 786464 | tf_op jit(solution)/shard_map/all_to_all | solution.py:434
  285.1 31.4 %all-gather.8.cloned.1.call-done = bf16[5376,768]{1,0:T(8,128)(2,1)} async-done(((bf16[336,768]{1,0:T(8,128)(2,1)}), bf16[5376,768]{1,0:T(8,128)(2,1)}) %all-gather.8.cloned.1.call-update) | async-done | bytes 8257552 | tf_op jit(solution)/shard_map/all_gather | solution.py:587
  317.8 8.3 %unpack.1 = (f32[384,2304]{1,0:T(8,128)}, f32[384,12]{1,0:T(8,128)}, f32[384,3072]{1,0:T(8,128)}, f32[4,4,96,768]{3,2,1,0:T(8,128)}) custom-call(bf16[4,4,336,768]{3,2,1,0:T(8,128)(2,1)} %bitcast.114), custom_call_target="tpu_custom_call" | custom-call | tf_op jit(solution)/shard_map/unpack/pallas_call | solution.py:349
  (188 shorter events, 64.4 us)
Async XLA Ops:
  7.2 54.3 %all-gather.6.cloned.1.call-start = ((), (), s32[]{:S(2)}) async-start(), calls=%async_computation.8 | async-start | bytes 3342336 | tf_op jit(solution)/shard_map/all_gather | solution.py:483
  14.5 16.8 %collective-permute-start = (bf16[400,640]{1,0:T(8,128)(2,1)}, bf16[400,640]{1,0:T(8,128)(2,1)S(1)}, u32[]{:S(2)}, u32[]{:S(2)}) collective-permute-start(bf16[400,640]{1,0:T(8,128)(2,1)} %arrange.1), channel_id=1, source_target_pairs={{0,16},{16,0},{1,17},{17,1},{2,18},{18,2},{3,19},{19,3},{4,20},{20... | collective-permute-start | bytes 1536008 | tf_op jit(solution)/shard_map/ppermute | solution.py:477
  19.3 12.0 %copy-start.9 = (bf16[400,640]{1,0:T(8,128)(2,1)S(1)}, bf16[400,640]{1,0:T(8,128)(2,1)}, u32[]{:S(2)}) copy-start(bf16[400,640]{1,0:T(8,128)(2,1)} %arrange.1) | copy-start | bytes 1536004
  32.6 16.3 %collective-permute-start.1 = (bf16[384,768]{1,0:T(8,128)(2,1)S(1)}, bf16[384,768]{1,0:T(8,128)(2,1)}, u32[]{:S(2)}, u32[]{:S(2)}) collective-permute-start(bf16[384,768]{1,0:T(8,128)(2,1)S(1)} %copy-done.20), channel_id=1, source_target_pairs={{0,16},{16,0},{1,17},{17,1},{2,18},{18,2},{3,19},{19,3},{4,20},{20... | collective-permute-start | bytes 1769480 | tf_op jit(solution)/shard_map/ppermute | solution.py:395
  34.0 27.5 %collective-permute-start.2 = (bf16[384,768]{1,0:T(8,128)(2,1)}, bf16[384,768]{1,0:T(8,128)(2,1)}, u32[]{:S(2)}, u32[]{:S(2)}) collective-permute-start(bf16[384,768]{1,0:T(8,128)(2,1)} %get-tuple-element.48), channel_id=1, source_target_pairs={{0,16},{16,0},{1,17},{17,1},{2,18},{18,2},{3,19},{19,3},{4,20},{20... | collective-permute-start | bytes 1769480 | tf_op jit(solution)/shard_map/ppermute | solution.py:395
  36.5 56.8 %collective-permute-start.3 = (bf16[384,768]{1,0:T(8,128)(2,1)}, bf16[384,768]{1,0:T(8,128)(2,1)}, u32[]{:S(2)}, u32[]{:S(2)}) collective-permute-start(bf16[384,768]{1,0:T(8,128)(2,1)} %get-tuple-element.53), channel_id=1, source_target_pairs={{0,16},{16,0},{1,17},{17,1},{2,18},{18,2},{3,19},{19,3},{4,20},{20... | collective-permute-start | bytes 1769480 | tf_op jit(solution)/shard_map/ppermute | solution.py:395
  39.4 26.0 %copy-start.30 = (f32[768]{0:T(1024)}, f32[768]{0:T(1024)S(1)}, u32[]{:S(2)}) copy-start(f32[768]{0:T(1024)S(1)} %maximum_convert_fusion.1) | copy-start | bytes 9220
  39.5 71.0 %copy-start.32 = (f32[768]{0:T(1024)}, f32[768]{0:T(1024)S(1)}, u32[]{:S(2)}) copy-start(f32[768]{0:T(1024)S(1)} %maximum_convert_fusion.2) | copy-start | bytes 9220
  113.4 7.3 %copy-start.16 = (bf16[768,768]{1,0:T(8,128)(2,1)}, bf16[768,768]{1,0:T(8,128)(2,1)S(1)}, u32[]{:S(2)}) copy-start(bf16[768,768]{1,0:T(8,128)(2,1)S(1)} %convolution_convert_fusion.2) | copy-start | bytes 3538948
  117.2 15.1 %all-to-all-start = ((bf16[4,128,768]{2,1,0:T(8,128)(2,1)}), bf16[4,128,768]{2,1,0:T(8,128)(2,1)S(1)}, u32[]{:S(2)}, u32[]{:S(2)}) async-start(bf16[4,128,768]{2,1,0:T(8,128)(2,1)} %bitcast.132), calls=%async_computation | async-start | bytes 1572864 | tf_op jit(solution)/shard_map/all_to_all | solution.py:434
  124.5 16.0 %collective-permute-start.4 = (bf16[4,96,768]{2,1,0:T(8,128)(2,1)}, bf16[4,96,768]{2,1,0:T(8,128)(2,1)}, u32[]{:S(2)}, u32[]{:S(2)}) collective-permute-start(bf16[4,96,768]{2,1,0:T(8,128)(2,1)} %dynamic-slice_bitcast_fusion.1), channel_id=1, source_target_pairs={{0,16},{16,0},{1,17},{17,1},{2,18},{18,2},{3,19},{19,3},{4,20},{20... | collective-permute-start | bytes 1769480 | tf_op jit(solution)/shard_map/ppermute | solution.py:412
  132.3 33.3 %all-to-all-start.1 = ((bf16[4,2,96,768]{3,2,1,0:T(8,128)(2,1)}), bf16[4,2,96,768]{3,2,1,0:T(8,128)(2,1)S(1)}, u32[]{:S(2)}, u32[]{:S(2)}) async-start(bf16[4,2,96,768]{3,2,1,0:T(8,128)(2,1)} %bitcast.116), calls=%async_computation.1 | async-start | bytes 2359296 | tf_op jit(solution)/shard_map/all_to_all | solution.py:553
  138.3 13.1 %copy-start.19 = (bf16[3,64,512]{2,1,0:T(8,128)(2,1)S(1)}, bf16[3,64,512]{2,1,0:T(8,128)(2,1)}, u32[]{:S(2)}) copy-start(bf16[3,64,512]{2,1,0:T(8,128)(2,1)} %get-tuple-element.54) | copy-start | bytes 589828
  142.5 9.2 %copy-start.23 = (bf16[3,128,768]{2,1,0:T(8,128)(2,1)S(1)}, bf16[3,128,768]{2,1,0:T(8,128)(2,1)}, u32[]{:S(2)}) copy-start(bf16[3,128,768]{2,1,0:T(8,128)(2,1)} %pad.14) | copy-start | bytes 1769476
  151.7 18.2 %copy-start.34 = (bf16[384,1]{0,1:T(2,128)(2,1)S(1)}, bf16[384,1]{0,1:T(2,128)(2,1)}, u32[]{:S(2)}) copy-start(bf16[384,1]{0,1:T(2,128)(2,1)} %get-tuple-element.129) | copy-start | bytes 2308
  151.7 18.2 %copy-start.35 = (bf16[384,1]{0,1:T(2,128)(2,1)S(1)}, bf16[384,1]{0,1:T(2,128)(2,1)}, u32[]{:S(2)}) copy-start(bf16[384,1]{0,1:T(2,128)(2,1)} %get-tuple-element.138) | copy-start | bytes 2308
  165.5 34.7 %all-to-all-start.2 = ((bf16[4,96,768]{2,1,0:T(8,128)(2,1)}), bf16[4,96,768]{2,1,0:T(8,128)(2,1)}, u32[]{:S(2)}, u32[]{:S(2)}) async-start(bf16[4,96,768]{2,1,0:T(8,128)(2,1)} %fusion.13), calls=%async_computation.3 | async-start | bytes 1179648 | tf_op jit(solution)/shard_map/all_to_all | solution.py:571
  169.7 70.4 %reduce-scatter.2.cloned.1.call-start = ((), (), s32[]{:S(2)}) async-start(), calls=%async_computation.7 | async-start | bytes 2027520 | tf_op jit(solution)/shard_map/reduce_scatter | solution.py:577
  187.0 9.6 %collective-permute-start.5 = (bf16[96,768]{1,0:T(8,128)(2,1)}, bf16[96,768]{1,0:T(8,128)(2,1)}, u32[]{:S(2)}, u32[]{:S(2)}) collective-permute-start(bf16[96,768]{1,0:T(8,128)(2,1)} %dynamic-slice_bitcast_fusion.2), channel_id=1, source_target_pairs={{0,16},{16,0},{1,17},{17,1},{2,18},{18,2},{3,19},{19,3},{4,20},{20... | collective-permute-start | bytes 442376 | tf_op jit(solution)/shard_map/ppermute | solution.py:412
  188.4 10.1 %collective-permute-start.6 = (bf16[192,768]{1,0:T(8,128)(2,1)S(1)}, bf16[192,768]{1,0:T(8,128)(2,1)}, u32[]{:S(2)}, u32[]{:S(2)}) collective-permute-start(bf16[192,768]{1,0:T(8,128)(2,1)S(1)} %convolution_convert_fusion.8), channel_id=1, source_target_pairs={{0,16},{16,0},{1,17},{17,1},{2,18},{18,2},{3,19},{19,3},{4,20},{20... | collective-permute-start | bytes 884744 | tf_op jit(solution)/shard_map/ppermute | solution.py:429
  200.2 13.9 %copy-start.14 = (bf16[192,768]{1,0:T(8,128)(2,1)S(1)}, bf16[192,768]{1,0:T(8,128)(2,1)}, u32[]{:S(2)}) copy-start(bf16[192,768]{1,0:T(8,128)(2,1)} %add_convert_fusion) | copy-start | bytes 884740
  200.3 13.7 %collective-permute-start.7 = (bf16[4,96,768]{2,1,0:T(8,128)(2,1)S(1)}, bf16[4,96,768]{2,1,0:T(8,128)(2,1)S(1)}, u32[]{:S(2)}, u32[]{:S(2)}) collective-permute-start(bf16[4,96,768]{2,1,0:T(8,128)(2,1)S(1)} %dynamic-slice_bitcast_fusion), channel_id=1, source_target_pairs={{0,16},{16,0},{1,17},{17,1},{2,18},{18,2},{3,19},{19,3},{4,20},{20... | collective-permute-start | bytes 1769480 | tf_op jit(solution)/shard_map/ppermute | solution.py:412
  215.1 24.0 %all-to-all-start.3 = ((bf16[4,144,768]{2,1,0:T(8,128)(2,1)}), bf16[4,144,768]{2,1,0:T(8,128)(2,1)S(1)}, u32[]{:S(2)}, u32[]{:S(2)}) async-start(bf16[4,144,768]{2,1,0:T(8,128)(2,1)} %pad_maximum_fusion.1), calls=%async_computation.4 | async-start | bytes 1769472 | tf_op jit(solution)/shard_map/all_to_all | solution.py:434
  219.4 19.9 %copy-start.25 = (bf16[96,768]{1,0:T(8,128)(2,1)S(1)}, bf16[96,768]{1,0:T(8,128)(2,1)}, u32[]{:S(2)}) copy-start(bf16[96,768]{1,0:T(8,128)(2,1)} %fusion.22) | copy-start | bytes 442372
  219.4 97.1 %all-gather.8.cloned.1.call-start = ((), (), s32[]{:S(2)}) async-start(), calls=%async_computation.9 | async-start | bytes 8773632 | tf_op jit(solution)/shard_map/all_gather | solution.py:587
  220.6 19.5 %copy-start.28 = (bf16[3,2048]{1,0:T(4,128)(2,1)S(1)}, bf16[3,2048]{1,0:T(4,128)(2,1)}, u32[]{:S(2)}) copy-start(bf16[3,2048]{1,0:T(4,128)(2,1)} %copy-done.27) | copy-start | bytes 36868
  240.8 7.6 %copy-start.6 = (bf16[1,128,768]{2,1,0:T(8,128)(2,1)S(1)}, bf16[1,128,768]{2,1,0:T(8,128)(2,1)}, u32[]{:S(2)}) copy-start(bf16[1,128,768]{2,1,0:T(8,128)(2,1)} %param.11) | copy-start | bytes 589828
  240.8 7.7 %copy-start.22 = (bf16[384,768]{1,0:T(8,128)(2,1)S(1)}, bf16[384,768]{1,0:T(8,128)(2,1)}, u32[]{:S(2)}) copy-start(bf16[384,768]{1,0:T(8,128)(2,1)} %get-tuple-element.53) | copy-start | bytes 1769476
  244.2 19.9 %all-to-all-start.5 = ((bf16[4,128,768]{2,1,0:T(8,128)(2,1)}), bf16[4,128,768]{2,1,0:T(8,128)(2,1)}, u32[]{:S(2)}, u32[]{:S(2)}) async-start(bf16[4,128,768]{2,1,0:T(8,128)(2,1)} %bitcast.122), calls=%async_computation.6 | async-start | bytes 1572864 | tf_op jit(solution)/shard_map/all_to_all | solution.py:434
  251.8 17.9 %copy-start.31 = (f32[768]{0:T(1024)S(1)}, f32[768]{0:T(1024)}, u32[]{:S(2)}) copy-start(f32[768]{0:T(1024)} %copy-done.30) | copy-start | bytes 9220
  264.1 18.7 %all-to-all-start.4 = ((bf16[4,128,768]{2,1,0:T(8,128)(2,1)}), bf16[4,128,768]{2,1,0:T(8,128)(2,1)}, u32[]{:S(2)}, u32[]{:S(2)}) async-start(bf16[4,128,768]{2,1,0:T(8,128)(2,1)} %bitcast.131), calls=%async_computation.5 | async-start | bytes 1572864 | tf_op jit(solution)/shard_map/all_to_all | solution.py:434
  268.3 15.8 %copy-start.13 = (bf16[1,128,768]{2,1,0:T(8,128)(2,1)S(1)}, bf16[1,128,768]{2,1,0:T(8,128)(2,1)}, u32[]{:S(2)}) copy-start(bf16[1,128,768]{2,1,0:T(8,128)(2,1)} %param.12) | copy-start | bytes 589828
  (25 other events, 74.4 us)
Sparse Core Ops, SparseCore 0:
  10.3 49.2 all-gather.5
  184.6 36.7 reduce-scatter.1
  240.3 76.2 all-gather.7

commit v3 on v2

--- a/solution.py
+++ b/solution.py
@@ -45,6 +45,50 @@
 
 PAD_ROWS = 16
 STEP = 128
+
+
+def project_kernel(heads, tokens_ref, gain_ref, in_ref, norm_ref, pair_ref, query_ref, score_ref):
+    f32, bf16 = jnp.float32, jnp.bfloat16
+    keys = heads * 2 * HD
+    norm = layer_norm(tokens_ref[...].astype(f32), gain_ref[...]).astype(bf16)
+    norm_ref[...] = norm
+    pair_ref[...] = jnp.dot(norm, in_ref[:, :keys], preferred_element_type=f32).astype(bf16)
+    rest = jnp.dot(norm, in_ref[:, keys:], preferred_element_type=f32)
+    for head in range(heads):
+        query = rest[:, head * HD : (head + 1) * HD]
+        query_ref[:, head * LANES : (head + 1) * LANES] = jnp.concatenate(
+            [query, jnp.zeros_like(query)], axis=1
+        ).astype(bf16)
+    scores = jnp.transpose(rest)[heads * HD : heads * HD + heads, :].astype(bf16)
+    for head in range(heads):
+        score_ref[head] = scores[head : head + 1, :]
+
+
+def project(heads, tokens, gain, weights):
+    slot, width = tokens.shape
+    block = 256
+    return pl.pallas_call(
+        functools.partial(project_kernel, heads),
+        grid=(slot // block,),
+        in_specs=[
+            pl.BlockSpec((block, width), lambda r: (r, 0)),
+            pl.BlockSpec((1, width), lambda r: (0, 0)),
+            pl.BlockSpec(weights.shape, lambda r: (0, 0)),
+        ],
+        out_specs=[
+            pl.BlockSpec((block, width), lambda r: (r, 0)),
+            pl.BlockSpec((block, heads * LANES), lambda r: (r, 0)),
+            pl.BlockSpec((block, heads * LANES), lambda r: (r, 0)),
+            pl.BlockSpec((heads, 1, block), lambda r: (0, 0, r)),
+        ],
+        out_shape=[
+            jax.ShapeDtypeStruct((slot, width), jnp.bfloat16),
+            jax.ShapeDtypeStruct((slot, heads * LANES), jnp.bfloat16),
+            jax.ShapeDtypeStruct((slot, heads * LANES), jnp.bfloat16),
+            jax.ShapeDtypeStruct((heads, 1, slot), jnp.bfloat16),
+        ],
+        name="project",
+    )(tokens, gain, weights)
 
 
 def attend_body(first, tiles, base, idx_ref, q_ref, kv_ref, key_ref, out_ref, prob_ref, score_ref, pair_ref, gate_ref):
@@ -141,7 +185,7 @@
         grid=(heads, parts),
         in_specs=[
             pl.BlockSpec((1, 1, block, keep), lambda h, r, b: (h, r, 0, 0)),
-            pl.BlockSpec((block, LANES), lambda h, r, b: (r, h)),
+            pl.BlockSpec((block, LANES), lambda h, r, b: (r * (chunk // block) + b[1], h)),
             pl.BlockSpec((slot, LANES), lambda h, r, b: (0, h)),
             pl.BlockSpec((1, 1, slot), lambda h, r, b: (h, 0, 0)),
         ],
@@ -213,7 +257,7 @@
             out_ref[at, height - PAD_ROWS :, :] = jnp.concatenate(rows_of, axis=0).astype(bf16)
 
 
-def attend_back_kernel(parts, chunk, *refs):
+def attend_back_kernel(parts, chunk, base_ref, *refs):
     part = pl.program_id(1)
     for at in range(parts):
         pl.when(part == at)(
@@ -221,27 +265,35 @@
         )
 
 
-def attend_back(count, query, grad, pairs, prob):
+def attend_back(count, base, query, grad, pairs, prob):
     heads, parts, block, slot = prob.shape
     width = pairs.shape[1]
     height = slot // count + PAD_ROWS
     chunk = slot // parts
     return pl.pallas_call(
         functools.partial(attend_back_kernel, parts, chunk),
+        grid_spec=pltpu.PrefetchScalarGridSpec(
+        num_scalar_prefetch=1,
         grid=(heads, parts),
         in_specs=[
-            pl.BlockSpec((block, LANES), lambda h, r: (r, h)),
-            pl.BlockSpec((block, LANES), lambda h, r: (r, h)),
-            pl.BlockSpec((slot, LANES), lambda h, r: (0, h)),
-            pl.BlockSpec((1, 1, block, slot), lambda h, r: (h, r, 0, 0)),
+            pl.BlockSpec((block, LANES), lambda h, r, b: (r * (chunk // block) + b[1], h)),
+            pl.BlockSpec((block, LANES), lambda h, r, b: (r, h)),
+            pl.BlockSpec((slot, LANES), lambda h, r, b: (0, h)),
+            pl.BlockSpec((1, 1, block, slot), lambda h, r, b: (h, r, 0, 0)),
         ],
         out_specs=[
-            pl.BlockSpec((block, LANES), lambda h, r: (r, h)),
-            pl.BlockSpec((count, height, LANES), lambda h, r: (0, 0, h)),
-            pl.BlockSpec((1, LANES, slot), lambda h, r: (h, 0, 0)),
-            pl.BlockSpec((1, HD, block), lambda h, r: (h, 0, r)),
-            pl.BlockSpec((1, 8, slot), lambda h, r: (h, 0, 0)),
-        ],
+            pl.BlockSpec((block, LANES), lambda h, r, b: (r, h)),
+            pl.BlockSpec((count, height, LANES), lambda h, r, b: (0, 0, h)),
+            pl.BlockSpec((1, LANES, slot), lambda h, r, b: (h, 0, 0)),
+            pl.BlockSpec((1, HD, block), lambda h, r, b: (h, 0, r)),
+            pl.BlockSpec((1, 8, slot), lambda h, r, b: (h, 0, 0)),
+        ],
+        scratch_shapes=[
+            pltpu.VMEM((block, slot), jnp.float32),
+            pltpu.VMEM((LANES, slot), jnp.float32),
+            pltpu.VMEM((8, slot), jnp.float32),
+        ],
+        ),
         out_shape=[
             jax.ShapeDtypeStruct((parts * block, heads * LANES), jnp.bfloat16),
             jax.ShapeDtypeStruct((count, height, width), jnp.bfloat16),
@@ -249,13 +301,8 @@
             jax.ShapeDtypeStruct((heads, HD, parts * block), jnp.bfloat16),
             jax.ShapeDtypeStruct((heads, 8, slot), jnp.float32),
         ],
-        scratch_shapes=[
-            pltpu.VMEM((block, slot), jnp.float32),
-            pltpu.VMEM((LANES, slot), jnp.float32),
-            pltpu.VMEM((8, slot), jnp.float32),
-        ],
         name="attend_back",
-    )(query, grad, pairs, prob)
+    )(base, query, grad, pairs, prob)
 
 
 def weight_kernel(turned_ref, dq_ref, gates_ref, score_ref, slot_ref, norm_ref, in_ref, gain_ref, out_ref):
@@ -500,8 +547,10 @@
 
     cot_group = lax.all_gather(cotangent[0], "sp", axis=0, tiled=True)
     kept = jnp.transpose(kept_keys[0], (2, 0, 1, 3))
-    tokens_slot, cot_group, out_came, fc_came, kept = lax.optimization_barrier(
-        (tokens_slot, cot_group, out_came, fc_came, kept)
+    out_full = dp_join(out_own, out_came)
+    fc_part = dp_join(fc_own, fc_came)
+    tokens_slot, cot_group, out_full, fc_part, kept = lax.optimization_barrier(
+        (tokens_slot, cot_group, out_full, fc_part, kept)
     )
 
     def group_of(values):
@@ -510,27 +559,17 @@
 
     inputs = tokens[0].astype(f32)
     inputs_group = group_of(tokens_slot).astype(f32)
-    norm_slot = layer_norm(tokens_slot.astype(f32), gain_one).astype(bf16)
-    pairs = jnp.dot(norm_slot, all_in[:, :keys], preferred_element_type=f32).astype(bf16)
-    score_slot = lax.dot_general(
-        all_in[:, head_cols : head_cols + heads], norm_slot, (((0,), (1,)), ((), ())), preferred_element_type=f32
-    ).astype(bf16)
+    norm_slot, pairs, query_slot, score_slot = project(heads, tokens_slot, gain_one[None], all_in)
     key_score = lax.dynamic_index_in_dim(
         score_slot.reshape(heads, seg_count, ctx_count, rows), ctx_at, 2, keepdims=False
     ).reshape(heads, group_rows)
     norm_one = group_of(norm_slot)
-    query_weight = jnp.pad(
-        all_in[:, keys:head_cols].reshape(width, heads, HD), ((0, 0), (0, 0), (0, HD))
-    ).reshape(width, heads * LANES)
-    query_wide = jnp.dot(norm_one, query_weight, preferred_element_type=f32).astype(bf16)
-    base = (ctx_at * rows).astype(jnp.int32)[None]
-    head_outs, prob = attend(base, kept, query_wide, pairs, score_slot[:, None])
+    base = jnp.stack([ctx_at * rows, ctx_at]).astype(jnp.int32)
+    head_outs, prob = attend(base, kept, query_slot, pairs, score_slot)
     head_outs, proj_came = lax.optimization_barrier((head_outs, proj_came))
     attended = head_outs.reshape(heads * HD, group_rows)
     attended_all = lax.all_gather(attended, "sp", axis=0, tiled=True)
-    out_full = dp_join(out_own, out_came)
     out_part = lax.dynamic_slice_in_dim(out_full, sp_at * heads * HD, heads * HD, 0)
-    fc_part = dp_join(fc_own, fc_came)
     proj_part = dp_join(proj_own, proj_came)
 
     group_at = jnp.arange(group_rows, dtype=jnp.int32)
@@ -550,10 +589,10 @@
     fc_parts = contract_rows(norm_two, grad_pre).astype(bf16).reshape(dp_count, ctx_count, piece, width)
     proj_parts = contract_rows(active, grad_out_group).astype(bf16).reshape(dp_count, ctx_count, -1, width)
     grad_pre, fc_parts, proj_parts = lax.optimization_barrier((grad_pre, fc_parts, proj_parts))
-    fc_came = lax.all_to_all(
-        jnp.transpose(fc_parts, (1, 0, 2, 3)), "ctx", split_axis=0, concat_axis=0, tiled=True
-    )
-    proj_dp = dp_scatter(proj_parts)
+    mlp_parts = jnp.transpose(jnp.concatenate([fc_parts, proj_parts], axis=2), (1, 0, 2, 3))
+    mlp_ctx = lax.psum_scatter(
+        mlp_parts.reshape(ctx_count, -1, width), "ctx", scatter_dimension=0, tiled=False
+    ).reshape(dp_count, -1, width)
     grad_norm_parts = contract_cols(grad_pre, fc_part).astype(bf16)
     grad_norm_two = exchange_sum(grad_norm_parts.reshape(seg_count, rows, width), "sp")
     _, second_pull = jax.vjp(layer_norm, mixed, gain_two)
@@ -565,24 +604,21 @@
     out_wide = jnp.pad(out_part.reshape(heads, HD, width), ((0, 0), (HD, 0), (0, 0))).reshape(heads * LANES, width)
     grad_wide = contract_cols(grad_branch, out_wide).astype(bf16)
     out_mine = jnp.dot(attended, grad_branch, preferred_element_type=f32).astype(bf16)
-    grad_wide, fc_came, proj_dp, out_mine = lax.optimization_barrier((grad_wide, fc_came, proj_dp, out_mine))
+    grad_wide, out_mine = lax.optimization_barrier((grad_wide, out_mine))
     out_sum = dp_sum(out_mine)
-    fc_own = dp_scatter(jnp.sum(fc_came.astype(f32), axis=0).astype(bf16))
-    proj_came = lax.all_to_all(proj_dp, "ctx", split_axis=0, concat_axis=0, tiled=True)
     gain_cols = jnp.stack([gain_one, second_gain_grad], axis=1)
     grad_wide, gain_cols = lax.optimization_barrier((grad_wide, gain_cols))
     query_grads, pair_grads, turned, query_turned, gates = attend_back(
-        ctx_count, query_wide, grad_wide, pairs, prob
-    )
+        ctx_count, base, query_slot, grad_wide, pairs, prob
+    )
+    turned, out_sum = lax.optimization_barrier((turned, out_sum))
     pair_mine = lax.psum_scatter(pair_grads, "ctx", scatter_dimension=0, tiled=False)
-    small = weight_grad(turned, query_turned, gates, score_slot, norm_slot, norm_one, all_in, gain_cols)
-    small, fc_own, proj_came, out_sum = lax.optimization_barrier((small, fc_own, proj_came, out_sum))
+    small = weight_grad(turned, query_turned, gates, score_slot[:, 0], norm_slot, norm_one, all_in, gain_cols)
     late = jnp.concatenate(
         [dp_scatter(small.reshape(dp_count, ctx_count, piece, width)), out_sum.reshape(ctx_count, -1, width)], axis=1
     )
     late_sum = exchange_sum(late, "ctx").astype(bf16)
-    proj_sum = jnp.sum(proj_came.astype(f32), axis=0).astype(bf16)
-    gradients = jnp.concatenate([late_sum[:piece], fc_own, proj_sum, late_sum[piece:]], axis=0)
+    gradients = jnp.concatenate([late_sum[:piece], dp_scatter(mlp_ctx), late_sum[piece:]], axis=0)
     pair_mine, gradients, active_late = lax.optimization_barrier((pair_mine, gradients, active))
     gathered = lax.all_gather(gradients, ("sp", "ctx"), axis=0, tiled=False).reshape(seg_count, ctx_count, -1, width)
     proj_piece = hidden // (seg_count * dp_count * ctx_count)

time: 338 us -> 317 us (0.938)
  starting transfers between devices: 37.4 us -> 25.1 us
  Pallas kernels: 54.3 us -> 64.8 us
  matrix products: 24 us -> 14.9 us
  other arithmetic: 27.8 us -> 20.3 us
  waiting for transfers between devices: 130 us -> 125 us
    all_to_all x2 -> x0, waiting for transfers between devices: 12.4 us -> none  [the longest x1 12.4 us: per_device(): lax.all_to_all(jnp.transpose(fc_parts, (1, 0, 2, 3)), 'ctx', split_axis=0...]
    pallas_call x1 -> x2, Pallas kernels: 14.4 us -> 24.5 us  [the longest x1 15.1 us: attend_back(): pl.pallas_call(functools.partial(attend_back_kernel, parts, chunk), grid_...]
    all_to_all x2 -> x0, starting transfers between devices: 9.08 us -> none  [the longest x1 4.94 us: per_device(): lax.all_to_all(jnp.transpose(fc_parts, (1, 0, 2, 3)), 'ctx', split_axis=0...]
    all_to_all x4, waiting for transfers between devices: 49.2 us -> 57.2 us  [exchange_sum(): came = lax.all_to_all(parts, axis, split_axis=0, concat_axis=0, tiled=True)]
    dot_general x3 -> x0, matrix products: 5.5 us -> none  [the longest x1 2.98 us: per_device(): jnp.dot(norm_slot, all_in[:, :keys], preferred_element_type=f32)]
    ppermute x3 -> x2, starting transfers between devices: 4.68 us -> 0.82 us  [dp_scatter(): other = lax.ppermute(sent, 'dp', [(0, 1), (1, 0)])]
    ppermute x3 -> x2, waiting for transfers between devices: 14.4 us -> 15.3 us  [dp_scatter(): other = lax.ppermute(sent, 'dp', [(0, 1), (1, 0)])]
  transfers between devices with their start and end apart: 17 -> 15, of which waited for: 11 -> 8; matrix products, arithmetic and copies ran while one was open for 15% -> 13% of each run, Pallas kernels for 14% -> 18%
where the time goes in v3:
time: 317 us; the launch traced here: 315 us
  waiting for transfers between devices  125 us (39%)
  Pallas kernels  64.8 us (20%)
  blocking collectives  26 us (8%)
  starting transfers between devices  25.1 us (8%)
  local copies, waits for them, and re-layouts  24.1 us (8%)
  other arithmetic  20.3 us (6%)
  between operations  15 us (5%)
  matrix products  14.9 us (5%)
    all_to_all x4, waiting for transfers between devices, exchange_sum(): came = lax.all_to_all(parts, axis, split_axis=0, concat_axis=0, tiled=True)  57.2 us
    all_gather x1, waiting for transfers between devices, per_device(): lax.all_gather(gradients, ('sp', 'ctx'), axis=0, tiled=False)  30.8 us
    ppermute x3, waiting for transfers between devices, dp_send(): return lax.ppermute(mine, 'dp', [(0, 1), (1, 0)])  21 us
    pallas_call x1, Pallas kernels, attend(): pl.pallas_call(functools.partial(attend_kernel, parts, chunk), grid_spec=...  20.3 us
    all_to_all x4, starting transfers between devices, exchange_sum(): came = lax.all_to_all(parts, axis, split_axis=0, concat_axis=0, tiled=True)  16 us
    ppermute x2, waiting for transfers between devices, dp_scatter(): other = lax.ppermute(sent, 'dp', [(0, 1), (1, 0)])  15.3 us
    pallas_call x1, Pallas kernels, attend_back(): pl.pallas_call(functools.partial(attend_back_kernel, parts, chunk), grid_...  15.1 us
    all_gather x1, blocking collectives, per_device(): cot_group = lax.all_gather(cotangent[0], 'sp', axis=0, tiled=True)  9.91 us
  transfers between devices with their start and end apart: 15, of which 8 were waited for; matrix products, arithmetic and copies ran while one was open for 13% of the time, Pallas kernels for 18%

profile of v3, /device:TPU:0, one launch (start us, length us, event | category | flops | bytes accessed | tf_op | source)
XLA Modules:
  0.0 315.2 jit_solution(4104102176707862128)
XLA Ops:
  12.5 2.1 arrange.1
  14.6 3.0 collective-permute-start
  19.4 2.0 pad_maximum_fusion.3
  21.4 9.9 %all-gather.1 = bf16[1,512,768]{2,1,0:T(8,128)(2,1)} all-gather(bf16[1,128,768]{2,1,0:T(8,128)(2,1)S(1)} %copy-done.6), channel_id=3, replica_groups=mesh['dp'=2,'sp'=4,'ctx'=4] {'sp'}, dimensions={1}, use_global_device_ids=true | all-gather | bytes 983040 | tf_op jit(solution)/shard_map/all_gather | solution.py:548
  38.5 10.4 %collective-permute-done.1 = bf16[384,768]{1,0:T(8,128)(2,1)} collective-permute-done((bf16[384,768]{1,0:T(8,128)(2,1)S(1)}, bf16[384,768]{1,0:T(8,128)(2,1)}, u32[]{:S(2)}, u32[]{:S(2)}) %collective-permute-start.1) | collective-permute-done | bytes 589856 | tf_op jit(solution)/shard_map/ppermute | solution.py:442
  49.0 1.9 maximum_select_fusion
  50.9 10.6 %collective-permute-done.2 = bf16[384,768]{1,0:T(8,128)(2,1)S(1)} collective-permute-done((bf16[384,768]{1,0:T(8,128)(2,1)S(1)}, bf16[384,768]{1,0:T(8,128)(2,1)S(1)}, u32[]{:S(2)}, u32[]{:S(2)}) %collective-permute-start.2) | collective-permute-done | bytes 589856 | tf_op jit(solution)/shard_map/ppermute | solution.py:442
  63.0 9.4 %project.1 = (bf16[2048,768]{1,0:T(8,128)(2,1)}, bf16[2048,384]{1,0:T(8,128)(2,1)}, bf16[2048,384]{1,0:T(8,128)(2,1)}, bf16[3,1,2048]{2,1,0:T(2,128)(2,1)}) custom-call(bf16[2048,768]{1,0:T(8,128)(2,1)} %bitcast.104, f32[1,768]{1,0:T(1,128)} %maximum_convert_fusion.gain_ref, bf16[768,640]{1,0:T(8,128)(2,1)} %pad_maximum_fusion.1.in_ref), custom_call_target="tpu_custom_call" | custom-call | tf_op jit(solution)/shard_map/project/pallas_call | solution.py:70
  72.4 20.3 %attend.1 = (bf16[3,64,512]{2,1,0:T(8,128)(2,1)}, bf16[3,4,128,2048]{3,2,1,0:T(8,128)(2,1)}) custom-call(s32[2]{0:T(128)} %pad_add_fusion.base_ref, s32[3,4,128,64]{3,2,1,0:T(8,128)} %bitcast.109, bf16[2048,384]{1,0:T(8,128)(2,1)} %get-tuple-element.52.refs_1_.refs_0_, bf16[2048,384]{1,0:T(8,128)(2,1)} %get-tuple-element.53.refs_2_, ...), custom_call_target="tpu_custom_call" | custom-call | tf_op jit(solution)/shard_map/attend/pallas_call | solution.py:202
  92.7 7.8 %all_gather.20 = bf16[768,512]{1,0:T(8,128)(2,1)S(1)} all-gather(bf16[192,512]{1,0:T(8,128)(2,1)} %bitcast.122), channel_id=1, replica_groups=mesh['dp'=2,'sp'=4,'ctx'=4] {'sp'}, dimensions={0}, use_global_device_ids=true | all-gather | bytes 983040 | tf_op jit(solution)/shard_map/all_gather | solution.py:571
  105.2 2.9 fusion.6
  111.8 2.8 convolution_convert_fusion.3
  114.6 3.5 %all-to-all-start = ((bf16[4,128,768]{2,1,0:T(8,128)(2,1)}), bf16[4,128,768]{2,1,0:T(8,128)(2,1)S(1)}, u32[]{:S(2)}, u32[]{:S(2)}) async-start(bf16[4,128,768]{2,1,0:T(8,128)(2,1)} %bitcast.118), calls=%async_computation | async-start | bytes 1572864 | tf_op jit(solution)/shard_map/all_to_all | solution.py:481
  120.4 9.3 %all-to-all-done = bf16[4,128,768]{2,1,0:T(8,128)(2,1)S(1)} async-done(((bf16[4,128,768]{2,1,0:T(8,128)(2,1)}), bf16[4,128,768]{2,1,0:T(8,128)(2,1)S(1)}, u32[]{:S(2)}, u32[]{:S(2)}) %all-to-all-start) | async-done | bytes 786464 | tf_op jit(solution)/shard_map/all_to_all | solution.py:481
  130.5 8.2 %all_gather.21 = bf16[512,768]{1,0:T(8,128)(2,1)S(1)} all-gather(bf16[128,768]{1,0:T(8,128)(2,1)S(1)} %fusion.16), channel_id=1, replica_groups=mesh['dp'=2,'sp'=4,'ctx'=4] {'sp'}, dimensions={0}, use_global_device_ids=true | all-gather | bytes 983040 | tf_op jit(solution)/shard_map/all_gather | solution.py:602
  140.4 1.7 collective-permute-start.4
  142.1 15.1 %attend_back.1 = (bf16[512,384]{1,0:T(8,128)(2,1)}, bf16[4,528,384]{2,1,0:T(8,128)(2,1)}, bf16[3,128,2048]{2,1,0:T(8,128)(2,1)}, bf16[3,64,512]{2,1,0:T(8,128)(2,1)}, f32[3,8,2048]{2,1,0:T(8,128)}) custom-call(s32[2]{0:T(128)} %pad_add_fusion.base_ref, bf16[2048,384]{1,0:T(8,128)(2,1)} %get-tuple-element.52.refs_1_.refs_0_, ...), custom_call_target="tpu_custom_call" | custom-call | tf_op jit(solution)/shard_map/attend_back/pallas_call | solution.py:273
  158.6 2.1 constant_dynamic-slice_fusion
  162.4 6.4 %weight_grad.1 = bf16[768,768]{1,0:T(8,128)(2,1)} custom-call(bf16[3,128,2048]{2,1,0:T(8,128)(2,1)} %get-tuple-element.69.turned_ref, bf16[3,64,512]{2,1,0:T(8,128)(2,1)} %get-tuple-element.70.dq_ref, f32[3,8,2048]{2,1,0:T(8,128)} %get-tuple-element.71.gates_ref, bf16[3,2048]{1,0:T(4,128)(2,1)} %bitcast.128, bf16[2048,768]{1,0:T(8,128)(2,1)} %get-tuple-element.72.slot_ref, ...), custom_call_target="tpu_custom_call" | custom-call | tf_op jit(solution)/shard_map/weight_grad/pallas_call | solution.py:333
  168.8 2.0 dynamic-slice_bitcast_fusion
  171.1 15.3 %collective-permute-done.5 = bf16[4,96,768]{2,1,0:T(8,128)(2,1)} collective-permute-done((bf16[4,96,768]{2,1,0:T(8,128)(2,1)}, bf16[4,96,768]{2,1,0:T(8,128)(2,1)}, u32[]{:S(2)}, u32[]{:S(2)}) %collective-permute-start.5) | collective-permute-done | bytes 589856 | tf_op jit(solution)/shard_map/ppermute | solution.py:459
  188.6 4.8 %all-to-all-start.1 = ((bf16[4,144,768]{2,1,0:T(8,128)(2,1)}), bf16[4,144,768]{2,1,0:T(8,128)(2,1)S(1)}, u32[]{:S(2)}, u32[]{:S(2)}) async-start(bf16[4,144,768]{2,1,0:T(8,128)(2,1)} %pad_maximum_fusion.2), calls=%async_computation.2 | async-start | bytes 1769472 | tf_op jit(solution)/shard_map/all_to_all | solution.py:481
  193.4 1.7 dynamic-slice_bitcast_fusion.1
  195.6 21.5 %all-to-all-done.1 = bf16[4,144,768]{2,1,0:T(8,128)(2,1)S(1)} async-done(((bf16[4,144,768]{2,1,0:T(8,128)(2,1)}), bf16[4,144,768]{2,1,0:T(8,128)(2,1)S(1)}, u32[]{:S(2)}, u32[]{:S(2)}) %all-to-all-start.1) | async-done | bytes 884768 | tf_op jit(solution)/shard_map/all_to_all | solution.py:481
  220.2 3.3 %finish.1 = bf16[512,768]{1,0:T(8,128)(2,1)} custom-call(bf16[528,384]{1,0:T(8,128)(2,1)} %bitcast.127, bf16[512,384]{1,0:T(8,128)(2,1)} %get-tuple-element.79.dq_ref, bf16[3,512]{1,0:T(4,128)(2,1)} %bitcast.129, bf16[768,640]{1,0:T(8,128)(2,1)} %pad_maximum_fusion.1.in_ref), custom_call_target="tpu_custom_call" | custom-call | tf_op jit(solution)/shard_map/finish/pallas_call | solution.py:366
  223.5 3.5 %all-to-all-start.3 = ((bf16[4,128,768]{2,1,0:T(8,128)(2,1)}), bf16[4,128,768]{2,1,0:T(8,128)(2,1)S(1)}, u32[]{:S(2)}, u32[]{:S(2)}) async-start(bf16[4,128,768]{2,1,0:T(8,128)(2,1)} %bitcast.110), calls=%async_computation.5 | async-start | bytes 1572864 | tf_op jit(solution)/shard_map/all_to_all | solution.py:481
  227.0 3.6 %convolution_convert_fusion.2 = bf16[512,768]{1,0:T(8,128)(2,1)} fusion(bf16[512,768]{1,0:T(8,128)(2,1)} %copy-done.23, bf16[384,768]{1,0:T(8,128)(2,1)} %collective-permute-done.3, bf16[384,768]{1,0:T(8,128)(2,1)} %get-tuple-element.56, pred[]{:T(512)S(6)} %eq.5), kind=kOutput, calls=%fused_computation.19 | convolution fusion | flops 609681408 | bytes 2752513 | tf_op jit(solution)/shard_map/dot_general | solution.py:628
  230.7 12.5 %all-to-all-done.3 = bf16[4,128,768]{2,1,0:T(8,128)(2,1)S(1)} async-done(((bf16[4,128,768]{2,1,0:T(8,128)(2,1)}), bf16[4,128,768]{2,1,0:T(8,128)(2,1)S(1)}, u32[]{:S(2)}, u32[]{:S(2)}) %all-to-all-start.3) | async-done | bytes 786464 | tf_op jit(solution)/shard_map/all_to_all | solution.py:481
  243.2 4.2 %all-to-all-start.2 = ((bf16[4,128,768]{2,1,0:T(8,128)(2,1)}), bf16[4,128,768]{2,1,0:T(8,128)(2,1)}, u32[]{:S(2)}, u32[]{:S(2)}) async-start(bf16[4,128,768]{2,1,0:T(8,128)(2,1)} %bitcast.117), calls=%async_computation.4 | async-start | bytes 1572864 | tf_op jit(solution)/shard_map/all_to_all | solution.py:481
  248.1 13.8 %all-to-all-done.2 = bf16[4,128,768]{2,1,0:T(8,128)(2,1)} async-done(((bf16[4,128,768]{2,1,0:T(8,128)(2,1)}), bf16[4,128,768]{2,1,0:T(8,128)(2,1)}, u32[]{:S(2)}, u32[]{:S(2)}) %all-to-all-start.2) | async-done | bytes 786464 | tf_op jit(solution)/shard_map/all_to_all | solution.py:481
  264.2 30.8 %all-gather.8.cloned.1.call-done = bf16[5376,768]{1,0:T(8,128)(2,1)} async-done(((bf16[336,768]{1,0:T(8,128)(2,1)}), bf16[5376,768]{1,0:T(8,128)(2,1)}) %all-gather.8.cloned.1.call-update) | async-done | bytes 8257552 | tf_op jit(solution)/shard_map/all_gather | solution.py:623
  296.2 8.3 %unpack.1 = (f32[384,2304]{1,0:T(8,128)}, f32[384,12]{1,0:T(8,128)}, f32[384,3072]{1,0:T(8,128)}, f32[4,4,96,768]{3,2,1,0:T(8,128)}) custom-call(bf16[4,4,336,768]{3,2,1,0:T(8,128)(2,1)} %bitcast.100), custom_call_target="tpu_custom_call" | custom-call | tf_op jit(solution)/shard_map/unpack/pallas_call | solution.py:396
  (143 shorter events, 45.3 us)
Async XLA Ops:
  7.2 4.3 %copy-start = (bf16[384,2304]{1,0:T(8,128)(2,1)S(1)}, bf16[384,2304]{1,0:T(8,128)(2,1)}, u32[]{:S(2)}) copy-start(bf16[384,2304]{1,0:T(8,128)(2,1)} %param.16) | copy-start | bytes 5308420
  7.2 55.8 %all-gather.6.cloned.1.call-start = ((), (), s32[]{:S(2)}) async-start(), calls=%async_computation.8 | async-start | bytes 3342336 | tf_op jit(solution)/shard_map/all_gather | solution.py:530
  7.9 185.5 %reduce-scatter.5.cloned.1.call-start = ((), (), s32[]{:S(2)}) async-start(), calls=%async_computation.7 | async-start | bytes 2949120 | tf_op jit(solution)/shard_map/reduce_scatter | solution.py:593
  14.6 16.8 %collective-permute-start = (bf16[400,640]{1,0:T(8,128)(2,1)}, bf16[400,640]{1,0:T(8,128)(2,1)S(1)}, u32[]{:S(2)}, u32[]{:S(2)}) collective-permute-start(bf16[400,640]{1,0:T(8,128)(2,1)} %arrange.1), channel_id=1, source_target_pairs={{0,16},{16,0},{1,17},{17,1},{2,18},{18,2},{3,19},{19,3},{4,20},{20... | collective-permute-start | bytes 1536008 | tf_op jit(solution)/shard_map/ppermute | solution.py:524
  18.2 3.2 %copy-start.6 = (bf16[1,128,768]{2,1,0:T(8,128)(2,1)S(1)}, bf16[1,128,768]{2,1,0:T(8,128)(2,1)}, u32[]{:S(2)}) copy-start(bf16[1,128,768]{2,1,0:T(8,128)(2,1)} %param.12) | copy-start | bytes 589828
  19.4 12.0 %copy-start.4 = (bf16[400,640]{1,0:T(8,128)(2,1)S(1)}, bf16[400,640]{1,0:T(8,128)(2,1)}, u32[]{:S(2)}) copy-start(bf16[400,640]{1,0:T(8,128)(2,1)} %arrange.1) | copy-start | bytes 1536004
  31.5 2.6 copy-start.14
  32.7 16.3 %collective-permute-start.1 = (bf16[384,768]{1,0:T(8,128)(2,1)S(1)}, bf16[384,768]{1,0:T(8,128)(2,1)}, u32[]{:S(2)}, u32[]{:S(2)}) collective-permute-start(bf16[384,768]{1,0:T(8,128)(2,1)S(1)} %copy-done.11), channel_id=1, source_target_pairs={{0,16},{16,0},{1,17},{17,1},{2,18},{18,2},{3,19},{19,3},{4,20},{20... | collective-permute-start | bytes 1769480 | tf_op jit(solution)/shard_map/ppermute | solution.py:442
  35.9 25.6 %collective-permute-start.2 = (bf16[384,768]{1,0:T(8,128)(2,1)S(1)}, bf16[384,768]{1,0:T(8,128)(2,1)S(1)}, u32[]{:S(2)}, u32[]{:S(2)}) collective-permute-start(bf16[384,768]{1,0:T(8,128)(2,1)S(1)} %get-tuple-element.48), channel_id=1, source_target_pairs={{0,16},{16,0},{1,17},{17,1},{2,18},{18,2},{3,19},{19,3},{4,20},{20... | collective-permute-start | bytes 1769480 | tf_op jit(solution)/shard_map/ppermute | solution.py:442
  36.5 56.2 %collective-permute-start.3 = (bf16[384,768]{1,0:T(8,128)(2,1)}, bf16[384,768]{1,0:T(8,128)(2,1)}, u32[]{:S(2)}, u32[]{:S(2)}) collective-permute-start(bf16[384,768]{1,0:T(8,128)(2,1)} %get-tuple-element.56), channel_id=1, source_target_pairs={{0,16},{16,0},{1,17},{17,1},{2,18},{18,2},{3,19},{19,3},{4,20},{20... | collective-permute-start | bytes 1769480 | tf_op jit(solution)/shard_map/ppermute | solution.py:442
  50.9 50.8 %copy-start.5 = (bf16[768,768]{1,0:T(8,128)(2,1)}, bf16[768,768]{1,0:T(8,128)(2,1)S(1)}, u32[]{:S(2)}) copy-start(bf16[768,768]{1,0:T(8,128)(2,1)S(1)} %maximum_select_fusion) | copy-start | bytes 3538948
  104.9 4.2 %copy-start.23 = (bf16[512,768]{1,0:T(8,128)(2,1)}, bf16[512,768]{1,0:T(8,128)(2,1)S(1)}, u32[]{:S(2)}) copy-start(bf16[512,768]{1,0:T(8,128)(2,1)S(1)} %get-tuple-element.77) | copy-start | bytes 2359300
  111.8 18.6 %copy-start.18 = (pred[128]{0:T(512)(128)(4,1)}, pred[128]{0:T(512)(128)(4,1)S(1)}, u32[]{:S(2)}) copy-start(pred[128]{0:T(512)(128)(4,1)S(1)} %add_compare_fusion) | copy-start | bytes 388
  114.6 15.1 %all-to-all-start = ((bf16[4,128,768]{2,1,0:T(8,128)(2,1)}), bf16[4,128,768]{2,1,0:T(8,128)(2,1)S(1)}, u32[]{:S(2)}, u32[]{:S(2)}) async-start(bf16[4,128,768]{2,1,0:T(8,128)(2,1)} %bitcast.118), calls=%async_computation | async-start | bytes 1572864 | tf_op jit(solution)/shard_map/all_to_all | solution.py:481
  118.1 101.2 %reduce-scatter.3.cloned.1.call-start = ((), (), s32[]{:S(2)}) async-start(), calls=%async_computation.6 | async-start | bytes 2027520 | tf_op jit(solution)/shard_map/reduce_scatter | solution.py:615
  130.1 8.7 %copy-start.10 = (bf16[3,64,512]{2,1,0:T(8,128)(2,1)S(1)}, bf16[3,64,512]{2,1,0:T(8,128)(2,1)}, u32[]{:S(2)}) copy-start(bf16[3,64,512]{2,1,0:T(8,128)(2,1)} %get-tuple-element.57) | copy-start | bytes 589828
  130.3 8.7 %copy-start.13 = (bf16[3,128,768]{2,1,0:T(8,128)(2,1)S(1)}, bf16[3,128,768]{2,1,0:T(8,128)(2,1)}, u32[]{:S(2)}) copy-start(bf16[3,128,768]{2,1,0:T(8,128)(2,1)} %pad.9) | copy-start | bytes 1769476
  130.4 10.1 %copy-start.20 = (f32[128]{0:T(128)}, f32[128]{0:T(128)S(1)}, u32[]{:S(2)}) copy-start(f32[128]{0:T(128)S(1)} %negate_multiply_fusion.1) | copy-start | bytes 1540
  140.4 21.2 %collective-permute-start.4 = (bf16[192,768]{1,0:T(8,128)(2,1)S(1)}, bf16[192,768]{1,0:T(8,128)(2,1)S(1)}, u32[]{:S(2)}, u32[]{:S(2)}) collective-permute-start(bf16[192,768]{1,0:T(8,128)(2,1)S(1)} %convolution_convert_fusion.5), channel_id=1, source_target_pairs={{0,16},{16,0},{1,17},{17,1},{2,18},{18,2},{3,19},{19,3},{4,20},{20... | collective-permute-start | bytes 884744 | tf_op jit(solution)/shard_map/ppermute | solution.py:476
  168.8 17.7 %copy-start.3 = (bf16[768,768]{1,0:T(8,128)(2,1)S(1)}, bf16[768,768]{1,0:T(8,128)(2,1)}, u32[]{:S(2)}) copy-start(bf16[768,768]{1,0:T(8,128)(2,1)} %weight_grad.1) | copy-start | bytes 3538948
  170.8 15.7 %collective-permute-start.5 = (bf16[4,96,768]{2,1,0:T(8,128)(2,1)}, bf16[4,96,768]{2,1,0:T(8,128)(2,1)}, u32[]{:S(2)}, u32[]{:S(2)}) collective-permute-start(bf16[4,96,768]{2,1,0:T(8,128)(2,1)} %dynamic-slice_bitcast_fusion), channel_id=1, source_target_pairs={{0,16},{16,0},{1,17},{17,1},{2,18},{18,2},{3,19},{19,3},{4,20},{20... | collective-permute-start | bytes 1769480 | tf_op jit(solution)/shard_map/ppermute | solution.py:459
  171.1 16.5 %copy-start.7 = (bf16[192,768]{1,0:T(8,128)(2,1)S(1)}, bf16[192,768]{1,0:T(8,128)(2,1)}, u32[]{:S(2)}) copy-start(bf16[192,768]{1,0:T(8,128)(2,1)} %add_convert_fusion) | copy-start | bytes 884740
  188.6 28.5 %all-to-all-start.1 = ((bf16[4,144,768]{2,1,0:T(8,128)(2,1)}), bf16[4,144,768]{2,1,0:T(8,128)(2,1)S(1)}, u32[]{:S(2)}, u32[]{:S(2)}) async-start(bf16[4,144,768]{2,1,0:T(8,128)(2,1)} %pad_maximum_fusion.2), calls=%async_computation.2 | async-start | bytes 1769472 | tf_op jit(solution)/shard_map/all_to_all | solution.py:481
  193.4 101.6 %all-gather.8.cloned.1.call-start = ((), (), s32[]{:S(2)}) async-start(), calls=%async_computation.9 | async-start | bytes 8773632 | tf_op jit(solution)/shard_map/all_gather | solution.py:623
  195.1 22.2 %collective-permute-start.6 = (bf16[192,768]{1,0:T(8,128)(2,1)}, bf16[192,768]{1,0:T(8,128)(2,1)}, u32[]{:S(2)}, u32[]{:S(2)}) collective-permute-start(bf16[192,768]{1,0:T(8,128)(2,1)} %dynamic-slice_bitcast_fusion.1), channel_id=1, source_target_pairs={{0,16},{16,0},{1,17},{17,1},{2,18},{18,2},{3,19},{19,3},{4,20},{20... | collective-permute-start | bytes 884744 | tf_op jit(solution)/shard_map/ppermute | solution.py:459
  217.3 2.2 copy-start.16
  223.5 19.7 %all-to-all-start.3 = ((bf16[4,128,768]{2,1,0:T(8,128)(2,1)}), bf16[4,128,768]{2,1,0:T(8,128)(2,1)S(1)}, u32[]{:S(2)}, u32[]{:S(2)}) async-start(bf16[4,128,768]{2,1,0:T(8,128)(2,1)} %bitcast.110), calls=%async_computation.5 | async-start | bytes 1572864 | tf_op jit(solution)/shard_map/all_to_all | solution.py:481
  243.2 18.7 %all-to-all-start.2 = ((bf16[4,128,768]{2,1,0:T(8,128)(2,1)}), bf16[4,128,768]{2,1,0:T(8,128)(2,1)}, u32[]{:S(2)}, u32[]{:S(2)}) async-start(bf16[4,128,768]{2,1,0:T(8,128)(2,1)} %bitcast.117), calls=%async_computation.4 | async-start | bytes 1572864 | tf_op jit(solution)/shard_map/all_to_all | solution.py:481
  247.5 15.8 %copy-start.19 = (pred[128]{0:T(512)(128)(4,1)S(1)}, pred[128]{0:T(512)(128)(4,1)}, u32[]{:S(2)}) copy-start(pred[128]{0:T(512)(128)(4,1)} %copy-done.18) | copy-start | bytes 388
  247.5 15.8 %copy-start.21 = (f32[128]{0:T(128)S(1)}, f32[128]{0:T(128)}, u32[]{:S(2)}) copy-start(f32[128]{0:T(128)} %copy-done.20) | copy-start | bytes 1540
  304.6 2.3 copy-start.17
  304.6 4.2 %copy-start.1 = (bf16[384,2304]{1,0:T(8,128)(2,1)S(1)}, bf16[384,2304]{1,0:T(8,128)(2,1)}, u32[]{:S(2)}) copy-start(bf16[384,2304]{1,0:T(8,128)(2,1)} %param.16) | copy-start | bytes 5308420
  (7 other events, 8.7 us)
Sparse Core Ops, SparseCore 0:
  10.3 49.3 all-gather.5
  111.9 48.8 reduce-scatter.4
  163.6 36.3 reduce-scatter.2
  219.5 75.5 all-gather.7

commit v4 on v3

--- a/solution.py
+++ b/solution.py
@@ -45,28 +45,31 @@
 
 PAD_ROWS = 16
 STEP = 128
+SUB = 256
 
 
 def project_kernel(heads, tokens_ref, gain_ref, in_ref, norm_ref, pair_ref, query_ref, score_ref):
     f32, bf16 = jnp.float32, jnp.bfloat16
     keys = heads * 2 * HD
-    norm = layer_norm(tokens_ref[...].astype(f32), gain_ref[...]).astype(bf16)
-    norm_ref[...] = norm
-    pair_ref[...] = jnp.dot(norm, in_ref[:, :keys], preferred_element_type=f32).astype(bf16)
-    rest = jnp.dot(norm, in_ref[:, keys:], preferred_element_type=f32)
-    for head in range(heads):
-        query = rest[:, head * HD : (head + 1) * HD]
-        query_ref[:, head * LANES : (head + 1) * LANES] = jnp.concatenate(
-            [query, jnp.zeros_like(query)], axis=1
-        ).astype(bf16)
-    scores = jnp.transpose(rest)[heads * HD : heads * HD + heads, :].astype(bf16)
-    for head in range(heads):
-        score_ref[head] = scores[head : head + 1, :]
+    for start in range(0, tokens_ref.shape[0], SUB):
+        rows = slice(start, start + SUB)
+        norm = layer_norm(tokens_ref[rows, :].astype(f32), gain_ref[...]).astype(bf16)
+        norm_ref[rows, :] = norm
+        pair_ref[rows, :] = jnp.dot(norm, in_ref[:, :keys], preferred_element_type=f32).astype(bf16)
+        rest = jnp.dot(norm, in_ref[:, keys:], preferred_element_type=f32)
+        for head in range(heads):
+            query = rest[:, head * HD : (head + 1) * HD]
+            query_ref[rows, head * LANES : (head + 1) * LANES] = jnp.concatenate(
+                [query, jnp.zeros_like(query)], axis=1
+            ).astype(bf16)
+        scores = jnp.transpose(rest[:, LANES:])[heads * HD - LANES : heads * HD - LANES + heads, :].astype(bf16)
+        for head in range(heads):
+            score_ref[head, :, rows] = scores[head : head + 1, :]
 
 
 def project(heads, tokens, gain, weights):
     slot, width = tokens.shape
-    block = 256
+    block = 4 * SUB if slot % (4 * SUB) == 0 else SUB
     return pl.pallas_call(
         functools.partial(project_kernel, heads),
         grid=(slot // block,),
@@ -324,15 +327,14 @@
     lane = lax.broadcasted_iota(jnp.int32, small.shape, 1)
     at = heads * 3 * HD + heads
     small = jnp.where(lane == at, gain_grad, jnp.where(lane == at + 1, gain_ref[:, 1:2], small))
-    out_ref[:, :wide] = small.astype(bf16)
-    out_ref[:, wide:] = jnp.zeros((width, width - wide), bf16)
+    out_ref[...] = small.astype(bf16)
 
 
 def weight_grad(turned, dq, gates, score, norm_slot, norm_one, weights, gains):
     width = norm_one.shape[1]
     return pl.pallas_call(
         weight_kernel,
-        out_shape=jax.ShapeDtypeStruct((width, width), jnp.bfloat16),
+        out_shape=jax.ShapeDtypeStruct((width, weights.shape[1]), jnp.bfloat16),
         name="weight_grad",
     )(turned, dq, gates, score, norm_slot, norm_one, weights, gains)
 
@@ -370,10 +372,14 @@
     )(pair, dq, score, weights)
 
 
-def unpack_kernel(groups, heads, piece, parts, all_ref, qkv_ref, score_ref, fc_ref, proj_ref):
+def unpack_kernel(groups, heads, piece, parts, dp_ref, all_ref, qkv_ref, score_ref, fc_ref, proj_ref, *rest):
     f32 = jnp.float32
     keys = heads * 2 * HD
     part_cols = fc_ref.shape[1] // (groups * parts)
+    for out_ref in rest:
+        mine = out_ref.shape[0]
+        for at in range(mine):
+            out_ref[at] = all_ref[dp_ref[0] * mine + at, :, 2 * piece + proj_ref.shape[2] :, :].astype(f32)
     for step in range(all_ref.shape[1]):
         rows = slice(step * piece, (step + 1) * piece)
         for at in range(groups):
@@ -390,27 +396,30 @@
             proj_ref[at, step] = all_ref[at, step, 2 * piece : 2 * piece + proj_ref.shape[2], :].astype(f32)
 
 
-def unpack(gathered, heads, piece, proj_piece, parts, hidden):
+def unpack(at, gathered, heads, piece, proj_piece, parts, hidden):
     groups, count, rows, width = gathered.shape
     step = 1 if piece % 16 == 0 else count
+    blocks = [
+        ((count * piece, groups * heads * 3 * HD), (step * piece, groups * heads * 3 * HD), lambda c, d: (c, 0)),
+        ((count * piece, groups * heads), (step * piece, groups * heads), lambda c, d: (c, 0)),
+        ((count * piece, hidden), (step * piece, hidden), lambda c, d: (c, 0)),
+        ((groups, count, proj_piece, width), (groups, step, proj_piece, width), lambda c, d: (0, c, 0, 0)),
+    ]
+    if groups % parts == 0:
+        last = rows - 2 * piece - proj_piece
+        mine = groups // parts
+        blocks.append(((mine, count, last, width), (mine, step, last, width), lambda c, d: (0, c, 0, 0)))
     return pl.pallas_call(
         functools.partial(unpack_kernel, groups, heads, piece, parts),
-        grid=(count // step,),
-        in_specs=[pl.BlockSpec((groups, step, rows, width), lambda c: (0, c, 0, 0))],
-        out_specs=[
-            pl.BlockSpec((step * piece, groups * heads * 3 * HD), lambda c: (c, 0)),
-            pl.BlockSpec((step * piece, groups * heads), lambda c: (c, 0)),
-            pl.BlockSpec((step * piece, hidden), lambda c: (c, 0)),
-            pl.BlockSpec((groups, step, proj_piece, width), lambda c: (0, c, 0, 0)),
-        ],
-        out_shape=[
-            jax.ShapeDtypeStruct((count * piece, groups * heads * 3 * HD), jnp.float32),
-            jax.ShapeDtypeStruct((count * piece, groups * heads), jnp.float32),
-            jax.ShapeDtypeStruct((count * piece, hidden), jnp.float32),
-            jax.ShapeDtypeStruct((groups, count, proj_piece, width), jnp.float32),
-        ],
+        grid_spec=pltpu.PrefetchScalarGridSpec(
+            num_scalar_prefetch=1,
+            grid=(count // step,),
+            in_specs=[pl.BlockSpec((groups, step, rows, width), lambda c, d: (0, c, 0, 0))],
+            out_specs=[pl.BlockSpec(block, index) for _, block, index in blocks],
+        ),
+        out_shape=[jax.ShapeDtypeStruct(shape, jnp.float32) for shape, _, _ in blocks],
         name="unpack",
-    )(gathered)
+    )(at, gathered)
 
 
 def arrange_kernel(heads, rows, qkv_ref, score_ref, gains_ref, out_ref):
@@ -468,6 +477,17 @@
     near = lax.dynamic_slice_in_dim(mine, group * count % height, count, 0)
     far = lax.ppermute(near, "dp", [(0, 1), (1, 0)])
     return jnp.where(lax.axis_index("dp") == group * count // height, near, far)
+
+
+def ctx_scatter(parts):
+    count = lax.axis_size("ctx")
+    at = lax.axis_index("ctx")
+    total = lax.dynamic_index_in_dim(parts, at, 0, keepdims=False).astype(jnp.float32)
+    for step in range(1, count):
+        sent = lax.dynamic_index_in_dim(parts, (at + step) % count, 0, keepdims=False)
+        came = lax.ppermute(sent, "ctx", [(source, (source + step) % count) for source in range(count)])
+        total += came.astype(jnp.float32)
+    return total.astype(parts.dtype)
 
 
 def dp_sum(mine):
@@ -545,7 +565,8 @@
     fc_came = dp_send(fc_own)
     proj_came = dp_send(proj_own)
 
-    cot_group = lax.all_gather(cotangent[0], "sp", axis=0, tiled=True)
+    cot_own, all_in = lax.optimization_barrier((cotangent[0], all_in))
+    cot_group = lax.all_gather(cot_own, "sp", axis=0, tiled=True)
     kept = jnp.transpose(kept_keys[0], (2, 0, 1, 3))
     out_full = dp_join(out_own, out_came)
     fc_part = dp_join(fc_own, fc_came)
@@ -594,7 +615,14 @@
         mlp_parts.reshape(ctx_count, -1, width), "ctx", scatter_dimension=0, tiled=False
     ).reshape(dp_count, -1, width)
     grad_norm_parts = contract_cols(grad_pre, fc_part).astype(bf16)
-    grad_norm_two = exchange_sum(grad_norm_parts.reshape(seg_count, rows, width), "sp")
+    norm_came = lax.all_to_all(
+        grad_norm_parts.reshape(seg_count, rows, width), "sp", split_axis=0, concat_axis=0, tiled=True
+    )
+    score_rows = score_slot[:, 0]
+    norm_came, norm_one, score_rows, key_score = lax.optimization_barrier(
+        (norm_came, norm_one, score_rows, key_score)
+    )
+    grad_norm_two = jnp.sum(norm_came.astype(f32), axis=0)
     _, second_pull = jax.vjp(layer_norm, mixed, gain_two)
     grad_mixed_norm, second_gain_grad = second_pull(grad_norm_two)
     grad_out = jnp.where(is_valid, cotangent[0], jnp.zeros_like(cotangent[0])).astype(f32)
@@ -605,20 +633,20 @@
     grad_wide = contract_cols(grad_branch, out_wide).astype(bf16)
     out_mine = jnp.dot(attended, grad_branch, preferred_element_type=f32).astype(bf16)
     grad_wide, out_mine = lax.optimization_barrier((grad_wide, out_mine))
-    out_sum = dp_sum(out_mine)
     gain_cols = jnp.stack([gain_one, second_gain_grad], axis=1)
     grad_wide, gain_cols = lax.optimization_barrier((grad_wide, gain_cols))
     query_grads, pair_grads, turned, query_turned, gates = attend_back(
         ctx_count, base, query_slot, grad_wide, pairs, prob
     )
-    turned, out_sum = lax.optimization_barrier((turned, out_sum))
     pair_mine = lax.psum_scatter(pair_grads, "ctx", scatter_dimension=0, tiled=False)
-    small = weight_grad(turned, query_turned, gates, score_slot[:, 0], norm_slot, norm_one, all_in, gain_cols)
-    late = jnp.concatenate(
-        [dp_scatter(small.reshape(dp_count, ctx_count, piece, width)), out_sum.reshape(ctx_count, -1, width)], axis=1
-    )
-    late_sum = exchange_sum(late, "ctx").astype(bf16)
-    gradients = jnp.concatenate([late_sum[:piece], dp_scatter(mlp_ctx), late_sum[piece:]], axis=0)
+    small = weight_grad(turned, query_turned, gates, score_rows, norm_slot, norm_one, all_in, gain_cols)
+    small, out_mine = lax.optimization_barrier((small, out_mine))
+    small_came = lax.all_to_all(
+        small.reshape(dp_count * ctx_count, piece, wide), ("dp", "ctx"), split_axis=0, concat_axis=0, tiled=True
+    )
+    small_own = jnp.pad(jnp.sum(small_came.astype(f32), axis=0).astype(bf16), ((0, 0), (0, width - wide)))
+    out_own = dp_sum(ctx_scatter(out_mine.reshape(ctx_count, -1, width)))
+    gradients = jnp.concatenate([small_own, dp_scatter(mlp_ctx), out_own], axis=0)
     pair_mine, gradients, active_late = lax.optimization_barrier((pair_mine, gradients, active))
     gathered = lax.all_gather(gradients, ("sp", "ctx"), axis=0, tiled=False).reshape(seg_count, ctx_count, -1, width)
     proj_piece = hidden // (seg_count * dp_count * ctx_count)
@@ -633,11 +661,16 @@
     grad_input_norm = first_pull(grad_norm_one)[0]
     input_grad = (grad_mixed + grad_input_norm).astype(bf16)[None]
 
-    qkv_grad, score_grad, fc_grad, proj_grad = unpack(gathered, heads, piece, proj_piece, dp_count, hidden)
+    qkv_grad, score_grad, fc_grad, proj_grad, *rest = unpack(
+        dp_at.astype(jnp.int32)[None], gathered, heads, piece, proj_piece, dp_count, hidden
+    )
     proj_grad = proj_grad.reshape(-1, width)
-    out_grad = lax.dynamic_slice_in_dim(
-        gathered[:, :, 2 * piece + proj_piece :].reshape(width, width), dp_at * weight_rows, weight_rows, 0
-    ).astype(f32)
+    if rest:
+        out_grad = rest[0].reshape(weight_rows, width)
+    else:
+        out_grad = lax.dynamic_slice_in_dim(
+            gathered[:, :, 2 * piece + proj_piece :].reshape(width, width), dp_at * weight_rows, weight_rows, 0
+        ).astype(f32)
     gains = jnp.sum(
         gathered[:, :, :piece, head_cols + heads : head_cols + heads + 2].astype(f32), axis=0
     ).reshape(weight_rows, 2)

time: 317 us -> 335 us (1.057)
  waiting for transfers between devices: 125 us -> 140 us
  starting transfers between devices: 25.1 us -> 31 us
  other arithmetic: 20.3 us -> 15.8 us
    ppermute x0 -> x3, waiting for transfers between devices: none -> 47.5 us  [ctx_scatter(): lax.ppermute(sent, 'ctx', [(source, (source + step) % count) for source i...]
    all_to_all x4 -> x2, waiting for transfers between devices: 57.2 us -> 25.6 us  [exchange_sum(): came = lax.all_to_all(parts, axis, split_axis=0, concat_axis=0, tiled=True)]
    all_to_all x0 -> x2, starting transfers between devices: none -> 9.33 us  [the longest x1 5.77 us: per_device(): lax.all_to_all(small.reshape(dp_count * ctx_count, piece, wide), ('dp', '...]
    ppermute x3, waiting for transfers between devices: 21 us -> 12.2 us  [dp_send(): return lax.ppermute(mine, 'dp', [(0, 1), (1, 0)])]
    all_to_all x4 -> x2, starting transfers between devices: 16 us -> 7.75 us  [exchange_sum(): came = lax.all_to_all(parts, axis, split_axis=0, concat_axis=0, tiled=True)]
    ppermute x2 -> x1, waiting for transfers between devices: 15.3 us -> 7.64 us  [dp_scatter(): other = lax.ppermute(sent, 'dp', [(0, 1), (1, 0)])]
    all_to_all x0 -> x2, waiting for transfers between devices: none -> 6.57 us  [the longest x1 6.57 us: per_device(): lax.all_to_all(grad_norm_parts.reshape(seg_count, rows, width), 'sp', spl...]
    ppermute x1, waiting for transfers between devices: 0.01 us -> 6.23 us  [per_device(): other_in = lax.ppermute(own_in, 'dp', [(0, 1), (1, 0)])]
  transfers between devices with their start and end apart: 15 -> 17, of which waited for: 8 -> 10; matrix products, arithmetic and copies ran while one was open for 13% -> 12% of each run, Pallas kernels for 18% -> 16%
where the time goes in v4:
time: 335 us; the launch traced here: 333 us
  waiting for transfers between devices  140 us (42%)
  Pallas kernels  63.6 us (19%)
  starting transfers between devices  31 us (9%)
  blocking collectives  29.2 us (9%)
  local copies, waits for them, and re-layouts  22.8 us (7%)
  matrix products  16 us (5%)
  other arithmetic  15.8 us (5%)
  between operations  14.9 us (4%)
    ppermute x3, waiting for transfers between devices, ctx_scatter(): lax.ppermute(sent, 'ctx', [(source, (source + step) % count) for source i...  47.5 us
    all_gather x1, waiting for transfers between devices, per_device(): lax.all_gather(gradients, ('sp', 'ctx'), axis=0, tiled=False)  32.8 us
    all_to_all x2, waiting for transfers between devices, exchange_sum(): came = lax.all_to_all(parts, axis, split_axis=0, concat_axis=0, tiled=True)  25.6 us
    pallas_call x1, Pallas kernels, attend(): pl.pallas_call(functools.partial(attend_kernel, parts, chunk), grid_spec=...  20.3 us
    pallas_call x1, Pallas kernels, attend_back(): pl.pallas_call(functools.partial(attend_back_kernel, parts, chunk), grid_...  15.1 us
    ppermute x3, waiting for transfers between devices, dp_send(): return lax.ppermute(mine, 'dp', [(0, 1), (1, 0)])  12.2 us
    all_gather x1, blocking collectives, per_device(): cot_group = lax.all_gather(cot_own, 'sp', axis=0, tiled=True)  11.7 us
    pallas_call x1, Pallas kernels, unpack(): pl.pallas_call(functools.partial(unpack_kernel, groups, heads, piece, par...  9.27 us
  transfers between devices with their start and end apart: 17, of which 10 were waited for; matrix products, arithmetic and copies ran while one was open for 12% of the time, Pallas kernels for 16%

profile of v4, /device:TPU:0, one launch (start us, length us, event | category | flops | bytes accessed | tf_op | source)
XLA Modules:
  0.0 333.1 jit_solution(6098764311070616781)
XLA Ops:
  12.5 2.1 arrange.1
  14.6 3.0 collective-permute-start
  21.2 2.0 pad_maximum_fusion.2
  23.2 6.2 %collective-permute-done = bf16[400,640]{1,0:T(8,128)(2,1)S(1)} collective-permute-done((bf16[400,640]{1,0:T(8,128)(2,1)}, bf16[400,640]{1,0:T(8,128)(2,1)S(1)}, u32[]{:S(2)}, u32[]{:S(2)}) %collective-permute-start) | collective-permute-done | bytes 512032 | tf_op jit(solution)/shard_map/ppermute | solution.py:544
  30.7 1.7 collective-permute-start.1
  32.9 1.7 collective-permute-start.3
  35.2 11.7 %all_gather.19 = bf16[512,768]{1,0:T(8,128)(2,1)} all-gather(bf16[128,768]{1,0:T(8,128)(2,1)S(1)} %bitcast.111), channel_id=1, replica_groups=mesh['dp'=2,'sp'=4,'ctx'=4] {'sp'}, dimensions={0}, use_global_device_ids=true | all-gather | bytes 983040 | tf_op jit(solution)/shard_map/all_gather | solution.py:569
  47.4 12.2 %collective-permute-done.2 = bf16[384,768]{1,0:T(8,128)(2,1)S(1)} collective-permute-done((bf16[384,768]{1,0:T(8,128)(2,1)S(1)}, bf16[384,768]{1,0:T(8,128)(2,1)S(1)}, u32[]{:S(2)}, u32[]{:S(2)}) %collective-permute-start.2) | collective-permute-done | bytes 589856 | tf_op jit(solution)/shard_map/ppermute | solution.py:451
  61.0 7.2 %project.1 = (bf16[2048,768]{1,0:T(8,128)(2,1)}, bf16[2048,384]{1,0:T(8,128)(2,1)}, bf16[2048,384]{1,0:T(8,128)(2,1)}, bf16[3,1,2048]{2,1,0:T(2,128)(2,1)}) custom-call(bf16[2048,768]{1,0:T(8,128)(2,1)} %bitcast.103, f32[1,768]{1,0:T(1,128)} %maximum_convert_fusion.gain_ref, bf16[768,640]{1,0:T(8,128)(2,1)} %pad_maximum_fusion.1.in_ref), custom_call_target="tpu_custom_call" | custom-call | tf_op jit(solution)/shard_map/project/pallas_call | solution.py:73
  68.3 20.3 %attend.1 = (bf16[3,64,512]{2,1,0:T(8,128)(2,1)}, bf16[3,4,128,2048]{3,2,1,0:T(8,128)(2,1)}) custom-call(s32[2]{0:T(128)} %pad_add_fusion.base_ref, s32[3,4,128,64]{3,2,1,0:T(8,128)} %bitcast.107, bf16[2048,384]{1,0:T(8,128)(2,1)} %get-tuple-element.61.refs_1_.refs_0_, bf16[2048,384]{1,0:T(8,128)(2,1)} %get-tuple-element.62.refs_2_, ...), custom_call_target="tpu_custom_call" | custom-call | tf_op jit(solution)/shard_map/attend/pallas_call | solution.py:205
  88.5 9.3 %all_gather.20 = bf16[768,512]{1,0:T(8,128)(2,1)S(1)} all-gather(bf16[192,512]{1,0:T(8,128)(2,1)} %bitcast.120), channel_id=1, replica_groups=mesh['dp'=2,'sp'=4,'ctx'=4] {'sp'}, dimensions={0}, use_global_device_ids=true | all-gather | bytes 983040 | tf_op jit(solution)/shard_map/all_gather | solution.py:592
  102.3 3.5 %fusion.6 = bf16[512,768]{1,0:T(8,128)(2,1)S(1)} fusion(f32[512,768]{1,0:T(8,128)S(1)} %get-tuple-element.165, bf16[512,768]{1,0:T(8,128)(2,1)S(1)} %copy-done.7, pred[512]{0:T(512)(128)(4,1)S(1)} %fusion.34, bf16[384,768]{1,0:T(8,128)(2,1)} %collective-permute-done.3, bf16[384,768]{1,0:T(8,128)(2,1)} %get-tuple-element.65, pred[]{:T(512)S(6)} %eq.15), kind=kOutput, calls=%fused_computation.9 | convolution fusion | flops 617545728 | bytes 4325889 | tf_op jit(solution)/shard_map/dot_general | solution.py:38
  110.7 2.8 convolution_convert_fusion.3
  113.6 3.6 %all-to-all-start = ((bf16[4,128,768]{2,1,0:T(8,128)(2,1)}), bf16[4,128,768]{2,1,0:T(8,128)(2,1)S(1)}, u32[]{:S(2)}, u32[]{:S(2)}) async-start(bf16[4,128,768]{2,1,0:T(8,128)(2,1)} %bitcast.117), calls=%async_computation | async-start | bytes 1572864 | tf_op jit(solution)/shard_map/all_to_all | solution.py:618
  120.1 2.1 constant_dynamic-slice_fusion.1
  122.2 6.6 %all-to-all-done = bf16[4,128,768]{2,1,0:T(8,128)(2,1)S(1)} async-done(((bf16[4,128,768]{2,1,0:T(8,128)(2,1)}), bf16[4,128,768]{2,1,0:T(8,128)(2,1)S(1)}, u32[]{:S(2)}, u32[]{:S(2)}) %all-to-all-start) | async-done | bytes 786464 | tf_op jit(solution)/shard_map/all_to_all | solution.py:618
  129.5 8.2 %all_gather.21 = bf16[512,768]{1,0:T(8,128)(2,1)S(1)} all-gather(bf16[128,768]{1,0:T(8,128)(2,1)S(1)} %fusion.18), channel_id=1, replica_groups=mesh['dp'=2,'sp'=4,'ctx'=4] {'sp'}, dimensions={0}, use_global_device_ids=true | all-gather | bytes 983040 | tf_op jit(solution)/shard_map/all_gather | solution.py:630
  140.2 15.1 %attend_back.1 = (bf16[512,384]{1,0:T(8,128)(2,1)}, bf16[4,528,384]{2,1,0:T(8,128)(2,1)}, bf16[3,128,2048]{2,1,0:T(8,128)(2,1)}, bf16[3,64,512]{2,1,0:T(8,128)(2,1)}, f32[3,8,2048]{2,1,0:T(8,128)}) custom-call(s32[2]{0:T(128)} %pad_add_fusion.base_ref, bf16[2048,384]{1,0:T(8,128)(2,1)} %get-tuple-element.61.refs_1_.refs_0_, ...), custom_call_target="tpu_custom_call" | custom-call | tf_op jit(solution)/shard_map/attend_back/pallas_call | solution.py:276
  156.2 6.3 %weight_grad.1 = bf16[768,640]{1,0:T(8,128)(2,1)} custom-call(bf16[3,128,2048]{2,1,0:T(8,128)(2,1)} %get-tuple-element.78.turned_ref, bf16[3,64,512]{2,1,0:T(8,128)(2,1)} %get-tuple-element.79.dq_ref, f32[3,8,2048]{2,1,0:T(8,128)} %get-tuple-element.80.gates_ref, bf16[3,2048]{1,0:T(4,128)(2,1)} %bitcast.126, bf16[2048,768]{1,0:T(8,128)(2,1)} %get-tuple-element.72.slot_ref, ...), custom_call_target="tpu_custom_call" | custom-call | tf_op jit(solution)/shard_map/weight_grad/pallas_call | solution.py:335
  162.5 5.8 %all-to-all-start.1 = ((bf16[8,96,640]{2,1,0:T(8,128)(2,1)}), bf16[8,96,640]{2,1,0:T(8,128)(2,1)S(1)}, u32[]{:S(2)}, u32[]{:S(2)}) async-start(bf16[8,96,640]{2,1,0:T(8,128)(2,1)} %bitcast.106), calls=%async_computation.2 | async-start | bytes 1966080 | tf_op jit(solution)/shard_map/all_to_all | solution.py:644
  170.0 3.7 %collective-permute-start.7 = (bf16[48,768]{1,0:T(8,128)(2,1)}, bf16[48,768]{1,0:T(8,128)(2,1)S(1)}, u32[]{:S(2)}, u32[]{:S(2)}) collective-permute-start(bf16[48,768]{1,0:T(8,128)(2,1)} %get-tuple-element.156), channel_id=1, source_target_pairs={{0,3},{1,0},{2,1},{3,2},{4,7},{5,4},{6,5},{7,6},{8,11},{9,8},{10,9... | collective-permute-start | bytes 221192 | tf_op jit(solution)/shard_map/ppermute | solution.py:488
  174.9 29.6 %collective-permute-done.7 = bf16[48,768]{1,0:T(8,128)(2,1)S(1)} collective-permute-done((bf16[48,768]{1,0:T(8,128)(2,1)}, bf16[48,768]{1,0:T(8,128)(2,1)S(1)}, u32[]{:S(2)}, u32[]{:S(2)}) %collective-permute-start.7) | collective-permute-done | bytes 73760 | tf_op jit(solution)/shard_map/ppermute | solution.py:488
  204.5 17.9 %collective-permute-done.6 = bf16[48,768]{1,0:T(8,128)(2,1)S(1)} collective-permute-done((bf16[48,768]{1,0:T(8,128)(2,1)S(1)}, bf16[48,768]{1,0:T(8,128)(2,1)S(1)}, u32[]{:S(2)}, u32[]{:S(2)}) %collective-permute-start.6) | collective-permute-done | bytes 73760 | tf_op jit(solution)/shard_map/ppermute | solution.py:488
  228.0 7.6 %collective-permute-done.4 = bf16[192,768]{1,0:T(8,128)(2,1)} collective-permute-done((bf16[192,768]{1,0:T(8,128)(2,1)}, bf16[192,768]{1,0:T(8,128)(2,1)}, u32[]{:S(2)}, u32[]{:S(2)}) %collective-permute-start.4) | collective-permute-done | bytes 294944 | tf_op jit(solution)/shard_map/ppermute | solution.py:468
  237.7 3.3 finish.1
  241.0 3.5 %all-to-all-start.3 = ((bf16[4,128,768]{2,1,0:T(8,128)(2,1)}), bf16[4,128,768]{2,1,0:T(8,128)(2,1)S(1)}, u32[]{:S(2)}, u32[]{:S(2)}) async-start(bf16[4,128,768]{2,1,0:T(8,128)(2,1)} %bitcast.108), calls=%async_computation.5 | async-start | bytes 1572864 | tf_op jit(solution)/shard_map/all_to_all | solution.py:501
  244.5 3.5 %convolution_convert_fusion.2 = bf16[512,768]{1,0:T(8,128)(2,1)} fusion(bf16[512,768]{1,0:T(8,128)(2,1)} %copy-done.18, bf16[384,768]{1,0:T(8,128)(2,1)} %collective-permute-done.3, bf16[384,768]{1,0:T(8,128)(2,1)} %get-tuple-element.65, pred[]{:T(512)S(6)} %eq.15), kind=kOutput, calls=%fused_computation.19 | convolution fusion | flops 609681408 | bytes 2752513 | tf_op jit(solution)/shard_map/dot_general | solution.py:656
  248.1 11.7 %all-to-all-done.3 = bf16[4,128,768]{2,1,0:T(8,128)(2,1)S(1)} async-done(((bf16[4,128,768]{2,1,0:T(8,128)(2,1)}), bf16[4,128,768]{2,1,0:T(8,128)(2,1)S(1)}, u32[]{:S(2)}, u32[]{:S(2)}) %all-to-all-start.3) | async-done | bytes 786464 | tf_op jit(solution)/shard_map/all_to_all | solution.py:501
  259.7 4.2 %all-to-all-start.2 = ((bf16[4,128,768]{2,1,0:T(8,128)(2,1)}), bf16[4,128,768]{2,1,0:T(8,128)(2,1)}, u32[]{:S(2)}, u32[]{:S(2)}) async-start(bf16[4,128,768]{2,1,0:T(8,128)(2,1)} %bitcast.118), calls=%async_computation.4 | async-start | bytes 1572864 | tf_op jit(solution)/shard_map/all_to_all | solution.py:501
  264.6 13.9 %all-to-all-done.2 = bf16[4,128,768]{2,1,0:T(8,128)(2,1)} async-done(((bf16[4,128,768]{2,1,0:T(8,128)(2,1)}), bf16[4,128,768]{2,1,0:T(8,128)(2,1)}, u32[]{:S(2)}, u32[]{:S(2)}) %all-to-all-start.2) | async-done | bytes 786464 | tf_op jit(solution)/shard_map/all_to_all | solution.py:501
  280.8 32.8 %all-gather.7.cloned.1.call-done = bf16[5376,768]{1,0:T(8,128)(2,1)} async-done(((bf16[336,768]{1,0:T(8,128)(2,1)}), bf16[5376,768]{1,0:T(8,128)(2,1)}) %all-gather.7.cloned.1.call-update) | async-done | bytes 8257552 | tf_op jit(solution)/shard_map/all_gather | solution.py:651
  315.7 9.3 %unpack.1 = (f32[384,2304]{1,0:T(8,128)}, f32[384,12]{1,0:T(8,128)}, f32[384,3072]{1,0:T(8,128)}, f32[4,4,96,768]{3,2,1,0:T(8,128)}, f32[2,4,48,768]{3,2,1,0:T(8,128)}) custom-call(s32[1]{0:T(128)} %bitcast.38.dp_ref, bf16[4,4,336,768]{3,2,1,0:T(8,128)(2,1)} %bitcast.102), custom_call_target="tpu_custom_call" | custom-call | tf_op jit(solution)/shard_map/unpack/pallas_call | solution.py:412
  (132 shorter events, 45.8 us)
Async XLA Ops:
  7.2 4.3 %copy-start = (bf16[384,2304]{1,0:T(8,128)(2,1)S(1)}, bf16[384,2304]{1,0:T(8,128)(2,1)}, u32[]{:S(2)}) copy-start(bf16[384,2304]{1,0:T(8,128)(2,1)} %param.16) | copy-start | bytes 5308420
  7.2 10.3 %copy-start.11 = (s32[1,4,128,3,64]{2,4,3,1,0:T(8,128)S(1)}, s32[1,4,128,3,64]{2,4,3,1,0:T(8,128)}, u32[]{:S(2)}) copy-start(s32[1,4,128,3,64]{2,4,3,1,0:T(8,128)} %param.14) | copy-start | bytes 1179652
  7.2 53.8 %all-gather.5.cloned.1.call-start = ((), (), s32[]{:S(2)}) async-start(), calls=%async_computation.8 | async-start | bytes 3342336 | tf_op jit(solution)/shard_map/all_gather | solution.py:550
  7.9 216.9 %reduce-scatter.5.cloned.1.call-start = ((), (), s32[]{:S(2)}) async-start(), calls=%async_computation.7 | async-start | bytes 2949120 | tf_op jit(solution)/shard_map/reduce_scatter | solution.py:614
  14.6 14.8 %collective-permute-start = (bf16[400,640]{1,0:T(8,128)(2,1)}, bf16[400,640]{1,0:T(8,128)(2,1)S(1)}, u32[]{:S(2)}, u32[]{:S(2)}) collective-permute-start(bf16[400,640]{1,0:T(8,128)(2,1)} %arrange.1), channel_id=1, source_target_pairs={{0,16},{16,0},{1,17},{17,1},{2,18},{18,2},{3,19},{19,3},{4,20},{20... | collective-permute-start | bytes 1536008 | tf_op jit(solution)/shard_map/ppermute | solution.py:544
  20.0 9.4 %copy-start.3 = (bf16[400,640]{1,0:T(8,128)(2,1)S(1)}, bf16[400,640]{1,0:T(8,128)(2,1)}, u32[]{:S(2)}) copy-start(bf16[400,640]{1,0:T(8,128)(2,1)} %arrange.1) | copy-start | bytes 1536004
  29.6 5.6 %copy-start.5 = (bf16[1,128,768]{2,1,0:T(8,128)(2,1)S(1)}, bf16[1,128,768]{2,1,0:T(8,128)(2,1)}, u32[]{:S(2)}) copy-start(bf16[1,128,768]{2,1,0:T(8,128)(2,1)} %param.12) | copy-start | bytes 589828
  30.7 16.2 %collective-permute-start.1 = (bf16[384,768]{1,0:T(8,128)(2,1)S(1)}, bf16[384,768]{1,0:T(8,128)(2,1)S(1)}, u32[]{:S(2)}, u32[]{:S(2)}) collective-permute-start(bf16[384,768]{1,0:T(8,128)(2,1)S(1)} %copy-done.9), channel_id=1, source_target_pairs={{0,16},{16,0},{1,17},{17,1},{2,18},{18,2},{3,19},{19,3},{4,20},{20... | collective-permute-start | bytes 1769480 | tf_op jit(solution)/shard_map/ppermute | solution.py:451
  32.5 27.1 %collective-permute-start.2 = (bf16[384,768]{1,0:T(8,128)(2,1)S(1)}, bf16[384,768]{1,0:T(8,128)(2,1)S(1)}, u32[]{:S(2)}, u32[]{:S(2)}) collective-permute-start(bf16[384,768]{1,0:T(8,128)(2,1)S(1)} %get-tuple-element.57), channel_id=1, source_target_pairs={{0,16},{16,0},{1,17},{17,1},{2,18},{18,2},{3,19},{19,3},{4,20},{20... | collective-permute-start | bytes 1769480 | tf_op jit(solution)/shard_map/ppermute | solution.py:451
  32.9 55.7 %collective-permute-start.3 = (bf16[384,768]{1,0:T(8,128)(2,1)}, bf16[384,768]{1,0:T(8,128)(2,1)}, u32[]{:S(2)}, u32[]{:S(2)}) collective-permute-start(bf16[384,768]{1,0:T(8,128)(2,1)} %get-tuple-element.65), channel_id=1, source_target_pairs={{0,16},{16,0},{1,17},{17,1},{2,18},{18,2},{3,19},{19,3},{4,20},{20... | collective-permute-start | bytes 1769480 | tf_op jit(solution)/shard_map/ppermute | solution.py:451
  47.4 51.6 %copy-start.4 = (bf16[768,768]{1,0:T(8,128)(2,1)}, bf16[768,768]{1,0:T(8,128)(2,1)S(1)}, u32[]{:S(2)}) copy-start(bf16[768,768]{1,0:T(8,128)(2,1)S(1)} %maximum_select_fusion) | copy-start | bytes 3538948
  99.9 1.3 copy-start.6
  102.2 4.6 %copy-start.18 = (bf16[512,768]{1,0:T(8,128)(2,1)}, bf16[512,768]{1,0:T(8,128)(2,1)S(1)}, u32[]{:S(2)}) copy-start(bf16[512,768]{1,0:T(8,128)(2,1)S(1)} %get-tuple-element.89) | copy-start | bytes 2359300
  109.4 19.9 %copy-start.13 = (pred[128]{0:T(512)(128)(4,1)}, pred[128]{0:T(512)(128)(4,1)S(1)}, u32[]{:S(2)}) copy-start(pred[128]{0:T(512)(128)(4,1)S(1)} %add_compare_fusion) | copy-start | bytes 388
  113.6 15.2 %all-to-all-start = ((bf16[4,128,768]{2,1,0:T(8,128)(2,1)}), bf16[4,128,768]{2,1,0:T(8,128)(2,1)S(1)}, u32[]{:S(2)}, u32[]{:S(2)}) async-start(bf16[4,128,768]{2,1,0:T(8,128)(2,1)} %bitcast.117), calls=%async_computation | async-start | bytes 1572864 | tf_op jit(solution)/shard_map/all_to_all | solution.py:618
  117.1 120.4 %reduce-scatter.3.cloned.1.call-start = ((), (), s32[]{:S(2)}) async-start(), calls=%async_computation.6 | async-start | bytes 2027520 | tf_op jit(solution)/shard_map/reduce_scatter | solution.py:641
  129.1 8.7 %copy-start.8 = (bf16[3,64,512]{2,1,0:T(8,128)(2,1)S(1)}, bf16[3,64,512]{2,1,0:T(8,128)(2,1)}, u32[]{:S(2)}) copy-start(bf16[3,64,512]{2,1,0:T(8,128)(2,1)} %get-tuple-element.66) | copy-start | bytes 589828
  129.3 9.5 %copy-start.10 = (bf16[3,128,768]{2,1,0:T(8,128)(2,1)S(1)}, bf16[3,128,768]{2,1,0:T(8,128)(2,1)}, u32[]{:S(2)}) copy-start(bf16[3,128,768]{2,1,0:T(8,128)(2,1)} %pad.13) | copy-start | bytes 1769476
  129.4 10.8 %copy-start.15 = (f32[128]{0:T(128)}, f32[128]{0:T(128)S(1)}, u32[]{:S(2)}) copy-start(f32[128]{0:T(128)S(1)} %negate_multiply_fusion.1) | copy-start | bytes 1540
  162.5 65.3 %all-to-all-start.1 = ((bf16[8,96,640]{2,1,0:T(8,128)(2,1)}), bf16[8,96,640]{2,1,0:T(8,128)(2,1)S(1)}, u32[]{:S(2)}, u32[]{:S(2)}) async-start(bf16[8,96,640]{2,1,0:T(8,128)(2,1)} %bitcast.106), calls=%async_computation.2 | async-start | bytes 1966080 | tf_op jit(solution)/shard_map/all_to_all | solution.py:644
  168.3 145.3 %all-gather.7.cloned.1.call-start = ((), (), s32[]{:S(2)}) async-start(), calls=%async_computation.9 | async-start | bytes 8773632 | tf_op jit(solution)/shard_map/all_gather | solution.py:651
  170.0 34.5 %collective-permute-start.7 = (bf16[48,768]{1,0:T(8,128)(2,1)}, bf16[48,768]{1,0:T(8,128)(2,1)S(1)}, u32[]{:S(2)}, u32[]{:S(2)}) collective-permute-start(bf16[48,768]{1,0:T(8,128)(2,1)} %get-tuple-element.156), channel_id=1, source_target_pairs={{0,3},{1,0},{2,1},{3,2},{4,7},{5,4},{6,5},{7,6},{8,11},{9,8},{10,9... | collective-permute-start | bytes 221192 | tf_op jit(solution)/shard_map/ppermute | solution.py:488
  173.7 48.6 %collective-permute-start.6 = (bf16[48,768]{1,0:T(8,128)(2,1)S(1)}, bf16[48,768]{1,0:T(8,128)(2,1)S(1)}, u32[]{:S(2)}, u32[]{:S(2)}) collective-permute-start(bf16[48,768]{1,0:T(8,128)(2,1)S(1)} %get-tuple-element.157), channel_id=1, source_target_pairs={{0,2},{1,3},{2,0},{3,1},{4,6},{5,7},{6,4},{7,5},{8,10},{9,11},{10,... | collective-permute-start | bytes 221192 | tf_op jit(solution)/shard_map/ppermute | solution.py:488
  173.7 48.6 %collective-permute-start.5 = (bf16[48,768]{1,0:T(8,128)(2,1)S(1)}, bf16[48,768]{1,0:T(8,128)(2,1)}, u32[]{:S(2)}, u32[]{:S(2)}) collective-permute-start(bf16[48,768]{1,0:T(8,128)(2,1)S(1)} %get-tuple-element.155), channel_id=1, source_target_pairs={{0,1},{1,2},{2,3},{3,0},{4,5},{5,6},{6,7},{7,4},{8,9},{9,10},{10,1... | collective-permute-start | bytes 221192 | tf_op jit(solution)/shard_map/ppermute | solution.py:488
  223.3 4.4 %collective-permute-start.8 = (bf16[48,768]{1,0:T(8,128)(2,1)S(1)}, bf16[48,768]{1,0:T(8,128)(2,1)S(1)}, u32[]{:S(2)}, u32[]{:S(2)}) collective-permute-start(bf16[48,768]{1,0:T(8,128)(2,1)S(1)} %fusion.23), channel_id=1, source_target_pairs={{0,16},{16,0},{1,17},{17,1},{2,18},{18,2},{3,19},{19,3},{4,20},{20... | collective-permute-start | bytes 221192 | tf_op jit(solution)/shard_map/ppermute | solution.py:496
  226.6 9.0 %collective-permute-start.4 = (bf16[192,768]{1,0:T(8,128)(2,1)}, bf16[192,768]{1,0:T(8,128)(2,1)}, u32[]{:S(2)}, u32[]{:S(2)}) collective-permute-start(bf16[192,768]{1,0:T(8,128)(2,1)} %dynamic-slice_bitcast_fusion), channel_id=1, source_target_pairs={{0,16},{16,0},{1,17},{17,1},{2,18},{18,2},{3,19},{19,3},{4,20},{20... | collective-permute-start | bytes 884744 | tf_op jit(solution)/shard_map/ppermute | solution.py:468
  227.8 9.8 %copy-start.2 = (bf16[1,128,768]{2,1,0:T(8,128)(2,1)S(1)}, bf16[1,128,768]{2,1,0:T(8,128)(2,1)}, u32[]{:S(2)}) copy-start(bf16[1,128,768]{2,1,0:T(8,128)(2,1)} %param.11) | copy-start | bytes 589828
  241.0 18.8 %all-to-all-start.3 = ((bf16[4,128,768]{2,1,0:T(8,128)(2,1)}), bf16[4,128,768]{2,1,0:T(8,128)(2,1)S(1)}, u32[]{:S(2)}, u32[]{:S(2)}) async-start(bf16[4,128,768]{2,1,0:T(8,128)(2,1)} %bitcast.108), calls=%async_computation.5 | async-start | bytes 1572864 | tf_op jit(solution)/shard_map/all_to_all | solution.py:501
  259.7 18.7 %all-to-all-start.2 = ((bf16[4,128,768]{2,1,0:T(8,128)(2,1)}), bf16[4,128,768]{2,1,0:T(8,128)(2,1)}, u32[]{:S(2)}, u32[]{:S(2)}) async-start(bf16[4,128,768]{2,1,0:T(8,128)(2,1)} %bitcast.118), calls=%async_computation.4 | async-start | bytes 1572864 | tf_op jit(solution)/shard_map/all_to_all | solution.py:501
  264.0 15.8 %copy-start.14 = (pred[128]{0:T(512)(128)(4,1)S(1)}, pred[128]{0:T(512)(128)(4,1)}, u32[]{:S(2)}) copy-start(pred[128]{0:T(512)(128)(4,1)} %copy-done.13) | copy-start | bytes 388
  264.0 15.8 %copy-start.16 = (f32[128]{0:T(128)S(1)}, f32[128]{0:T(128)}, u32[]{:S(2)}) copy-start(f32[128]{0:T(128)} %copy-done.15) | copy-start | bytes 1540
  315.7 10.9 %copy-start.1 = (bf16[384,2304]{1,0:T(8,128)(2,1)S(1)}, bf16[384,2304]{1,0:T(8,128)(2,1)}, u32[]{:S(2)}) copy-start(bf16[384,2304]{1,0:T(8,128)(2,1)} %param.16) | copy-start | bytes 5308420
  (4 other events, 4.0 us)
Sparse Core Ops, SparseCore 0:
  10.3 49.9 all-gather.4
  109.5 47.9 reduce-scatter.4
  160.5 56.2 reduce-scatter.2
  237.7 75.8 all-gather.6

commit v5 on v4

--- a/solution.py
+++ b/solution.py
@@ -382,18 +382,34 @@
             out_ref[at] = all_ref[dp_ref[0] * mine + at, :, 2 * piece + proj_ref.shape[2] :, :].astype(f32)
     for step in range(all_ref.shape[1]):
         rows = slice(step * piece, (step + 1) * piece)
+        scores, gains = [], None
         for at in range(groups):
             values = all_ref[at, step, :piece, :].astype(f32)
             for head in range(heads):
                 start = (at * heads + head) * 3 * HD
                 qkv_ref[rows, start : start + HD] = values[:, keys + head * HD : keys + (head + 1) * HD]
                 qkv_ref[rows, start + HD : start + 3 * HD] = values[:, head * 2 * HD : (head + 1) * 2 * HD]
-            score_ref[rows, at * heads : (at + 1) * heads] = values[:, keys + heads * HD : keys + heads * HD + heads]
+            scores.append(values[:, keys + heads * HD : keys + heads * HD + heads])
+            gain = values[:, keys + heads * HD + heads : keys + heads * HD + heads + 2]
+            gains = gain if gains is None else gains + gain
             values = all_ref[at, step, piece : 2 * piece, :].astype(f32)
             for part in range(parts):
                 start = (part * groups + at) * part_cols
                 fc_ref[rows, start : start + part_cols] = values[:, part * part_cols : (part + 1) * part_cols]
             proj_ref[at, step] = all_ref[at, step, 2 * piece : 2 * piece + proj_ref.shape[2], :].astype(f32)
+        narrow = jnp.concatenate(
+            scores + [gains, jnp.zeros((piece, LANES - groups * heads - 2), f32)], axis=1
+        )
+        turned = jnp.transpose(jnp.concatenate([narrow, jnp.zeros((LANES - piece, LANES), f32)], axis=0))
+
+        def store(index):
+            score_ref[:, index * piece : (index + 1) * piece] = turned[: score_ref.shape[0], :piece]
+
+        if all_ref.shape[1] > 1:
+            store(step)
+        else:
+            for index in range(score_ref.shape[1] // piece):
+                pl.when(pl.program_id(0) == index)(functools.partial(store, index))
 
 
 def unpack(at, gathered, heads, piece, proj_piece, parts, hidden):
@@ -401,7 +417,7 @@
     step = 1 if piece % 16 == 0 else count
     blocks = [
         ((count * piece, groups * heads * 3 * HD), (step * piece, groups * heads * 3 * HD), lambda c, d: (c, 0)),
-        ((count * piece, groups * heads), (step * piece, groups * heads), lambda c, d: (c, 0)),
+        ((PAD_ROWS, count * piece), (PAD_ROWS, count * piece), lambda c, d: (0, 0)),
         ((count * piece, hidden), (step * piece, hidden), lambda c, d: (c, 0)),
         ((groups, count, proj_piece, width), (groups, step, proj_piece, width), lambda c, d: (0, c, 0, 0)),
     ]
@@ -477,17 +493,6 @@
     near = lax.dynamic_slice_in_dim(mine, group * count % height, count, 0)
     far = lax.ppermute(near, "dp", [(0, 1), (1, 0)])
     return jnp.where(lax.axis_index("dp") == group * count // height, near, far)
-
-
-def ctx_scatter(parts):
-    count = lax.axis_size("ctx")
-    at = lax.axis_index("ctx")
-    total = lax.dynamic_index_in_dim(parts, at, 0, keepdims=False).astype(jnp.float32)
-    for step in range(1, count):
-        sent = lax.dynamic_index_in_dim(parts, (at + step) % count, 0, keepdims=False)
-        came = lax.ppermute(sent, "ctx", [(source, (source + step) % count) for source in range(count)])
-        total += came.astype(jnp.float32)
-    return total.astype(parts.dtype)
 
 
 def dp_sum(mine):
@@ -607,14 +612,14 @@
     grad_active = contract_cols(grad_out_group, proj_part)
     _, gelu_pull = jax.vjp(tanh_gelu, hidden_pre)
     grad_pre = gelu_pull(grad_active)[0].astype(bf16)
-    fc_parts = contract_rows(norm_two, grad_pre).astype(bf16).reshape(dp_count, ctx_count, piece, width)
+    grad_norm_parts = contract_cols(grad_pre, fc_part).astype(bf16)
+    grad_norm_parts, norm_late, active = lax.optimization_barrier((grad_norm_parts, norm_two, active))
+    fc_parts = contract_rows(norm_late, grad_pre).astype(bf16).reshape(dp_count, ctx_count, piece, width)
     proj_parts = contract_rows(active, grad_out_group).astype(bf16).reshape(dp_count, ctx_count, -1, width)
-    grad_pre, fc_parts, proj_parts = lax.optimization_barrier((grad_pre, fc_parts, proj_parts))
     mlp_parts = jnp.transpose(jnp.concatenate([fc_parts, proj_parts], axis=2), (1, 0, 2, 3))
     mlp_ctx = lax.psum_scatter(
         mlp_parts.reshape(ctx_count, -1, width), "ctx", scatter_dimension=0, tiled=False
     ).reshape(dp_count, -1, width)
-    grad_norm_parts = contract_cols(grad_pre, fc_part).astype(bf16)
     norm_came = lax.all_to_all(
         grad_norm_parts.reshape(seg_count, rows, width), "sp", split_axis=0, concat_axis=0, tiled=True
     )
@@ -633,6 +638,7 @@
     grad_wide = contract_cols(grad_branch, out_wide).astype(bf16)
     out_mine = jnp.dot(attended, grad_branch, preferred_element_type=f32).astype(bf16)
     grad_wide, out_mine = lax.optimization_barrier((grad_wide, out_mine))
+    out_sum = dp_sum(out_mine)
     gain_cols = jnp.stack([gain_one, second_gain_grad], axis=1)
     grad_wide, gain_cols = lax.optimization_barrier((grad_wide, gain_cols))
     query_grads, pair_grads, turned, query_turned, gates = attend_back(
@@ -640,13 +646,12 @@
     )
     pair_mine = lax.psum_scatter(pair_grads, "ctx", scatter_dimension=0, tiled=False)
     small = weight_grad(turned, query_turned, gates, score_rows, norm_slot, norm_one, all_in, gain_cols)
-    small, out_mine = lax.optimization_barrier((small, out_mine))
-    small_came = lax.all_to_all(
-        small.reshape(dp_count * ctx_count, piece, wide), ("dp", "ctx"), split_axis=0, concat_axis=0, tiled=True
-    )
-    small_own = jnp.pad(jnp.sum(small_came.astype(f32), axis=0).astype(bf16), ((0, 0), (0, width - wide)))
-    out_own = dp_sum(ctx_scatter(out_mine.reshape(ctx_count, -1, width)))
-    gradients = jnp.concatenate([small_own, dp_scatter(mlp_ctx), out_own], axis=0)
+    small_dp = jnp.pad(
+        dp_scatter(small.reshape(dp_count, ctx_count, piece, wide)), ((0, 0), (0, 0), (0, width - wide))
+    )
+    late = jnp.concatenate([small_dp, out_sum.reshape(ctx_count, -1, width)], axis=1)
+    late_sum = exchange_sum(late, "ctx").astype(bf16)
+    gradients = jnp.concatenate([late_sum[:piece], dp_scatter(mlp_ctx), late_sum[piece:]], axis=0)
     pair_mine, gradients, active_late = lax.optimization_barrier((pair_mine, gradients, active))
     gathered = lax.all_gather(gradients, ("sp", "ctx"), axis=0, tiled=False).reshape(seg_count, ctx_count, -1, width)
     proj_piece = hidden // (seg_count * dp_count * ctx_count)
@@ -661,7 +666,7 @@
     grad_input_norm = first_pull(grad_norm_one)[0]
     input_grad = (grad_mixed + grad_input_norm).astype(bf16)[None]
 
-    qkv_grad, score_grad, fc_grad, proj_grad, *rest = unpack(
+    qkv_grad, turned_rows, fc_grad, proj_grad, *rest = unpack(
         dp_at.astype(jnp.int32)[None], gathered, heads, piece, proj_piece, dp_count, hidden
     )
     proj_grad = proj_grad.reshape(-1, width)
@@ -671,10 +676,8 @@
         out_grad = lax.dynamic_slice_in_dim(
             gathered[:, :, 2 * piece + proj_piece :].reshape(width, width), dp_at * weight_rows, weight_rows, 0
         ).astype(f32)
-    gains = jnp.sum(
-        gathered[:, :, :piece, head_cols + heads : head_cols + heads + 2].astype(f32), axis=0
-    ).reshape(weight_rows, 2)
-    return (output, input_grad, gains[:, 0], qkv_grad, score_grad, out_grad, gains[:, 1], fc_grad, proj_grad)
+    score_grad = turned_rows[:H].T
+    return (output, input_grad, turned_rows[H], qkv_grad, score_grad, out_grad, turned_rows[H + 1], fc_grad, proj_grad)
 
 
 def solution(mesh):

time: 335 us -> 313 us (0.934)
  waiting for transfers between devices: 140 us -> 122 us
  starting transfers between devices: 31 us -> 26.2 us
    ppermute x3 -> x0, waiting for transfers between devices: 47.5 us -> none  [ctx_scatter(): lax.ppermute(sent, 'ctx', [(source, (source + step) % count) for source i...]
    all_to_all x2 -> x3, waiting for transfers between devices: 25.6 us -> 53.1 us  [exchange_sum(): came = lax.all_to_all(parts, axis, split_axis=0, concat_axis=0, tiled=True)]
    all_to_all x1 -> x0, starting transfers between devices: 5.77 us -> none  [per_device(): lax.all_to_all(small.reshape(dp_count * ctx_count, piece, wide), ('dp', '...]
    all_to_all x2 -> x3, starting transfers between devices: 7.75 us -> 13.2 us  [exchange_sum(): came = lax.all_to_all(parts, axis, split_axis=0, concat_axis=0, tiled=True)]
    ppermute x3 -> x0, starting transfers between devices: 4.85 us -> none  [ctx_scatter(): lax.ppermute(sent, 'ctx', [(source, (source + step) % count) for source i...]
    ppermute x1 -> x2, waiting for transfers between devices: 7.64 us -> 12 us  [dp_scatter(): other = lax.ppermute(sent, 'dp', [(0, 1), (1, 0)])]
  transfers between devices with their start and end apart: 17 -> 15, of which waited for: 10 -> 8; matrix products, arithmetic and copies ran while one was open for 12% -> 12% of each run, Pallas kernels for 16% -> 17%
where the time goes in v5:
time: 313 us; the launch traced here: 312 us
  waiting for transfers between devices  122 us (39%)
  Pallas kernels  63.6 us (20%)
  blocking collectives  29.6 us (9%)
  starting transfers between devices  26.2 us (8%)
  local copies, waits for them, and re-layouts  23.3 us (7%)
  other arithmetic  17.9 us (6%)
  between operations  14.9 us (5%)
  matrix products  14 us (4%)
    all_to_all x3, waiting for transfers between devices, exchange_sum(): came = lax.all_to_all(parts, axis, split_axis=0, concat_axis=0, tiled=True)  53.1 us
    all_gather x1, waiting for transfers between devices, per_device(): lax.all_gather(gradients, ('sp', 'ctx'), axis=0, tiled=False)  30.7 us
    pallas_call x1, Pallas kernels, attend(): pl.pallas_call(functools.partial(attend_kernel, parts, chunk), grid_spec=...  20.3 us
    pallas_call x1, Pallas kernels, attend_back(): pl.pallas_call(functools.partial(attend_back_kernel, parts, chunk), grid_...  15.1 us
    all_to_all x3, starting transfers between devices, exchange_sum(): came = lax.all_to_all(parts, axis, split_axis=0, concat_axis=0, tiled=True)  13.2 us
    all_gather x1, blocking collectives, per_device(): cot_group = lax.all_gather(cot_own, 'sp', axis=0, tiled=True)  12.2 us
    ppermute x2, waiting for transfers between devices, dp_scatter(): other = lax.ppermute(sent, 'dp', [(0, 1), (1, 0)])  12 us
    ppermute x3, waiting for transfers between devices, dp_send(): return lax.ppermute(mine, 'dp', [(0, 1), (1, 0)])  11.2 us
  transfers between devices with their start and end apart: 15, of which 8 were waited for; matrix products, arithmetic and copies ran while one was open for 12% of the time, Pallas kernels for 17%

profile of v5, /device:TPU:0, one launch (start us, length us, event | category | flops | bytes accessed | tf_op | source)
XLA Modules:
  0.0 311.8 jit_solution(13274653819377659087)
XLA Ops:
  12.5 2.1 arrange.1
  14.6 3.0 collective-permute-start
  22.9 6.5 %collective-permute-done = bf16[400,640]{1,0:T(8,128)(2,1)S(1)} collective-permute-done((bf16[400,640]{1,0:T(8,128)(2,1)}, bf16[400,640]{1,0:T(8,128)(2,1)S(1)}, u32[]{:S(2)}, u32[]{:S(2)}) %collective-permute-start) | collective-permute-done | bytes 512032 | tf_op jit(solution)/shard_map/ppermute | solution.py:549
  30.7 1.7 collective-permute-start.1
  33.3 1.7 collective-permute-start.3
  35.7 12.2 %all_gather.19 = bf16[512,768]{1,0:T(8,128)(2,1)} all-gather(bf16[128,768]{1,0:T(8,128)(2,1)S(1)} %bitcast.109), channel_id=1, replica_groups=mesh['dp'=2,'sp'=4,'ctx'=4] {'sp'}, dimensions={0}, use_global_device_ids=true | all-gather | bytes 983040 | tf_op jit(solution)/shard_map/all_gather | solution.py:574
  48.3 11.2 %collective-permute-done.2 = bf16[384,768]{1,0:T(8,128)(2,1)S(1)} collective-permute-done((bf16[384,768]{1,0:T(8,128)(2,1)S(1)}, bf16[384,768]{1,0:T(8,128)(2,1)S(1)}, u32[]{:S(2)}, u32[]{:S(2)}) %collective-permute-start.2) | collective-permute-done | bytes 589856 | tf_op jit(solution)/shard_map/ppermute | solution.py:467
  61.0 7.3 %project.1 = (bf16[2048,768]{1,0:T(8,128)(2,1)}, bf16[2048,384]{1,0:T(8,128)(2,1)}, bf16[2048,384]{1,0:T(8,128)(2,1)}, bf16[3,1,2048]{2,1,0:T(2,128)(2,1)}) custom-call(bf16[2048,768]{1,0:T(8,128)(2,1)} %bitcast.102, f32[1,768]{1,0:T(1,128)} %maximum_convert_fusion.gain_ref, bf16[768,640]{1,0:T(8,128)(2,1)} %pad_maximum_fusion.1.in_ref), custom_call_target="tpu_custom_call" | custom-call | tf_op jit(solution)/shard_map/project/pallas_call | solution.py:73
  68.3 20.3 %attend.1 = (bf16[3,64,512]{2,1,0:T(8,128)(2,1)}, bf16[3,4,128,2048]{3,2,1,0:T(8,128)(2,1)}) custom-call(s32[2]{0:T(128)} %pad_add_fusion.base_ref, s32[3,4,128,64]{3,2,1,0:T(8,128)} %bitcast.106, bf16[2048,384]{1,0:T(8,128)(2,1)} %get-tuple-element.59.refs_1_.refs_0_, bf16[2048,384]{1,0:T(8,128)(2,1)} %get-tuple-element.60.refs_2_, ...), custom_call_target="tpu_custom_call" | custom-call | tf_op jit(solution)/shard_map/attend/pallas_call | solution.py:205
  88.6 9.3 %all_gather.20 = bf16[768,512]{1,0:T(8,128)(2,1)S(1)} all-gather(bf16[192,512]{1,0:T(8,128)(2,1)} %bitcast.115), channel_id=1, replica_groups=mesh['dp'=2,'sp'=4,'ctx'=4] {'sp'}, dimensions={0}, use_global_device_ids=true | all-gather | bytes 983040 | tf_op jit(solution)/shard_map/all_gather | solution.py:597
  102.6 3.0 fusion.7
  105.7 1.7 convolution_convert_fusion.3
  109.3 1.6 copy.46
  112.9 3.5 %all-to-all-start = ((bf16[4,128,768]{2,1,0:T(8,128)(2,1)}), bf16[4,128,768]{2,1,0:T(8,128)(2,1)S(1)}, u32[]{:S(2)}, u32[]{:S(2)}) async-start(bf16[4,128,768]{2,1,0:T(8,128)(2,1)} %bitcast.10), calls=%async_computation | async-start | bytes 1572864 | tf_op jit(solution)/shard_map/all_to_all | solution.py:623
  117.9 2.1 constant_dynamic-slice_fusion.1
  120.0 8.0 %all-to-all-done = bf16[4,128,768]{2,1,0:T(8,128)(2,1)S(1)} async-done(((bf16[4,128,768]{2,1,0:T(8,128)(2,1)}), bf16[4,128,768]{2,1,0:T(8,128)(2,1)S(1)}, u32[]{:S(2)}, u32[]{:S(2)}) %all-to-all-start) | async-done | bytes 786464 | tf_op jit(solution)/shard_map/all_to_all | solution.py:623
  128.8 8.2 %all_gather.21 = bf16[512,768]{1,0:T(8,128)(2,1)S(1)} all-gather(bf16[128,768]{1,0:T(8,128)(2,1)S(1)} %fusion.18), channel_id=1, replica_groups=mesh['dp'=2,'sp'=4,'ctx'=4] {'sp'}, dimensions={0}, use_global_device_ids=true | all-gather | bytes 983040 | tf_op jit(solution)/shard_map/all_gather | solution.py:635
  139.4 15.1 %attend_back.1 = (bf16[512,384]{1,0:T(8,128)(2,1)}, bf16[4,528,384]{2,1,0:T(8,128)(2,1)}, bf16[3,128,2048]{2,1,0:T(8,128)(2,1)}, bf16[3,64,512]{2,1,0:T(8,128)(2,1)}, f32[3,8,2048]{2,1,0:T(8,128)}) custom-call(s32[2]{0:T(128)} %pad_add_fusion.base_ref, bf16[2048,384]{1,0:T(8,128)(2,1)} %get-tuple-element.59.refs_1_.refs_0_, ...), custom_call_target="tpu_custom_call" | custom-call | tf_op jit(solution)/shard_map/attend_back/pallas_call | solution.py:276
  157.0 6.3 %weight_grad.1 = bf16[768,640]{1,0:T(8,128)(2,1)} custom-call(bf16[3,128,2048]{2,1,0:T(8,128)(2,1)} %get-tuple-element.76.turned_ref, bf16[3,64,512]{2,1,0:T(8,128)(2,1)} %get-tuple-element.77.dq_ref, f32[3,8,2048]{2,1,0:T(8,128)} %get-tuple-element.78.gates_ref, bf16[3,2048]{1,0:T(4,128)(2,1)} %bitcast.121, bf16[2048,768]{1,0:T(8,128)(2,1)} %get-tuple-element.70.slot_ref, ...), custom_call_target="tpu_custom_call" | custom-call | tf_op jit(solution)/shard_map/weight_grad/pallas_call | solution.py:335
  163.4 1.9 dynamic-slice_bitcast_fusion
  166.8 12.0 %collective-permute-done.4 = bf16[4,96,640]{2,1,0:T(8,128)(2,1)} collective-permute-done((bf16[4,96,640]{2,1,0:T(8,128)(2,1)}, bf16[4,96,640]{2,1,0:T(8,128)(2,1)}, u32[]{:S(2)}, u32[]{:S(2)}) %collective-permute-start.4) | collective-permute-done | bytes 491552 | tf_op jit(solution)/shard_map/ppermute | solution.py:484
  180.9 4.8 %all-to-all-start.1 = ((bf16[4,144,768]{2,1,0:T(8,128)(2,1)}), bf16[4,144,768]{2,1,0:T(8,128)(2,1)S(1)}, u32[]{:S(2)}, u32[]{:S(2)}) async-start(bf16[4,144,768]{2,1,0:T(8,128)(2,1)} %fusion.9), calls=%async_computation.2 | async-start | bytes 1769472 | tf_op jit(solution)/shard_map/all_to_all | solution.py:506
  185.8 1.7 dynamic-slice_bitcast_fusion.1
  188.1 27.3 %all-to-all-done.1 = bf16[4,144,768]{2,1,0:T(8,128)(2,1)S(1)} async-done(((bf16[4,144,768]{2,1,0:T(8,128)(2,1)}), bf16[4,144,768]{2,1,0:T(8,128)(2,1)S(1)}, u32[]{:S(2)}, u32[]{:S(2)}) %all-to-all-start.1) | async-done | bytes 884768 | tf_op jit(solution)/shard_map/all_to_all | solution.py:506
  217.7 3.3 %finish.1 = bf16[512,768]{1,0:T(8,128)(2,1)} custom-call(bf16[528,384]{1,0:T(8,128)(2,1)} %bitcast.120, bf16[512,384]{1,0:T(8,128)(2,1)} %get-tuple-element.87.dq_ref, bf16[3,512]{1,0:T(4,128)(2,1)} %bitcast.122, bf16[768,640]{1,0:T(8,128)(2,1)} %pad_maximum_fusion.1.in_ref), custom_call_target="tpu_custom_call" | custom-call | tf_op jit(solution)/shard_map/finish/pallas_call | solution.py:368
  221.1 4.2 %all-to-all-start.3 = ((bf16[4,128,768]{2,1,0:T(8,128)(2,1)}), bf16[4,128,768]{2,1,0:T(8,128)(2,1)}, u32[]{:S(2)}, u32[]{:S(2)}) async-start(bf16[4,128,768]{2,1,0:T(8,128)(2,1)} %bitcast.107), calls=%async_computation.5 | async-start | bytes 1572864 | tf_op jit(solution)/shard_map/all_to_all | solution.py:506
  225.3 3.3 %convolution_convert_fusion.2 = bf16[512,768]{1,0:T(8,128)(2,1)} fusion(bf16[512,768]{1,0:T(8,128)(2,1)} %copy-done.17, bf16[384,768]{1,0:T(8,128)(2,1)} %collective-permute-done.3, bf16[384,768]{1,0:T(8,128)(2,1)S(1)} %copy-done.12, pred[]{:T(512)S(6)} %eq.5), kind=kOutput, calls=%fused_computation.21 | convolution fusion | flops 609681408 | bytes 2752513 | tf_op jit(solution)/shard_map/dot_general | solution.py:661
  228.6 13.0 %all-to-all-done.3 = bf16[4,128,768]{2,1,0:T(8,128)(2,1)} async-done(((bf16[4,128,768]{2,1,0:T(8,128)(2,1)}), bf16[4,128,768]{2,1,0:T(8,128)(2,1)}, u32[]{:S(2)}, u32[]{:S(2)}) %all-to-all-start.3) | async-done | bytes 786464 | tf_op jit(solution)/shard_map/all_to_all | solution.py:506
  241.6 4.2 %all-to-all-start.2 = ((bf16[4,128,768]{2,1,0:T(8,128)(2,1)}), bf16[4,128,768]{2,1,0:T(8,128)(2,1)}, u32[]{:S(2)}, u32[]{:S(2)}) async-start(bf16[4,128,768]{2,1,0:T(8,128)(2,1)} %bitcast.29), calls=%async_computation.4 | async-start | bytes 1572864 | tf_op jit(solution)/shard_map/all_to_all | solution.py:506
  247.5 12.8 %all-to-all-done.2 = bf16[4,128,768]{2,1,0:T(8,128)(2,1)} async-done(((bf16[4,128,768]{2,1,0:T(8,128)(2,1)}), bf16[4,128,768]{2,1,0:T(8,128)(2,1)}, u32[]{:S(2)}, u32[]{:S(2)}) %all-to-all-start.2) | async-done | bytes 786464 | tf_op jit(solution)/shard_map/all_to_all | solution.py:506
  262.6 30.7 %all-gather.7.cloned.1.call-done = bf16[5376,768]{1,0:T(8,128)(2,1)} async-done(((bf16[336,768]{1,0:T(8,128)(2,1)}), bf16[5376,768]{1,0:T(8,128)(2,1)}) %all-gather.7.cloned.1.call-update) | async-done | bytes 8257552 | tf_op jit(solution)/shard_map/all_gather | solution.py:656
  293.3 9.2 %unpack.1 = (f32[384,2304]{1,0:T(8,128)}, f32[16,384]{1,0:T(8,128)}, f32[384,3072]{1,0:T(8,128)}, f32[4,4,96,768]{3,2,1,0:T(8,128)}, f32[2,4,48,768]{3,2,1,0:T(8,128)}) custom-call(s32[1]{0:T(128)} %bitcast.34.dp_ref, bf16[4,4,336,768]{3,2,1,0:T(8,128)(2,1)} %bitcast.100), custom_call_target="tpu_custom_call" | custom-call | tf_op jit(solution)/shard_map/unpack/pallas_call | solution.py:428
  (129 shorter events, 43.6 us)
Async XLA Ops:
  7.2 4.3 %copy-start = (bf16[384,2304]{1,0:T(8,128)(2,1)S(1)}, bf16[384,2304]{1,0:T(8,128)(2,1)}, u32[]{:S(2)}) copy-start(bf16[384,2304]{1,0:T(8,128)(2,1)} %param.16) | copy-start | bytes 5308420
  7.2 11.0 %copy-start.13 = (s32[1,4,128,3,64]{2,4,3,1,0:T(8,128)S(1)}, s32[1,4,128,3,64]{2,4,3,1,0:T(8,128)}, u32[]{:S(2)}) copy-start(s32[1,4,128,3,64]{2,4,3,1,0:T(8,128)} %param.14) | copy-start | bytes 1179652
  7.2 53.8 %all-gather.5.cloned.1.call-start = ((), (), s32[]{:S(2)}) async-start(), calls=%async_computation.8 | async-start | bytes 3342336 | tf_op jit(solution)/shard_map/all_gather | solution.py:555
  7.9 177.8 %reduce-scatter.5.cloned.1.call-start = ((), (), s32[]{:S(2)}) async-start(), calls=%async_computation.7 | async-start | bytes 2949120 | tf_op jit(solution)/shard_map/reduce_scatter | solution.py:620
  14.6 14.8 %collective-permute-start = (bf16[400,640]{1,0:T(8,128)(2,1)}, bf16[400,640]{1,0:T(8,128)(2,1)S(1)}, u32[]{:S(2)}, u32[]{:S(2)}) collective-permute-start(bf16[400,640]{1,0:T(8,128)(2,1)} %arrange.1), channel_id=1, source_target_pairs={{0,16},{16,0},{1,17},{17,1},{2,18},{18,2},{3,19},{19,3},{4,20},{20... | collective-permute-start | bytes 1536008 | tf_op jit(solution)/shard_map/ppermute | solution.py:549
  20.5 8.9 %copy-start.4 = (bf16[400,640]{1,0:T(8,128)(2,1)S(1)}, bf16[400,640]{1,0:T(8,128)(2,1)}, u32[]{:S(2)}) copy-start(bf16[400,640]{1,0:T(8,128)(2,1)} %arrange.1) | copy-start | bytes 1536004
  22.9 79.7 %copy-start.11 = (bf16[384,768]{1,0:T(8,128)(2,1)}, bf16[384,768]{1,0:T(8,128)(2,1)S(1)}, u32[]{:S(2)}) copy-start(bf16[384,768]{1,0:T(8,128)(2,1)S(1)} %get-tuple-element.63) | copy-start | bytes 1769476
  29.6 1.2 copy-start.10
  29.6 6.1 %copy-start.6 = (bf16[1,128,768]{2,1,0:T(8,128)(2,1)S(1)}, bf16[1,128,768]{2,1,0:T(8,128)(2,1)}, u32[]{:S(2)}) copy-start(bf16[1,128,768]{2,1,0:T(8,128)(2,1)} %param.12) | copy-start | bytes 589828
  30.7 17.1 %collective-permute-start.1 = (bf16[384,768]{1,0:T(8,128)(2,1)S(1)}, bf16[384,768]{1,0:T(8,128)(2,1)S(1)}, u32[]{:S(2)}, u32[]{:S(2)}) collective-permute-start(bf16[384,768]{1,0:T(8,128)(2,1)S(1)} %copy-done.10), channel_id=1, source_target_pairs={{0,16},{16,0},{1,17},{17,1},{2,18},{18,2},{3,19},{19,3},{4,20},{20... | collective-permute-start | bytes 1769480 | tf_op jit(solution)/shard_map/ppermute | solution.py:467
  33.0 26.5 %collective-permute-start.2 = (bf16[384,768]{1,0:T(8,128)(2,1)S(1)}, bf16[384,768]{1,0:T(8,128)(2,1)S(1)}, u32[]{:S(2)}, u32[]{:S(2)}) collective-permute-start(bf16[384,768]{1,0:T(8,128)(2,1)S(1)} %get-tuple-element.55), channel_id=1, source_target_pairs={{0,16},{16,0},{1,17},{17,1},{2,18},{18,2},{3,19},{19,3},{4,20},{20... | collective-permute-start | bytes 1769480 | tf_op jit(solution)/shard_map/ppermute | solution.py:467
  33.3 55.2 %collective-permute-start.3 = (bf16[384,768]{1,0:T(8,128)(2,1)S(1)}, bf16[384,768]{1,0:T(8,128)(2,1)}, u32[]{:S(2)}, u32[]{:S(2)}) collective-permute-start(bf16[384,768]{1,0:T(8,128)(2,1)S(1)} %get-tuple-element.63), channel_id=1, source_target_pairs={{0,16},{16,0},{1,17},{17,1},{2,18},{18,2},{3,19},{19,3},{4,20},{20... | collective-permute-start | bytes 1769480 | tf_op jit(solution)/shard_map/ppermute | solution.py:467
  48.3 50.7 %copy-start.5 = (bf16[768,768]{1,0:T(8,128)(2,1)}, bf16[768,768]{1,0:T(8,128)(2,1)S(1)}, u32[]{:S(2)}) copy-start(bf16[768,768]{1,0:T(8,128)(2,1)S(1)} %maximum_select_fusion) | copy-start | bytes 3538948
  100.2 1.3 copy-start.7
  101.5 1.1 copy-start.8
  101.5 1.1 copy-start.16
  102.5 4.9 %copy-start.17 = (bf16[512,768]{1,0:T(8,128)(2,1)}, bf16[512,768]{1,0:T(8,128)(2,1)S(1)}, u32[]{:S(2)}) copy-start(bf16[512,768]{1,0:T(8,128)(2,1)S(1)} %get-tuple-element.85) | copy-start | bytes 2359300
  112.9 15.1 %all-to-all-start = ((bf16[4,128,768]{2,1,0:T(8,128)(2,1)}), bf16[4,128,768]{2,1,0:T(8,128)(2,1)S(1)}, u32[]{:S(2)}, u32[]{:S(2)}) async-start(bf16[4,128,768]{2,1,0:T(8,128)(2,1)} %bitcast.10), calls=%async_computation | async-start | bytes 1572864 | tf_op jit(solution)/shard_map/all_to_all | solution.py:623
  116.4 101.2 %reduce-scatter.3.cloned.1.call-start = ((), (), s32[]{:S(2)}) async-start(), calls=%async_computation.6 | async-start | bytes 2027520 | tf_op jit(solution)/shard_map/reduce_scatter | solution.py:647
  128.3 8.6 %copy-start.9 = (bf16[3,64,512]{2,1,0:T(8,128)(2,1)S(1)}, bf16[3,64,512]{2,1,0:T(8,128)(2,1)}, u32[]{:S(2)}) copy-start(bf16[3,64,512]{2,1,0:T(8,128)(2,1)} %get-tuple-element.64) | copy-start | bytes 589828
  154.5 11.3 %collective-permute-start.5 = (bf16[192,768]{1,0:T(8,128)(2,1)}, bf16[192,768]{1,0:T(8,128)(2,1)S(1)}, u32[]{:S(2)}, u32[]{:S(2)}) collective-permute-start(bf16[192,768]{1,0:T(8,128)(2,1)} %convolution_convert_fusion.5), channel_id=1, source_target_pairs={{0,16},{16,0},{1,17},{17,1},{2,18},{18,2},{3,19},{19,3},{4,20},{20... | collective-permute-start | bytes 884744 | tf_op jit(solution)/shard_map/ppermute | solution.py:501
  163.4 15.4 %copy-start.3 = (bf16[768,640]{1,0:T(8,128)(2,1)S(1)}, bf16[768,640]{1,0:T(8,128)(2,1)}, u32[]{:S(2)}) copy-start(bf16[768,640]{1,0:T(8,128)(2,1)} %weight_grad.1) | copy-start | bytes 2949124
  165.3 13.5 %collective-permute-start.4 = (bf16[4,96,640]{2,1,0:T(8,128)(2,1)}, bf16[4,96,640]{2,1,0:T(8,128)(2,1)}, u32[]{:S(2)}, u32[]{:S(2)}) collective-permute-start(bf16[4,96,640]{2,1,0:T(8,128)(2,1)} %dynamic-slice_bitcast_fusion), channel_id=1, source_target_pairs={{0,16},{16,0},{1,17},{17,1},{2,18},{18,2},{3,19},{19,3},{4,20},{20... | collective-permute-start | bytes 1474568 | tf_op jit(solution)/shard_map/ppermute | solution.py:484
  180.9 34.4 %all-to-all-start.1 = ((bf16[4,144,768]{2,1,0:T(8,128)(2,1)}), bf16[4,144,768]{2,1,0:T(8,128)(2,1)S(1)}, u32[]{:S(2)}, u32[]{:S(2)}) async-start(bf16[4,144,768]{2,1,0:T(8,128)(2,1)} %fusion.9), calls=%async_computation.2 | async-start | bytes 1769472 | tf_op jit(solution)/shard_map/all_to_all | solution.py:506
  185.8 107.6 %all-gather.7.cloned.1.call-start = ((), (), s32[]{:S(2)}) async-start(), calls=%async_computation.9 | async-start | bytes 8773632 | tf_op jit(solution)/shard_map/all_gather | solution.py:656
  187.5 28.1 %collective-permute-start.6 = (bf16[192,768]{1,0:T(8,128)(2,1)}, bf16[192,768]{1,0:T(8,128)(2,1)}, u32[]{:S(2)}, u32[]{:S(2)}) collective-permute-start(bf16[192,768]{1,0:T(8,128)(2,1)} %dynamic-slice_bitcast_fusion.1), channel_id=1, source_target_pairs={{0,16},{16,0},{1,17},{17,1},{2,18},{18,2},{3,19},{19,3},{4,20},{20... | collective-permute-start | bytes 884744 | tf_op jit(solution)/shard_map/ppermute | solution.py:484
  215.5 2.1 copy-start.2
  217.7 7.6 %copy-start.15 = (bf16[384]{0:T(512)(128)(2,1)S(1)}, bf16[384]{0:T(512)(128)(2,1)}, u32[]{:S(2)}) copy-start(bf16[384]{0:T(512)(128)(2,1)} %get-tuple-element.126) | copy-start | bytes 2308
  217.7 7.6 %copy-start.12 = (bf16[384,768]{1,0:T(8,128)(2,1)S(1)}, bf16[384,768]{1,0:T(8,128)(2,1)}, u32[]{:S(2)}) copy-start(bf16[384,768]{1,0:T(8,128)(2,1)} %copy-done.11) | copy-start | bytes 1769476
  221.1 20.5 %all-to-all-start.3 = ((bf16[4,128,768]{2,1,0:T(8,128)(2,1)}), bf16[4,128,768]{2,1,0:T(8,128)(2,1)}, u32[]{:S(2)}, u32[]{:S(2)}) async-start(bf16[4,128,768]{2,1,0:T(8,128)(2,1)} %bitcast.107), calls=%async_computation.5 | async-start | bytes 1572864 | tf_op jit(solution)/shard_map/all_to_all | solution.py:506
  241.6 18.7 %all-to-all-start.2 = ((bf16[4,128,768]{2,1,0:T(8,128)(2,1)}), bf16[4,128,768]{2,1,0:T(8,128)(2,1)}, u32[]{:S(2)}, u32[]{:S(2)}) async-start(bf16[4,128,768]{2,1,0:T(8,128)(2,1)} %bitcast.29), calls=%async_computation.4 | async-start | bytes 1572864 | tf_op jit(solution)/shard_map/all_to_all | solution.py:506
  293.3 11.9 %copy-start.1 = (bf16[384,2304]{1,0:T(8,128)(2,1)S(1)}, bf16[384,2304]{1,0:T(8,128)(2,1)}, u32[]{:S(2)}) copy-start(bf16[384,2304]{1,0:T(8,128)(2,1)} %param.16) | copy-start | bytes 5308420
  (1 other events, 0.7 us)
Sparse Core Ops, SparseCore 0:
  10.3 50.3 all-gather.4
  111.0 47.9 reduce-scatter.4
  161.9 42.7 reduce-scatter.2
  217.7 75.5 all-gather.6

commit v6 on v5

--- a/solution.py
+++ b/solution.py
@@ -638,7 +638,6 @@
     grad_wide = contract_cols(grad_branch, out_wide).astype(bf16)
     out_mine = jnp.dot(attended, grad_branch, preferred_element_type=f32).astype(bf16)
     grad_wide, out_mine = lax.optimization_barrier((grad_wide, out_mine))
-    out_sum = dp_sum(out_mine)
     gain_cols = jnp.stack([gain_one, second_gain_grad], axis=1)
     grad_wide, gain_cols = lax.optimization_barrier((grad_wide, gain_cols))
     query_grads, pair_grads, turned, query_turned, gates = attend_back(
@@ -646,12 +645,16 @@
     )
     pair_mine = lax.psum_scatter(pair_grads, "ctx", scatter_dimension=0, tiled=False)
     small = weight_grad(turned, query_turned, gates, score_rows, norm_slot, norm_one, all_in, gain_cols)
-    small_dp = jnp.pad(
-        dp_scatter(small.reshape(dp_count, ctx_count, piece, wide)), ((0, 0), (0, 0), (0, width - wide))
-    )
-    late = jnp.concatenate([small_dp, out_sum.reshape(ctx_count, -1, width)], axis=1)
-    late_sum = exchange_sum(late, "ctx").astype(bf16)
-    gradients = jnp.concatenate([late_sum[:piece], dp_scatter(mlp_ctx), late_sum[piece:]], axis=0)
+    small, out_mine = lax.optimization_barrier((small, out_mine))
+    out_came = lax.all_to_all(
+        out_mine.reshape(ctx_count, -1, width), "ctx", split_axis=0, concat_axis=0, tiled=True
+    )
+    small_dp, out_came = lax.optimization_barrier(
+        (dp_scatter(small.reshape(dp_count, ctx_count, piece, wide)), out_came)
+    )
+    small_own = jnp.pad(exchange_sum(small_dp, "ctx").astype(bf16), ((0, 0), (0, width - wide)))
+    out_own = dp_sum(jnp.sum(out_came.astype(f32), axis=0).astype(bf16))
+    gradients = jnp.concatenate([small_own, dp_scatter(mlp_ctx), out_own], axis=0)
     pair_mine, gradients, active_late = lax.optimization_barrier((pair_mine, gradients, active))
     gathered = lax.all_gather(gradients, ("sp", "ctx"), axis=0, tiled=False).reshape(seg_count, ctx_count, -1, width)
     proj_piece = hidden // (seg_count * dp_count * ctx_count)

time: 313 us -> 312 us (level)
  waiting for transfers between devices: 122 us -> 115 us
  starting transfers between devices: 26.2 us -> 30.9 us
    all_to_all x3, waiting for transfers between devices: 53.1 us -> 41.8 us  [exchange_sum(): came = lax.all_to_all(parts, axis, split_axis=0, concat_axis=0, tiled=True)]
    all_to_all x0 -> x1, waiting for transfers between devices: none -> 9.13 us  [per_device(): lax.all_to_all(out_mine.reshape(ctx_count, -1, width), 'ctx', split_axis=...]
    all_to_all x0 -> x1, starting transfers between devices: none -> 4.91 us  [per_device(): lax.all_to_all(out_mine.reshape(ctx_count, -1, width), 'ctx', split_axis=...]
    ppermute x2, waiting for transfers between devices: 12 us -> 7.4 us  [dp_scatter(): other = lax.ppermute(sent, 'dp', [(0, 1), (1, 0)])]
  transfers between devices with their start and end apart: 15 -> 16, of which waited for: 8 -> 10; matrix products, arithmetic and copies ran while one was open for 12% -> 13% of each run, Pallas kernels for 17% -> 18%
where the time goes in v6:
time: 312 us; the launch traced here: 310 us
  waiting for transfers between devices  115 us (37%)
  Pallas kernels  63.5 us (20%)
  starting transfers between devices  30.9 us (10%)
  blocking collectives  29.3 us (9%)
  local copies, waits for them, and re-layouts  23.5 us (8%)
  other arithmetic  17.8 us (6%)
  between operations  14.8 us (5%)
  matrix products  14.5 us (5%)
    all_to_all x3, waiting for transfers between devices, exchange_sum(): came = lax.all_to_all(parts, axis, split_axis=0, concat_axis=0, tiled=True)  41.8 us
    all_gather x1, waiting for transfers between devices, per_device(): lax.all_gather(gradients, ('sp', 'ctx'), axis=0, tiled=False)  30 us
    pallas_call x1, Pallas kernels, attend(): pl.pallas_call(functools.partial(attend_kernel, parts, chunk), grid_spec=...  20.3 us
    pallas_call x1, Pallas kernels, attend_back(): pl.pallas_call(functools.partial(attend_back_kernel, parts, chunk), grid_...  15.1 us
    ppermute x3, waiting for transfers between devices, dp_send(): return lax.ppermute(mine, 'dp', [(0, 1), (1, 0)])  12.2 us
    all_to_all x3, starting transfers between devices, exchange_sum(): came = lax.all_to_all(parts, axis, split_axis=0, concat_axis=0, tiled=True)  11.9 us
    all_gather x1, blocking collectives, per_device(): cot_group = lax.all_gather(cot_own, 'sp', axis=0, tiled=True)  11.7 us
    all_gather x1, blocking collectives, per_device(): attended_all = lax.all_gather(attended, 'sp', axis=0, tiled=True)  9.25 us
  transfers between devices with their start and end apart: 16, of which 10 were waited for; matrix products, arithmetic and copies ran while one was open for 13% of the time, Pallas kernels for 18%

profile of v6, /device:TPU:0, one launch (start us, length us, event | category | flops | bytes accessed | tf_op | source)
XLA Modules:
  0.0 309.7 jit_solution(8964690544685601954)
XLA Ops:
  12.5 2.1 arrange.1
  14.6 3.0 collective-permute-start
  21.1 2.0 pad_maximum_fusion.2
  23.1 6.2 %collective-permute-done = bf16[400,640]{1,0:T(8,128)(2,1)S(1)} collective-permute-done((bf16[400,640]{1,0:T(8,128)(2,1)}, bf16[400,640]{1,0:T(8,128)(2,1)S(1)}, u32[]{:S(2)}, u32[]{:S(2)}) %collective-permute-start) | collective-permute-done | bytes 512032 | tf_op jit(solution)/shard_map/ppermute | solution.py:549
  30.7 1.7 collective-permute-start.1
  35.2 11.7 %all_gather.19 = bf16[512,768]{1,0:T(8,128)(2,1)} all-gather(bf16[128,768]{1,0:T(8,128)(2,1)S(1)} %bitcast.109), channel_id=1, replica_groups=mesh['dp'=2,'sp'=4,'ctx'=4] {'sp'}, dimensions={0}, use_global_device_ids=true | all-gather | bytes 983040 | tf_op jit(solution)/shard_map/all_gather | solution.py:574
  47.4 12.2 %collective-permute-done.2 = bf16[384,768]{1,0:T(8,128)(2,1)S(1)} collective-permute-done((bf16[384,768]{1,0:T(8,128)(2,1)S(1)}, bf16[384,768]{1,0:T(8,128)(2,1)S(1)}, u32[]{:S(2)}, u32[]{:S(2)}) %collective-permute-start.2) | collective-permute-done | bytes 589856 | tf_op jit(solution)/shard_map/ppermute | solution.py:467
  61.0 7.2 %project.1 = (bf16[2048,768]{1,0:T(8,128)(2,1)}, bf16[2048,384]{1,0:T(8,128)(2,1)}, bf16[2048,384]{1,0:T(8,128)(2,1)}, bf16[3,1,2048]{2,1,0:T(2,128)(2,1)}) custom-call(bf16[2048,768]{1,0:T(8,128)(2,1)} %bitcast.102, f32[1,768]{1,0:T(1,128)} %maximum_convert_fusion.gain_ref, bf16[768,640]{1,0:T(8,128)(2,1)} %pad_maximum_fusion.1.in_ref), custom_call_target="tpu_custom_call" | custom-call | tf_op jit(solution)/shard_map/project/pallas_call | solution.py:73
  68.3 20.3 %attend.1 = (bf16[3,64,512]{2,1,0:T(8,128)(2,1)}, bf16[3,4,128,2048]{3,2,1,0:T(8,128)(2,1)}) custom-call(s32[2]{0:T(128)} %pad_add_fusion.base_ref, s32[3,4,128,64]{3,2,1,0:T(8,128)} %bitcast.106, bf16[2048,384]{1,0:T(8,128)(2,1)} %get-tuple-element.63.refs_1_.refs_0_, bf16[2048,384]{1,0:T(8,128)(2,1)} %get-tuple-element.64.refs_2_, ...), custom_call_target="tpu_custom_call" | custom-call | tf_op jit(solution)/shard_map/attend/pallas_call | solution.py:205
  88.5 9.2 %all_gather.20 = bf16[768,512]{1,0:T(8,128)(2,1)S(1)} all-gather(bf16[192,512]{1,0:T(8,128)(2,1)} %bitcast.116), channel_id=1, replica_groups=mesh['dp'=2,'sp'=4,'ctx'=4] {'sp'}, dimensions={0}, use_global_device_ids=true | all-gather | bytes 983040 | tf_op jit(solution)/shard_map/all_gather | solution.py:597
  102.6 3.4 %fusion.6 = bf16[512,768]{1,0:T(8,128)(2,1)S(1)} fusion(f32[512,768]{1,0:T(8,128)S(1)} %get-tuple-element.130, bf16[512,768]{1,0:T(8,128)(2,1)S(1)} %copy-done.8, pred[512]{0:T(512)(128)(4,1)S(1)} %fusion.32, bf16[384,768]{1,0:T(8,128)(2,1)} %collective-permute-done.3, bf16[384,768]{1,0:T(8,128)(2,1)} %get-tuple-element.67, pred[]{:T(512)S(6)} %eq.5), kind=kOutput, calls=%fused_computation.9 | convolution fusion | flops 617545728 | bytes 4325889 | tf_op jit(solution)/shard_map/dot_general | solution.py:38
  113.2 3.5 %all-to-all-start = ((bf16[4,128,768]{2,1,0:T(8,128)(2,1)}), bf16[4,128,768]{2,1,0:T(8,128)(2,1)S(1)}, u32[]{:S(2)}, u32[]{:S(2)}) async-start(bf16[4,128,768]{2,1,0:T(8,128)(2,1)} %bitcast.114), calls=%async_computation | async-start | bytes 1572864 | tf_op jit(solution)/shard_map/all_to_all | solution.py:623
  119.0 2.1 constant_dynamic-slice_fusion.1
  121.1 7.2 %all-to-all-done = bf16[4,128,768]{2,1,0:T(8,128)(2,1)S(1)} async-done(((bf16[4,128,768]{2,1,0:T(8,128)(2,1)}), bf16[4,128,768]{2,1,0:T(8,128)(2,1)S(1)}, u32[]{:S(2)}, u32[]{:S(2)}) %all-to-all-start) | async-done | bytes 786464 | tf_op jit(solution)/shard_map/all_to_all | solution.py:623
  129.1 8.4 %all_gather.21 = bf16[512,768]{1,0:T(8,128)(2,1)S(1)} all-gather(bf16[128,768]{1,0:T(8,128)(2,1)S(1)} %fusion.19), channel_id=1, replica_groups=mesh['dp'=2,'sp'=4,'ctx'=4] {'sp'}, dimensions={0}, use_global_device_ids=true | all-gather | bytes 983040 | tf_op jit(solution)/shard_map/all_gather | solution.py:635
  139.8 15.1 %attend_back.1 = (bf16[512,384]{1,0:T(8,128)(2,1)}, bf16[4,528,384]{2,1,0:T(8,128)(2,1)}, bf16[3,128,2048]{2,1,0:T(8,128)(2,1)}, bf16[3,64,512]{2,1,0:T(8,128)(2,1)}, f32[3,8,2048]{2,1,0:T(8,128)}) custom-call(s32[2]{0:T(128)} %pad_add_fusion.base_ref, bf16[2048,384]{1,0:T(8,128)(2,1)} %get-tuple-element.63.refs_1_.refs_0_, ...), custom_call_target="tpu_custom_call" | custom-call | tf_op jit(solution)/shard_map/attend_back/pallas_call | solution.py:276
  155.9 6.3 %weight_grad.1 = bf16[768,640]{1,0:T(8,128)(2,1)} custom-call(bf16[3,128,2048]{2,1,0:T(8,128)(2,1)} %get-tuple-element.80.turned_ref, bf16[3,64,512]{2,1,0:T(8,128)(2,1)} %get-tuple-element.81.dq_ref, f32[3,8,2048]{2,1,0:T(8,128)} %get-tuple-element.82.gates_ref, bf16[3,2048]{1,0:T(4,128)(2,1)} %bitcast.122, bf16[2048,768]{1,0:T(8,128)(2,1)} %get-tuple-element.74.slot_ref, ...), custom_call_target="tpu_custom_call" | custom-call | tf_op jit(solution)/shard_map/weight_grad/pallas_call | solution.py:335
  162.2 1.9 dynamic-slice_bitcast_fusion
  165.6 4.9 %all-to-all-start.1 = ((bf16[4,48,768]{2,1,0:T(8,128)(2,1)}), bf16[4,48,768]{2,1,0:T(8,128)(2,1)}, u32[]{:S(2)}, u32[]{:S(2)}) async-start(bf16[4,48,768]{2,1,0:T(8,128)(2,1)} %bitcast.110), calls=%async_computation.2 | async-start | bytes 589824 | tf_op jit(solution)/shard_map/all_to_all | solution.py:649
  170.5 7.4 %collective-permute-done.4 = bf16[4,96,640]{2,1,0:T(8,128)(2,1)} collective-permute-done((bf16[4,96,640]{2,1,0:T(8,128)(2,1)}, bf16[4,96,640]{2,1,0:T(8,128)(2,1)}, u32[]{:S(2)}, u32[]{:S(2)}) %collective-permute-start.4) | collective-permute-done | bytes 491552 | tf_op jit(solution)/shard_map/ppermute | solution.py:484
  177.9 1.9 fusion.8
  179.8 9.1 %all-to-all-done.1 = bf16[4,48,768]{2,1,0:T(8,128)(2,1)} async-done(((bf16[4,48,768]{2,1,0:T(8,128)(2,1)}), bf16[4,48,768]{2,1,0:T(8,128)(2,1)}, u32[]{:S(2)}, u32[]{:S(2)}) %all-to-all-start.1) | async-done | bytes 294944 | tf_op jit(solution)/shard_map/all_to_all | solution.py:649
  189.0 3.5 %all-to-all-start.2 = ((bf16[4,96,640]{2,1,0:T(8,128)(2,1)}), bf16[4,96,640]{2,1,0:T(8,128)(2,1)S(1)}, u32[]{:S(2)}, u32[]{:S(2)}) async-start(bf16[4,96,640]{2,1,0:T(8,128)(2,1)} %fusion.8), calls=%async_computation.3 | async-start | bytes 983040 | tf_op jit(solution)/shard_map/all_to_all | solution.py:506
  198.0 15.6 %all-to-all-done.2 = bf16[4,96,640]{2,1,0:T(8,128)(2,1)S(1)} async-done(((bf16[4,96,640]{2,1,0:T(8,128)(2,1)}), bf16[4,96,640]{2,1,0:T(8,128)(2,1)S(1)}, u32[]{:S(2)}, u32[]{:S(2)}) %all-to-all-start.2) | async-done | bytes 491552 | tf_op jit(solution)/shard_map/all_to_all | solution.py:506
  215.7 3.3 %finish.1 = bf16[512,768]{1,0:T(8,128)(2,1)} custom-call(bf16[528,384]{1,0:T(8,128)(2,1)} %bitcast.121, bf16[512,384]{1,0:T(8,128)(2,1)} %get-tuple-element.95.dq_ref, bf16[3,512]{1,0:T(4,128)(2,1)} %bitcast.123, bf16[768,640]{1,0:T(8,128)(2,1)} %pad_maximum_fusion.1.in_ref), custom_call_target="tpu_custom_call" | custom-call | tf_op jit(solution)/shard_map/finish/pallas_call | solution.py:368
  219.0 4.2 %all-to-all-start.4 = ((bf16[4,128,768]{2,1,0:T(8,128)(2,1)}), bf16[4,128,768]{2,1,0:T(8,128)(2,1)}, u32[]{:S(2)}, u32[]{:S(2)}) async-start(bf16[4,128,768]{2,1,0:T(8,128)(2,1)} %bitcast.107), calls=%async_computation.6 | async-start | bytes 1572864 | tf_op jit(solution)/shard_map/all_to_all | solution.py:506
  223.3 3.5 %convolution_convert_fusion.2 = bf16[512,768]{1,0:T(8,128)(2,1)} fusion(bf16[512,768]{1,0:T(8,128)(2,1)S(1)} %copy-done.15, bf16[384,768]{1,0:T(8,128)(2,1)} %collective-permute-done.3, bf16[384,768]{1,0:T(8,128)(2,1)} %get-tuple-element.67, pred[]{:T(512)S(6)} %eq.5), kind=kOutput, calls=%fused_computation.19 | convolution fusion | flops 609681408 | bytes 2752513 | tf_op jit(solution)/shard_map/dot_general | solution.py:664
  226.7 13.4 %all-to-all-done.4 = bf16[4,128,768]{2,1,0:T(8,128)(2,1)} async-done(((bf16[4,128,768]{2,1,0:T(8,128)(2,1)}), bf16[4,128,768]{2,1,0:T(8,128)(2,1)}, u32[]{:S(2)}, u32[]{:S(2)}) %all-to-all-start.4) | async-done | bytes 786464 | tf_op jit(solution)/shard_map/all_to_all | solution.py:506
  240.1 4.2 %all-to-all-start.3 = ((bf16[4,128,768]{2,1,0:T(8,128)(2,1)}), bf16[4,128,768]{2,1,0:T(8,128)(2,1)}, u32[]{:S(2)}, u32[]{:S(2)}) async-start(bf16[4,128,768]{2,1,0:T(8,128)(2,1)} %bitcast.29), calls=%async_computation.5 | async-start | bytes 1572864 | tf_op jit(solution)/shard_map/all_to_all | solution.py:506
  246.2 12.8 %all-to-all-done.3 = bf16[4,128,768]{2,1,0:T(8,128)(2,1)} async-done(((bf16[4,128,768]{2,1,0:T(8,128)(2,1)}), bf16[4,128,768]{2,1,0:T(8,128)(2,1)}, u32[]{:S(2)}, u32[]{:S(2)}) %all-to-all-start.3) | async-done | bytes 786464 | tf_op jit(solution)/shard_map/all_to_all | solution.py:506
  261.3 30.0 %all-gather.7.cloned.1.call-done = bf16[5376,768]{1,0:T(8,128)(2,1)} async-done(((bf16[336,768]{1,0:T(8,128)(2,1)}), bf16[5376,768]{1,0:T(8,128)(2,1)}) %all-gather.7.cloned.1.call-update) | async-done | bytes 8257552 | tf_op jit(solution)/shard_map/all_gather | solution.py:659
  291.2 9.2 %unpack.1 = (f32[384,2304]{1,0:T(8,128)}, f32[16,384]{1,0:T(8,128)}, f32[384,3072]{1,0:T(8,128)}, f32[4,4,96,768]{3,2,1,0:T(8,128)}, f32[2,4,48,768]{3,2,1,0:T(8,128)}) custom-call(s32[1]{0:T(128)} %bitcast.34.dp_ref, bf16[4,4,336,768]{3,2,1,0:T(8,128)(2,1)} %bitcast.100), custom_call_target="tpu_custom_call" | custom-call | tf_op jit(solution)/shard_map/unpack/pallas_call | solution.py:428
  (125 shorter events, 48.4 us)
Async XLA Ops:
  7.2 4.3 %copy-start = (bf16[384,2304]{1,0:T(8,128)(2,1)S(1)}, bf16[384,2304]{1,0:T(8,128)(2,1)}, u32[]{:S(2)}) copy-start(bf16[384,2304]{1,0:T(8,128)(2,1)} %param.16) | copy-start | bytes 5308420
  7.2 11.0 %copy-start.12 = (s32[1,4,128,3,64]{2,4,3,1,0:T(8,128)S(1)}, s32[1,4,128,3,64]{2,4,3,1,0:T(8,128)}, u32[]{:S(2)}) copy-start(s32[1,4,128,3,64]{2,4,3,1,0:T(8,128)} %param.14) | copy-start | bytes 1179652
  7.2 53.8 %all-gather.5.cloned.1.call-start = ((), (), s32[]{:S(2)}) async-start(), calls=%async_computation.9 | async-start | bytes 3342336 | tf_op jit(solution)/shard_map/all_gather | solution.py:555
  7.9 186.6 %reduce-scatter.5.cloned.1.call-start = ((), (), s32[]{:S(2)}) async-start(), calls=%async_computation.8 | async-start | bytes 2949120 | tf_op jit(solution)/shard_map/reduce_scatter | solution.py:620
  14.6 14.8 %collective-permute-start = (bf16[400,640]{1,0:T(8,128)(2,1)}, bf16[400,640]{1,0:T(8,128)(2,1)S(1)}, u32[]{:S(2)}, u32[]{:S(2)}) collective-permute-start(bf16[400,640]{1,0:T(8,128)(2,1)} %arrange.1), channel_id=1, source_target_pairs={{0,16},{16,0},{1,17},{17,1},{2,18},{18,2},{3,19},{19,3},{4,20},{20... | collective-permute-start | bytes 1536008 | tf_op jit(solution)/shard_map/ppermute | solution.py:549
  19.9 9.4 %copy-start.4 = (bf16[400,640]{1,0:T(8,128)(2,1)S(1)}, bf16[400,640]{1,0:T(8,128)(2,1)}, u32[]{:S(2)}) copy-start(bf16[400,640]{1,0:T(8,128)(2,1)} %arrange.1) | copy-start | bytes 1536004
  29.6 1.2 copy-start.10
  29.6 5.6 %copy-start.6 = (bf16[1,128,768]{2,1,0:T(8,128)(2,1)S(1)}, bf16[1,128,768]{2,1,0:T(8,128)(2,1)}, u32[]{:S(2)}) copy-start(bf16[1,128,768]{2,1,0:T(8,128)(2,1)} %param.12) | copy-start | bytes 589828
  30.7 16.2 %collective-permute-start.1 = (bf16[384,768]{1,0:T(8,128)(2,1)S(1)}, bf16[384,768]{1,0:T(8,128)(2,1)S(1)}, u32[]{:S(2)}, u32[]{:S(2)}) collective-permute-start(bf16[384,768]{1,0:T(8,128)(2,1)S(1)} %copy-done.10), channel_id=1, source_target_pairs={{0,16},{16,0},{1,17},{17,1},{2,18},{18,2},{3,19},{19,3},{4,20},{20... | collective-permute-start | bytes 1769480 | tf_op jit(solution)/shard_map/ppermute | solution.py:467
  32.5 27.1 %collective-permute-start.2 = (bf16[384,768]{1,0:T(8,128)(2,1)S(1)}, bf16[384,768]{1,0:T(8,128)(2,1)S(1)}, u32[]{:S(2)}, u32[]{:S(2)}) collective-permute-start(bf16[384,768]{1,0:T(8,128)(2,1)S(1)} %get-tuple-element.59), channel_id=1, source_target_pairs={{0,16},{16,0},{1,17},{17,1},{2,18},{18,2},{3,19},{19,3},{4,20},{20... | collective-permute-start | bytes 1769480 | tf_op jit(solution)/shard_map/ppermute | solution.py:467
  32.9 55.7 %collective-permute-start.3 = (bf16[384,768]{1,0:T(8,128)(2,1)}, bf16[384,768]{1,0:T(8,128)(2,1)}, u32[]{:S(2)}, u32[]{:S(2)}) collective-permute-start(bf16[384,768]{1,0:T(8,128)(2,1)} %get-tuple-element.67), channel_id=1, source_target_pairs={{0,16},{16,0},{1,17},{17,1},{2,18},{18,2},{3,19},{19,3},{4,20},{20... | collective-permute-start | bytes 1769480 | tf_op jit(solution)/shard_map/ppermute | solution.py:467
  47.4 51.6 %copy-start.5 = (bf16[768,768]{1,0:T(8,128)(2,1)}, bf16[768,768]{1,0:T(8,128)(2,1)S(1)}, u32[]{:S(2)}) copy-start(bf16[768,768]{1,0:T(8,128)(2,1)S(1)} %maximum_select_fusion) | copy-start | bytes 3538948
  100.2 1.3 copy-start.7
  101.5 1.1 copy-start.8
  102.5 5.2 %copy-start.14 = (bf16[512,768]{1,0:T(8,128)(2,1)}, bf16[512,768]{1,0:T(8,128)(2,1)S(1)}, u32[]{:S(2)}) copy-start(bf16[512,768]{1,0:T(8,128)(2,1)S(1)} %get-tuple-element.93) | copy-start | bytes 2359300
  111.1 0.7 copy-start.13
  113.2 15.1 %all-to-all-start = ((bf16[4,128,768]{2,1,0:T(8,128)(2,1)}), bf16[4,128,768]{2,1,0:T(8,128)(2,1)S(1)}, u32[]{:S(2)}, u32[]{:S(2)}) async-start(bf16[4,128,768]{2,1,0:T(8,128)(2,1)} %bitcast.114), calls=%async_computation | async-start | bytes 1572864 | tf_op jit(solution)/shard_map/all_to_all | solution.py:623
  116.7 98.8 %reduce-scatter.3.cloned.1.call-start = ((), (), s32[]{:S(2)}) async-start(), calls=%async_computation.7 | async-start | bytes 2027520 | tf_op jit(solution)/shard_map/reduce_scatter | solution.py:646
  128.6 8.8 %copy-start.9 = (bf16[3,64,512]{2,1,0:T(8,128)(2,1)S(1)}, bf16[3,64,512]{2,1,0:T(8,128)(2,1)}, u32[]{:S(2)}) copy-start(bf16[3,64,512]{2,1,0:T(8,128)(2,1)} %get-tuple-element.68) | copy-start | bytes 589828
  128.9 9.6 %copy-start.11 = (bf16[3,128,768]{2,1,0:T(8,128)(2,1)S(1)}, bf16[3,128,768]{2,1,0:T(8,128)(2,1)}, u32[]{:S(2)}) copy-start(bf16[3,128,768]{2,1,0:T(8,128)(2,1)} %pad.13) | copy-start | bytes 1769476
  162.2 15.7 %copy-start.3 = (bf16[768,640]{1,0:T(8,128)(2,1)S(1)}, bf16[768,640]{1,0:T(8,128)(2,1)}, u32[]{:S(2)}) copy-start(bf16[768,640]{1,0:T(8,128)(2,1)} %weight_grad.1) | copy-start | bytes 2949124
  164.1 13.8 %collective-permute-start.4 = (bf16[4,96,640]{2,1,0:T(8,128)(2,1)}, bf16[4,96,640]{2,1,0:T(8,128)(2,1)}, u32[]{:S(2)}, u32[]{:S(2)}) collective-permute-start(bf16[4,96,640]{2,1,0:T(8,128)(2,1)} %dynamic-slice_bitcast_fusion), channel_id=1, source_target_pairs={{0,16},{16,0},{1,17},{17,1},{2,18},{18,2},{3,19},{19,3},{4,20},{20... | collective-permute-start | bytes 1474568 | tf_op jit(solution)/shard_map/ppermute | solution.py:484
  165.6 23.4 %all-to-all-start.1 = ((bf16[4,48,768]{2,1,0:T(8,128)(2,1)}), bf16[4,48,768]{2,1,0:T(8,128)(2,1)}, u32[]{:S(2)}, u32[]{:S(2)}) async-start(bf16[4,48,768]{2,1,0:T(8,128)(2,1)} %bitcast.110), calls=%async_computation.2 | async-start | bytes 589824 | tf_op jit(solution)/shard_map/all_to_all | solution.py:649
  189.0 24.6 %all-to-all-start.2 = ((bf16[4,96,640]{2,1,0:T(8,128)(2,1)}), bf16[4,96,640]{2,1,0:T(8,128)(2,1)S(1)}, u32[]{:S(2)}, u32[]{:S(2)}) async-start(bf16[4,96,640]{2,1,0:T(8,128)(2,1)} %fusion.8), calls=%async_computation.3 | async-start | bytes 983040 | tf_op jit(solution)/shard_map/all_to_all | solution.py:506
  192.5 98.8 %all-gather.7.cloned.1.call-start = ((), (), s32[]{:S(2)}) async-start(), calls=%async_computation.10 | async-start | bytes 8773632 | tf_op jit(solution)/shard_map/all_gather | solution.py:659
  193.5 4.5 %collective-permute-start.6 = (bf16[48,768]{1,0:T(8,128)(2,1)S(1)}, bf16[48,768]{1,0:T(8,128)(2,1)S(1)}, u32[]{:S(2)}, u32[]{:S(2)}) collective-permute-start(bf16[48,768]{1,0:T(8,128)(2,1)S(1)} %reduce_sum.179), channel_id=1, source_target_pairs={{0,16},{16,0},{1,17},{17,1},{2,18},{18,2},{3,19},{19,3},{4,20},{20... | collective-permute-start | bytes 221192 | tf_op jit(solution)/shard_map/ppermute | solution.py:501
  196.2 19.4 %copy-start.2 = (bf16[1,128,768]{2,1,0:T(8,128)(2,1)S(1)}, bf16[1,128,768]{2,1,0:T(8,128)(2,1)}, u32[]{:S(2)}) copy-start(bf16[1,128,768]{2,1,0:T(8,128)(2,1)} %param.11) | copy-start | bytes 589828
  196.2 17.5 %collective-permute-start.5 = (bf16[192,768]{1,0:T(8,128)(2,1)}, bf16[192,768]{1,0:T(8,128)(2,1)S(1)}, u32[]{:S(2)}, u32[]{:S(2)}) collective-permute-start(bf16[192,768]{1,0:T(8,128)(2,1)} %dynamic-slice_bitcast_fusion.1), channel_id=1, source_target_pairs={{0,16},{16,0},{1,17},{17,1},{2,18},{18,2},{3,19},{19,3},{4,20},{20... | collective-permute-start | bytes 884744 | tf_op jit(solution)/shard_map/ppermute | solution.py:484
  215.7 7.6 %copy-start.15 = (bf16[512,768]{1,0:T(8,128)(2,1)S(1)}, bf16[512,768]{1,0:T(8,128)(2,1)}, u32[]{:S(2)}) copy-start(bf16[512,768]{1,0:T(8,128)(2,1)} %copy-done.14) | copy-start | bytes 2359300
  219.0 21.1 %all-to-all-start.4 = ((bf16[4,128,768]{2,1,0:T(8,128)(2,1)}), bf16[4,128,768]{2,1,0:T(8,128)(2,1)}, u32[]{:S(2)}, u32[]{:S(2)}) async-start(bf16[4,128,768]{2,1,0:T(8,128)(2,1)} %bitcast.107), calls=%async_computation.6 | async-start | bytes 1572864 | tf_op jit(solution)/shard_map/all_to_all | solution.py:506
  240.1 18.8 %all-to-all-start.3 = ((bf16[4,128,768]{2,1,0:T(8,128)(2,1)}), bf16[4,128,768]{2,1,0:T(8,128)(2,1)}, u32[]{:S(2)}, u32[]{:S(2)}) async-start(bf16[4,128,768]{2,1,0:T(8,128)(2,1)} %bitcast.29), calls=%async_computation.5 | async-start | bytes 1572864 | tf_op jit(solution)/shard_map/all_to_all | solution.py:506
  291.2 11.9 %copy-start.1 = (bf16[384,2304]{1,0:T(8,128)(2,1)S(1)}, bf16[384,2304]{1,0:T(8,128)(2,1)}, u32[]{:S(2)}) copy-start(bf16[384,2304]{1,0:T(8,128)(2,1)} %param.16) | copy-start | bytes 5308420
Sparse Core Ops, SparseCore 0:
  10.3 49.9 all-gather.4
  111.3 48.0 reduce-scatter.4
  162.2 44.8 reduce-scatter.2
  215.7 75.4 all-gather.6

commit v7 on v6

--- a/solution.py
+++ b/solution.py
@@ -213,59 +213,55 @@
     )(base, kept, query, pairs, key_score)
 
 
-def attend_back_body(first, last, tiles, chunk, q_ref, grad_ref, kv_ref, prob_ref, dq_ref, out_ref, turned_ref, dq_turned_ref, gates_ref, raw_ref, dkv_ref, gate_ref):
+def attend_back_kernel(parts, chunk, base_ref, q_ref, grad_ref, kv_ref, prob_ref, dq_ref, out_ref, turned_ref, dq_turned_ref, gates_ref, raw_ref, dkv_ref, gate_ref):
     f32, bf16 = jnp.float32, jnp.bfloat16
-    rows = q_ref.shape[0]
-    steps = tiles * LANES // chunk
-    if first:
-        dkv_ref[...] = jnp.zeros_like(dkv_ref)
-        gate_ref[...] = jnp.zeros_like(gate_ref)
-    dot_sum = None
-    for at in range(steps):
-        cols = slice(at * chunk, (at + 1) * chunk)
-        raw = lax.dot_general(grad_ref[...], kv_ref[cols, :], NT, preferred_element_type=f32)
-        raw_ref[:, cols] = raw
-        part = jnp.sum(raw * prob_ref[0, 0, :, cols].astype(f32), axis=1, keepdims=True)
-        dot_sum = part if dot_sum is None else dot_sum + part
+    rows = prob_ref.shape[2]
+    count, height, _ = out_ref.shape
     lane = lax.broadcasted_iota(jnp.int32, (rows, LANES), 1)
-    scaled = jnp.where(lane == HD, 1.0, q_ref[...].astype(f32) * HD ** (-0.5))
-    query_t = jnp.transpose(scaled)[: HD + 16].astype(bf16)
-    grad_t = jnp.transpose(grad_ref[...].astype(f32))[HD:].astype(bf16)
-    dq = None
-    for at in range(steps):
-        cols = slice(at * chunk, (at + 1) * chunk)
-        prob = prob_ref[0, 0, :, cols]
-        grad_score = (prob.astype(f32) * (raw_ref[:, cols] - dot_sum)).astype(bf16)
-        piece = jnp.dot(grad_score, kv_ref[cols, :], preferred_element_type=f32)
-        dq = piece if dq is None else dq + piece
-        keys = jnp.dot(query_t, grad_score, preferred_element_type=f32)
-        dkv_ref[:HD, cols] += keys[:HD]
-        gate_ref[:, cols] += keys[HD : HD + 8]
-        dkv_ref[HD:, cols] += jnp.dot(grad_t, prob, preferred_element_type=f32)
-    dq = dq * HD ** (-0.5)
-    dq_ref[...] = dq.astype(dq_ref.dtype)
-    dq_turned_ref[0] = jnp.transpose(dq)[:HD, :].astype(bf16)
-    if last:
-        turned_ref[0] = dkv_ref[...].astype(bf16)
-        gates_ref[0] = gate_ref[...]
-        count, height, _ = out_ref.shape
-        parts = (height - PAD_ROWS) // LANES
-        for at in range(count):
-            rows_of = []
-            for part in range(parts):
-                cols = slice((part * count + at) * LANES, (part * count + at + 1) * LANES)
-                out_ref[at, part * LANES : (part + 1) * LANES, :] = jnp.transpose(dkv_ref[:, cols]).astype(bf16)
-                rows_of.append(gate_ref[0:1, cols])
-            rows_of.append(jnp.zeros((PAD_ROWS - parts, LANES), f32))
-            out_ref[at, height - PAD_ROWS :, :] = jnp.concatenate(rows_of, axis=0).astype(bf16)
-
-
-def attend_back_kernel(parts, chunk, base_ref, *refs):
-    part = pl.program_id(1)
-    for at in range(parts):
-        pl.when(part == at)(
-            functools.partial(attend_back_body, at == 0, at == parts - 1, (at + 1) * chunk // LANES, chunk, *refs)
-        )
+    for part in reversed(range(parts)):
+        last = part == parts - 1
+        query = q_ref[pl.ds(pl.multiple_of((part * (chunk // rows) + base_ref[1]) * rows, rows), rows), :]
+        grad = grad_ref[part * rows : (part + 1) * rows, :]
+        dot_sum = None
+        for at in range(part + 1):
+            cols = slice(at * chunk, (at + 1) * chunk)
+            raw = lax.dot_general(grad, kv_ref[cols, :], NT, preferred_element_type=f32)
+            raw_ref[part, :, cols] = raw
+            piece = jnp.sum(raw * prob_ref[0, part, :, cols].astype(f32), axis=1, keepdims=True)
+            dot_sum = piece if dot_sum is None else dot_sum + piece
+        scaled = jnp.where(lane == HD, 1.0, query.astype(f32) * HD ** (-0.5))
+        query_t = jnp.transpose(scaled)[: HD + 16].astype(bf16)
+        grad_t = jnp.transpose(grad.astype(f32))[HD:].astype(bf16)
+        dq = None
+        for at in range(part + 1):
+            cols = slice(at * chunk, (at + 1) * chunk)
+            prob = prob_ref[0, part, :, cols]
+            grad_score = (prob.astype(f32) * (raw_ref[part, :, cols] - dot_sum)).astype(bf16)
+            piece = jnp.dot(grad_score, kv_ref[cols, :], preferred_element_type=f32)
+            dq = piece if dq is None else dq + piece
+            keys = jnp.dot(query_t, grad_score, preferred_element_type=f32)
+            values = jnp.dot(grad_t, prob, preferred_element_type=f32)
+            if last:
+                dkv_ref[:HD, cols] = keys[:HD]
+                gate_ref[:, cols] = keys[HD : HD + 8]
+                dkv_ref[HD:, cols] = values
+            else:
+                dkv_ref[:HD, cols] += keys[:HD]
+                gate_ref[:, cols] += keys[HD : HD + 8]
+                dkv_ref[HD:, cols] += values
+        dq = dq * HD ** (-0.5)
+        dq_ref[part * rows : (part + 1) * rows, :] = dq.astype(dq_ref.dtype)
+        dq_turned_ref[0, :, part * rows : (part + 1) * rows] = jnp.transpose(dq)[:HD, :].astype(bf16)
+    turned_ref[0] = dkv_ref[...].astype(bf16)
+    gates_ref[0] = gate_ref[...]
+    for at in range(count):
+        rows_of = []
+        for part in range(parts):
+            cols = slice((part * count + at) * LANES, (part * count + at + 1) * LANES)
+            out_ref[at, part * LANES : (part + 1) * LANES, :] = jnp.transpose(dkv_ref[:, cols]).astype(bf16)
+            rows_of.append(gate_ref[0:1, cols])
+        rows_of.append(jnp.zeros((PAD_ROWS - parts, LANES), f32))
+        out_ref[at, height - PAD_ROWS :, :] = jnp.concatenate(rows_of, axis=0).astype(bf16)
 
 
 def attend_back(count, base, query, grad, pairs, prob):
@@ -276,26 +272,26 @@
     return pl.pallas_call(
         functools.partial(attend_back_kernel, parts, chunk),
         grid_spec=pltpu.PrefetchScalarGridSpec(
-        num_scalar_prefetch=1,
-        grid=(heads, parts),
-        in_specs=[
-            pl.BlockSpec((block, LANES), lambda h, r, b: (r * (chunk // block) + b[1], h)),
-            pl.BlockSpec((block, LANES), lambda h, r, b: (r, h)),
-            pl.BlockSpec((slot, LANES), lambda h, r, b: (0, h)),
-            pl.BlockSpec((1, 1, block, slot), lambda h, r, b: (h, r, 0, 0)),
-        ],
-        out_specs=[
-            pl.BlockSpec((block, LANES), lambda h, r, b: (r, h)),
-            pl.BlockSpec((count, height, LANES), lambda h, r, b: (0, 0, h)),
-            pl.BlockSpec((1, LANES, slot), lambda h, r, b: (h, 0, 0)),
-            pl.BlockSpec((1, HD, block), lambda h, r, b: (h, 0, r)),
-            pl.BlockSpec((1, 8, slot), lambda h, r, b: (h, 0, 0)),
-        ],
-        scratch_shapes=[
-            pltpu.VMEM((block, slot), jnp.float32),
-            pltpu.VMEM((LANES, slot), jnp.float32),
-            pltpu.VMEM((8, slot), jnp.float32),
-        ],
+            num_scalar_prefetch=1,
+            grid=(heads,),
+            in_specs=[
+                pl.BlockSpec((slot, LANES), lambda h, b: (0, h)),
+                pl.BlockSpec((parts * block, LANES), lambda h, b: (0, h)),
+                pl.BlockSpec((slot, LANES), lambda h, b: (0, h)),
+                pl.BlockSpec((1, parts, block, slot), lambda h, b: (h, 0, 0, 0)),
+            ],
+            out_specs=[
+                pl.BlockSpec((parts * block, LANES), lambda h, b: (0, h)),
+                pl.BlockSpec((count, height, LANES), lambda h, b: (0, 0, h)),
+                pl.BlockSpec((1, LANES, slot), lambda h, b: (h, 0, 0)),
+                pl.BlockSpec((1, HD, parts * block), lambda h, b: (h, 0, 0)),
+                pl.BlockSpec((1, 8, slot), lambda h, b: (h, 0, 0)),
+            ],
+            scratch_shapes=[
+                pltpu.VMEM((parts, block, slot), jnp.float32),
+                pltpu.VMEM((LANES, slot), jnp.float32),
+                pltpu.VMEM((8, slot), jnp.float32),
+            ],
         ),
         out_shape=[
             jax.ShapeDtypeStruct((parts * block, heads * LANES), jnp.bfloat16),
@@ -372,7 +368,7 @@
     )(pair, dq, score, weights)
 
 
-def unpack_kernel(groups, heads, piece, parts, dp_ref, all_ref, qkv_ref, score_ref, fc_ref, proj_ref, *rest):
+def unpack_kernel(groups, heads, piece, parts, dp_ref, all_ref, qkv_ref, score_ref, gain_ref, fc_ref, proj_ref, *rest):
     f32 = jnp.float32
     keys = heads * 2 * HD
     part_cols = fc_ref.shape[1] // (groups * parts)
@@ -403,7 +399,8 @@
         turned = jnp.transpose(jnp.concatenate([narrow, jnp.zeros((LANES - piece, LANES), f32)], axis=0))
 
         def store(index):
-            score_ref[:, index * piece : (index + 1) * piece] = turned[: score_ref.shape[0], :piece]
+            gain_ref[:, index * piece : (index + 1) * piece] = turned[groups * heads : groups * heads + 8, :piece]
+            score_ref[:, index * piece : (index + 1) * piece] = turned[: groups * heads, :piece]
 
         if all_ref.shape[1] > 1:
             store(step)
@@ -417,7 +414,8 @@
     step = 1 if piece % 16 == 0 else count
     blocks = [
         ((count * piece, groups * heads * 3 * HD), (step * piece, groups * heads * 3 * HD), lambda c, d: (c, 0)),
-        ((PAD_ROWS, count * piece), (PAD_ROWS, count * piece), lambda c, d: (0, 0)),
+        ((groups * heads, count * piece), (groups * heads, count * piece), lambda c, d: (0, 0)),
+        ((8, count * piece), (8, count * piece), lambda c, d: (0, 0)),
         ((count * piece, hidden), (step * piece, hidden), lambda c, d: (c, 0)),
         ((groups, count, proj_piece, width), (groups, step, proj_piece, width), lambda c, d: (0, c, 0, 0)),
     ]
@@ -669,7 +667,7 @@
     grad_input_norm = first_pull(grad_norm_one)[0]
     input_grad = (grad_mixed + grad_input_norm).astype(bf16)[None]
 
-    qkv_grad, turned_rows, fc_grad, proj_grad, *rest = unpack(
+    qkv_grad, turned_scores, gains, fc_grad, proj_grad, *rest = unpack(
         dp_at.astype(jnp.int32)[None], gathered, heads, piece, proj_piece, dp_count, hidden
     )
     proj_grad = proj_grad.reshape(-1, width)
@@ -679,8 +677,8 @@
         out_grad = lax.dynamic_slice_in_dim(
             gathered[:, :, 2 * piece + proj_piece :].reshape(width, width), dp_at * weight_rows, weight_rows, 0
         ).astype(f32)
-    score_grad = turned_rows[:H].T
-    return (output, input_grad, turned_rows[H], qkv_grad, score_grad, out_grad, turned_rows[H + 1], fc_grad, proj_grad)
+    score_grad = turned_scores.T
+    return (output, input_grad, gains[0], qkv_grad, score_grad, out_grad, gains[1], fc_grad, proj_grad)
 
 
 def solution(mesh):

time: 312 us -> 310 us (level)
  waiting for transfers between devices: 115 us -> 120 us
  Pallas kernels: 63.5 us -> 59.6 us
    pallas_call x1, Pallas kernels: 15.1 us -> 11.1 us  [attend_back(): pl.pallas_call(functools.partial(attend_back_kernel, parts, chunk), grid_...]
  transfers between devices with their start and end apart: 16 -> 16, of which waited for: 10 -> 10; matrix products, arithmetic and copies ran while one was open for 13% -> 13% of each run, Pallas kernels for 18% -> 16%
where the time goes in v7:
time: 310 us; the launch traced here: 309 us
  waiting for transfers between devices  120 us (39%)
  Pallas kernels  59.6 us (19%)
  starting transfers between devices  30.8 us (10%)
  blocking collectives  29.3 us (9%)
  local copies, waits for them, and re-layouts  22.2 us (7%)
  other arithmetic  17.8 us (6%)
  between operations  14.8 us (5%)
  matrix products  14.4 us (5%)
    all_to_all x3, waiting for transfers between devices, exchange_sum(): came = lax.all_to_all(parts, axis, split_axis=0, concat_axis=0, tiled=True)  44.6 us
    all_gather x1, waiting for transfers between devices, per_device(): lax.all_gather(gradients, ('sp', 'ctx'), axis=0, tiled=False)  32.1 us
    pallas_call x1, Pallas kernels, attend(): pl.pallas_call(functools.partial(attend_kernel, parts, chunk), grid_spec=...  20.3 us
    ppermute x3, waiting for transfers between devices, dp_send(): return lax.ppermute(mine, 'dp', [(0, 1), (1, 0)])  12.2 us
    all_to_all x3, starting transfers between devices, exchange_sum(): came = lax.all_to_all(parts, axis, split_axis=0, concat_axis=0, tiled=True)  11.9 us
    all_gather x1, blocking collectives, per_device(): cot_group = lax.all_gather(cot_own, 'sp', axis=0, tiled=True)  11.7 us
    pallas_call x1, Pallas kernels, attend_back(): pl.pallas_call(functools.partial(attend_back_kernel, parts, chunk), grid_...  11.1 us
    all_gather x1, blocking collectives, per_device(): attended_all = lax.all_gather(attended, 'sp', axis=0, tiled=True)  9.25 us
  transfers between devices with their start and end apart: 16, of which 10 were waited for; matrix products, arithmetic and copies ran while one was open for 13% of the time, Pallas kernels for 16%

profile of v7, /device:TPU:0, one launch (start us, length us, event | category | flops | bytes accessed | tf_op | source)
XLA Modules:
  0.0 309.1 jit_solution(15807099030188192055)
XLA Ops:
  12.5 2.1 arrange.1
  14.6 3.0 collective-permute-start
  21.1 2.0 pad_maximum_fusion.2
  23.1 6.2 %collective-permute-done = bf16[400,640]{1,0:T(8,128)(2,1)S(1)} collective-permute-done((bf16[400,640]{1,0:T(8,128)(2,1)}, bf16[400,640]{1,0:T(8,128)(2,1)S(1)}, u32[]{:S(2)}, u32[]{:S(2)}) %collective-permute-start) | collective-permute-done | bytes 512032 | tf_op jit(solution)/shard_map/ppermute | solution.py:547
  30.7 1.7 collective-permute-start.1
  35.2 11.7 %all_gather.19 = bf16[512,768]{1,0:T(8,128)(2,1)} all-gather(bf16[128,768]{1,0:T(8,128)(2,1)S(1)} %bitcast.108), channel_id=1, replica_groups=mesh['dp'=2,'sp'=4,'ctx'=4] {'sp'}, dimensions={0}, use_global_device_ids=true | all-gather | bytes 983040 | tf_op jit(solution)/shard_map/all_gather | solution.py:572
  47.4 12.2 %collective-permute-done.2 = bf16[384,768]{1,0:T(8,128)(2,1)S(1)} collective-permute-done((bf16[384,768]{1,0:T(8,128)(2,1)S(1)}, bf16[384,768]{1,0:T(8,128)(2,1)S(1)}, u32[]{:S(2)}, u32[]{:S(2)}) %collective-permute-start.2) | collective-permute-done | bytes 589856 | tf_op jit(solution)/shard_map/ppermute | solution.py:465
  61.0 7.2 %project.1 = (bf16[2048,768]{1,0:T(8,128)(2,1)}, bf16[2048,384]{1,0:T(8,128)(2,1)}, bf16[2048,384]{1,0:T(8,128)(2,1)}, bf16[3,1,2048]{2,1,0:T(2,128)(2,1)}) custom-call(bf16[2048,768]{1,0:T(8,128)(2,1)} %bitcast.101, f32[1,768]{1,0:T(1,128)} %maximum_convert_fusion.gain_ref, bf16[768,640]{1,0:T(8,128)(2,1)} %pad_maximum_fusion.1.in_ref), custom_call_target="tpu_custom_call" | custom-call | tf_op jit(solution)/shard_map/project/pallas_call | solution.py:73
  68.3 20.3 %attend.1 = (bf16[3,64,512]{2,1,0:T(8,128)(2,1)}, bf16[3,4,128,2048]{3,2,1,0:T(8,128)(2,1)}) custom-call(s32[2]{0:T(128)} %pad_add_fusion.base_ref, s32[3,4,128,64]{3,2,1,0:T(8,128)} %bitcast.105, bf16[2048,384]{1,0:T(8,128)(2,1)} %get-tuple-element.64.refs_1_.q_ref, bf16[2048,384]{1,0:T(8,128)(2,1)} %get-tuple-element.65.refs_2_.kv_ref, ...), custom_call_target="tpu_custom_call" | custom-call | tf_op jit(solution)/shard_map/attend/pallas_call | solution.py:205
  88.5 9.2 %all_gather.20 = bf16[768,512]{1,0:T(8,128)(2,1)S(1)} all-gather(bf16[192,512]{1,0:T(8,128)(2,1)} %bitcast.115), channel_id=1, replica_groups=mesh['dp'=2,'sp'=4,'ctx'=4] {'sp'}, dimensions={0}, use_global_device_ids=true | all-gather | bytes 983040 | tf_op jit(solution)/shard_map/all_gather | solution.py:595
  102.6 3.4 %fusion.6 = bf16[512,768]{1,0:T(8,128)(2,1)S(1)} fusion(f32[512,768]{1,0:T(8,128)S(1)} %get-tuple-element.132, bf16[512,768]{1,0:T(8,128)(2,1)S(1)} %copy-done.8, pred[512]{0:T(512)(128)(4,1)S(1)} %fusion.32, bf16[384,768]{1,0:T(8,128)(2,1)} %collective-permute-done.3, bf16[384,768]{1,0:T(8,128)(2,1)} %get-tuple-element.68, pred[]{:T(512)S(6)} %eq.5), kind=kOutput, calls=%fused_computation.9 | convolution fusion | flops 617545728 | bytes 4325889 | tf_op jit(solution)/shard_map/dot_general | solution.py:38
  113.2 3.5 %all-to-all-start = ((bf16[4,128,768]{2,1,0:T(8,128)(2,1)}), bf16[4,128,768]{2,1,0:T(8,128)(2,1)S(1)}, u32[]{:S(2)}, u32[]{:S(2)}) async-start(bf16[4,128,768]{2,1,0:T(8,128)(2,1)} %bitcast.113), calls=%async_computation | async-start | bytes 1572864 | tf_op jit(solution)/shard_map/all_to_all | solution.py:621
  119.0 2.1 constant_dynamic-slice_fusion.1
  121.1 7.2 %all-to-all-done = bf16[4,128,768]{2,1,0:T(8,128)(2,1)S(1)} async-done(((bf16[4,128,768]{2,1,0:T(8,128)(2,1)}), bf16[4,128,768]{2,1,0:T(8,128)(2,1)S(1)}, u32[]{:S(2)}, u32[]{:S(2)}) %all-to-all-start) | async-done | bytes 786464 | tf_op jit(solution)/shard_map/all_to_all | solution.py:621
  129.1 8.4 %all_gather.21 = bf16[512,768]{1,0:T(8,128)(2,1)S(1)} all-gather(bf16[128,768]{1,0:T(8,128)(2,1)S(1)} %fusion.19), channel_id=1, replica_groups=mesh['dp'=2,'sp'=4,'ctx'=4] {'sp'}, dimensions={0}, use_global_device_ids=true | all-gather | bytes 983040 | tf_op jit(solution)/shard_map/all_gather | solution.py:633
  139.8 11.1 %attend_back.1 = (bf16[512,384]{1,0:T(8,128)(2,1)}, bf16[4,528,384]{2,1,0:T(8,128)(2,1)}, bf16[3,128,2048]{2,1,0:T(8,128)(2,1)}, bf16[3,64,512]{2,1,0:T(8,128)(2,1)}, f32[3,8,2048]{2,1,0:T(8,128)}) custom-call(s32[2]{0:T(128)} %pad_add_fusion.base_ref, bf16[2048,384]{1,0:T(8,128)(2,1)} %get-tuple-element.64.refs_1_.q_ref, ...), custom_call_target="tpu_custom_call" | custom-call | tf_op jit(solution)/shard_map/attend_back/pallas_call | solution.py:272
  151.9 6.3 %weight_grad.1 = bf16[768,640]{1,0:T(8,128)(2,1)} custom-call(bf16[3,128,2048]{2,1,0:T(8,128)(2,1)} %get-tuple-element.81.turned_ref, bf16[3,64,512]{2,1,0:T(8,128)(2,1)} %get-tuple-element.82.dq_ref, f32[3,8,2048]{2,1,0:T(8,128)} %get-tuple-element.83.gates_ref, bf16[3,2048]{1,0:T(4,128)(2,1)} %bitcast.121, bf16[2048,768]{1,0:T(8,128)(2,1)} %get-tuple-element.75.slot_ref, ...), custom_call_target="tpu_custom_call" | custom-call | tf_op jit(solution)/shard_map/weight_grad/pallas_call | solution.py:331
  158.3 1.9 dynamic-slice_bitcast_fusion
  161.7 4.8 %all-to-all-start.1 = ((bf16[4,48,768]{2,1,0:T(8,128)(2,1)}), bf16[4,48,768]{2,1,0:T(8,128)(2,1)}, u32[]{:S(2)}, u32[]{:S(2)}) async-start(bf16[4,48,768]{2,1,0:T(8,128)(2,1)} %bitcast.109), calls=%async_computation.2 | async-start | bytes 589824 | tf_op jit(solution)/shard_map/all_to_all | solution.py:647
  166.5 7.4 %collective-permute-done.4 = bf16[4,96,640]{2,1,0:T(8,128)(2,1)} collective-permute-done((bf16[4,96,640]{2,1,0:T(8,128)(2,1)}, bf16[4,96,640]{2,1,0:T(8,128)(2,1)}, u32[]{:S(2)}, u32[]{:S(2)}) %collective-permute-start.4) | collective-permute-done | bytes 491552 | tf_op jit(solution)/shard_map/ppermute | solution.py:482
  173.9 1.9 fusion.8
  175.9 8.2 %all-to-all-done.1 = bf16[4,48,768]{2,1,0:T(8,128)(2,1)} async-done(((bf16[4,48,768]{2,1,0:T(8,128)(2,1)}), bf16[4,48,768]{2,1,0:T(8,128)(2,1)}, u32[]{:S(2)}, u32[]{:S(2)}) %all-to-all-start.1) | async-done | bytes 294944 | tf_op jit(solution)/shard_map/all_to_all | solution.py:647
  184.1 3.5 %all-to-all-start.2 = ((bf16[4,96,640]{2,1,0:T(8,128)(2,1)}), bf16[4,96,640]{2,1,0:T(8,128)(2,1)S(1)}, u32[]{:S(2)}, u32[]{:S(2)}) async-start(bf16[4,96,640]{2,1,0:T(8,128)(2,1)} %fusion.8), calls=%async_computation.3 | async-start | bytes 983040 | tf_op jit(solution)/shard_map/all_to_all | solution.py:504
  193.9 18.0 %all-to-all-done.2 = bf16[4,96,640]{2,1,0:T(8,128)(2,1)S(1)} async-done(((bf16[4,96,640]{2,1,0:T(8,128)(2,1)}), bf16[4,96,640]{2,1,0:T(8,128)(2,1)S(1)}, u32[]{:S(2)}, u32[]{:S(2)}) %all-to-all-start.2) | async-done | bytes 491552 | tf_op jit(solution)/shard_map/all_to_all | solution.py:504
  214.0 3.3 %finish.1 = bf16[512,768]{1,0:T(8,128)(2,1)} custom-call(bf16[528,384]{1,0:T(8,128)(2,1)} %bitcast.120, bf16[512,384]{1,0:T(8,128)(2,1)} %get-tuple-element.96.dq_ref, bf16[3,512]{1,0:T(4,128)(2,1)} %bitcast.122, bf16[768,640]{1,0:T(8,128)(2,1)} %pad_maximum_fusion.1.in_ref), custom_call_target="tpu_custom_call" | custom-call | tf_op jit(solution)/shard_map/finish/pallas_call | solution.py:364
  217.3 4.2 %all-to-all-start.4 = ((bf16[4,128,768]{2,1,0:T(8,128)(2,1)}), bf16[4,128,768]{2,1,0:T(8,128)(2,1)}, u32[]{:S(2)}, u32[]{:S(2)}) async-start(bf16[4,128,768]{2,1,0:T(8,128)(2,1)} %bitcast.106), calls=%async_computation.6 | async-start | bytes 1572864 | tf_op jit(solution)/shard_map/all_to_all | solution.py:504
  221.6 3.4 %convolution_convert_fusion.2 = bf16[512,768]{1,0:T(8,128)(2,1)} fusion(bf16[512,768]{1,0:T(8,128)(2,1)S(1)} %copy-done.15, bf16[384,768]{1,0:T(8,128)(2,1)} %collective-permute-done.3, bf16[384,768]{1,0:T(8,128)(2,1)} %get-tuple-element.68, pred[]{:T(512)S(6)} %eq.5), kind=kOutput, calls=%fused_computation.19 | convolution fusion | flops 609681408 | bytes 2752513 | tf_op jit(solution)/shard_map/dot_general | solution.py:662
  225.0 13.8 %all-to-all-done.4 = bf16[4,128,768]{2,1,0:T(8,128)(2,1)} async-done(((bf16[4,128,768]{2,1,0:T(8,128)(2,1)}), bf16[4,128,768]{2,1,0:T(8,128)(2,1)}, u32[]{:S(2)}, u32[]{:S(2)}) %all-to-all-start.4) | async-done | bytes 786464 | tf_op jit(solution)/shard_map/all_to_all | solution.py:504
  238.7 4.2 %all-to-all-start.3 = ((bf16[4,128,768]{2,1,0:T(8,128)(2,1)}), bf16[4,128,768]{2,1,0:T(8,128)(2,1)}, u32[]{:S(2)}, u32[]{:S(2)}) async-start(bf16[4,128,768]{2,1,0:T(8,128)(2,1)} %bitcast.29), calls=%async_computation.5 | async-start | bytes 1572864 | tf_op jit(solution)/shard_map/all_to_all | solution.py:504
  244.8 12.8 %all-to-all-done.3 = bf16[4,128,768]{2,1,0:T(8,128)(2,1)} async-done(((bf16[4,128,768]{2,1,0:T(8,128)(2,1)}), bf16[4,128,768]{2,1,0:T(8,128)(2,1)}, u32[]{:S(2)}, u32[]{:S(2)}) %all-to-all-start.3) | async-done | bytes 786464 | tf_op jit(solution)/shard_map/all_to_all | solution.py:504
  259.9 32.1 %all-gather.7.cloned.1.call-done = bf16[5376,768]{1,0:T(8,128)(2,1)} async-done(((bf16[336,768]{1,0:T(8,128)(2,1)}), bf16[5376,768]{1,0:T(8,128)(2,1)}) %all-gather.7.cloned.1.call-update) | async-done | bytes 8257552 | tf_op jit(solution)/shard_map/all_gather | solution.py:657
  292.0 9.2 %unpack.1 = (f32[384,2304]{1,0:T(8,128)}, f32[12,384]{1,0:T(8,128)}, f32[8,384]{1,0:T(8,128)}, f32[384,3072]{1,0:T(8,128)}, f32[4,4,96,768]{3,2,1,0:T(8,128)}, /*index=5*/f32[2,4,48,768]{3,2,1,0:T(8,128)}) custom-call(s32[1]{0:T(128)} %bitcast.34.dp_ref, bf16[4,4,336,768]{3,2,1,0:T(8,128)(2,1)} %bitcast.99), custom_call_target="tpu_custom_call" | custom-call | tf_op jit(solution)/shard_map/unpack/pallas_call | solution.py:426
  (124 shorter events, 47.7 us)
Async XLA Ops:
  7.2 4.3 %copy-start = (bf16[384,2304]{1,0:T(8,128)(2,1)S(1)}, bf16[384,2304]{1,0:T(8,128)(2,1)}, u32[]{:S(2)}) copy-start(bf16[384,2304]{1,0:T(8,128)(2,1)} %param.16) | copy-start | bytes 5308420
  7.2 11.0 %copy-start.12 = (s32[1,4,128,3,64]{2,4,3,1,0:T(8,128)S(1)}, s32[1,4,128,3,64]{2,4,3,1,0:T(8,128)}, u32[]{:S(2)}) copy-start(s32[1,4,128,3,64]{2,4,3,1,0:T(8,128)} %param.14) | copy-start | bytes 1179652
  7.2 53.8 %all-gather.5.cloned.1.call-start = ((), (), s32[]{:S(2)}) async-start(), calls=%async_computation.9 | async-start | bytes 3342336 | tf_op jit(solution)/shard_map/all_gather | solution.py:553
  7.9 181.2 %reduce-scatter.5.cloned.1.call-start = ((), (), s32[]{:S(2)}) async-start(), calls=%async_computation.8 | async-start | bytes 2949120 | tf_op jit(solution)/shard_map/reduce_scatter | solution.py:618
  14.6 14.8 %collective-permute-start = (bf16[400,640]{1,0:T(8,128)(2,1)}, bf16[400,640]{1,0:T(8,128)(2,1)S(1)}, u32[]{:S(2)}, u32[]{:S(2)}) collective-permute-start(bf16[400,640]{1,0:T(8,128)(2,1)} %arrange.1), channel_id=1, source_target_pairs={{0,16},{16,0},{1,17},{17,1},{2,18},{18,2},{3,19},{19,3},{4,20},{20... | collective-permute-start | bytes 1536008 | tf_op jit(solution)/shard_map/ppermute | solution.py:547
  19.9 9.4 %copy-start.4 = (bf16[400,640]{1,0:T(8,128)(2,1)S(1)}, bf16[400,640]{1,0:T(8,128)(2,1)}, u32[]{:S(2)}) copy-start(bf16[400,640]{1,0:T(8,128)(2,1)} %arrange.1) | copy-start | bytes 1536004
  29.6 1.2 copy-start.10
  29.6 5.6 %copy-start.6 = (bf16[1,128,768]{2,1,0:T(8,128)(2,1)S(1)}, bf16[1,128,768]{2,1,0:T(8,128)(2,1)}, u32[]{:S(2)}) copy-start(bf16[1,128,768]{2,1,0:T(8,128)(2,1)} %param.12) | copy-start | bytes 589828
  30.7 16.2 %collective-permute-start.1 = (bf16[384,768]{1,0:T(8,128)(2,1)S(1)}, bf16[384,768]{1,0:T(8,128)(2,1)S(1)}, u32[]{:S(2)}, u32[]{:S(2)}) collective-permute-start(bf16[384,768]{1,0:T(8,128)(2,1)S(1)} %copy-done.10), channel_id=1, source_target_pairs={{0,16},{16,0},{1,17},{17,1},{2,18},{18,2},{3,19},{19,3},{4,20},{20... | collective-permute-start | bytes 1769480 | tf_op jit(solution)/shard_map/ppermute | solution.py:465
  32.5 27.1 %collective-permute-start.2 = (bf16[384,768]{1,0:T(8,128)(2,1)S(1)}, bf16[384,768]{1,0:T(8,128)(2,1)S(1)}, u32[]{:S(2)}, u32[]{:S(2)}) collective-permute-start(bf16[384,768]{1,0:T(8,128)(2,1)S(1)} %get-tuple-element.60), channel_id=1, source_target_pairs={{0,16},{16,0},{1,17},{17,1},{2,18},{18,2},{3,19},{19,3},{4,20},{20... | collective-permute-start | bytes 1769480 | tf_op jit(solution)/shard_map/ppermute | solution.py:465
  32.9 55.7 %collective-permute-start.3 = (bf16[384,768]{1,0:T(8,128)(2,1)}, bf16[384,768]{1,0:T(8,128)(2,1)}, u32[]{:S(2)}, u32[]{:S(2)}) collective-permute-start(bf16[384,768]{1,0:T(8,128)(2,1)} %get-tuple-element.68), channel_id=1, source_target_pairs={{0,16},{16,0},{1,17},{17,1},{2,18},{18,2},{3,19},{19,3},{4,20},{20... | collective-permute-start | bytes 1769480 | tf_op jit(solution)/shard_map/ppermute | solution.py:465
  47.4 51.6 %copy-start.5 = (bf16[768,768]{1,0:T(8,128)(2,1)}, bf16[768,768]{1,0:T(8,128)(2,1)S(1)}, u32[]{:S(2)}) copy-start(bf16[768,768]{1,0:T(8,128)(2,1)S(1)} %maximum_select_fusion) | copy-start | bytes 3538948
  100.2 1.3 copy-start.7
  101.5 1.1 copy-start.8
  102.5 5.2 %copy-start.14 = (bf16[512,768]{1,0:T(8,128)(2,1)}, bf16[512,768]{1,0:T(8,128)(2,1)S(1)}, u32[]{:S(2)}) copy-start(bf16[512,768]{1,0:T(8,128)(2,1)S(1)} %get-tuple-element.94) | copy-start | bytes 2359300
  111.1 0.7 copy-start.13
  113.2 15.1 %all-to-all-start = ((bf16[4,128,768]{2,1,0:T(8,128)(2,1)}), bf16[4,128,768]{2,1,0:T(8,128)(2,1)S(1)}, u32[]{:S(2)}, u32[]{:S(2)}) async-start(bf16[4,128,768]{2,1,0:T(8,128)(2,1)} %bitcast.113), calls=%async_computation | async-start | bytes 1572864 | tf_op jit(solution)/shard_map/all_to_all | solution.py:621
  116.7 97.1 %reduce-scatter.3.cloned.1.call-start = ((), (), s32[]{:S(2)}) async-start(), calls=%async_computation.7 | async-start | bytes 2027520 | tf_op jit(solution)/shard_map/reduce_scatter | solution.py:644
  128.6 8.8 %copy-start.9 = (bf16[3,64,512]{2,1,0:T(8,128)(2,1)S(1)}, bf16[3,64,512]{2,1,0:T(8,128)(2,1)}, u32[]{:S(2)}) copy-start(bf16[3,64,512]{2,1,0:T(8,128)(2,1)} %get-tuple-element.69) | copy-start | bytes 589828
  128.9 9.6 %copy-start.11 = (bf16[3,128,768]{2,1,0:T(8,128)(2,1)S(1)}, bf16[3,128,768]{2,1,0:T(8,128)(2,1)}, u32[]{:S(2)}) copy-start(bf16[3,128,768]{2,1,0:T(8,128)(2,1)} %pad.13) | copy-start | bytes 1769476
  158.3 15.7 %copy-start.3 = (bf16[768,640]{1,0:T(8,128)(2,1)S(1)}, bf16[768,640]{1,0:T(8,128)(2,1)}, u32[]{:S(2)}) copy-start(bf16[768,640]{1,0:T(8,128)(2,1)} %weight_grad.1) | copy-start | bytes 2949124
  160.2 13.7 %collective-permute-start.4 = (bf16[4,96,640]{2,1,0:T(8,128)(2,1)}, bf16[4,96,640]{2,1,0:T(8,128)(2,1)}, u32[]{:S(2)}, u32[]{:S(2)}) collective-permute-start(bf16[4,96,640]{2,1,0:T(8,128)(2,1)} %dynamic-slice_bitcast_fusion), channel_id=1, source_target_pairs={{0,16},{16,0},{1,17},{17,1},{2,18},{18,2},{3,19},{19,3},{4,20},{20... | collective-permute-start | bytes 1474568 | tf_op jit(solution)/shard_map/ppermute | solution.py:482
  161.7 22.4 %all-to-all-start.1 = ((bf16[4,48,768]{2,1,0:T(8,128)(2,1)}), bf16[4,48,768]{2,1,0:T(8,128)(2,1)}, u32[]{:S(2)}, u32[]{:S(2)}) async-start(bf16[4,48,768]{2,1,0:T(8,128)(2,1)} %bitcast.109), calls=%async_computation.2 | async-start | bytes 589824 | tf_op jit(solution)/shard_map/all_to_all | solution.py:647
  184.1 27.8 %all-to-all-start.2 = ((bf16[4,96,640]{2,1,0:T(8,128)(2,1)}), bf16[4,96,640]{2,1,0:T(8,128)(2,1)S(1)}, u32[]{:S(2)}, u32[]{:S(2)}) async-start(bf16[4,96,640]{2,1,0:T(8,128)(2,1)} %fusion.8), calls=%async_computation.3 | async-start | bytes 983040 | tf_op jit(solution)/shard_map/all_to_all | solution.py:504
  187.6 104.4 %all-gather.7.cloned.1.call-start = ((), (), s32[]{:S(2)}) async-start(), calls=%async_computation.10 | async-start | bytes 8773632 | tf_op jit(solution)/shard_map/all_gather | solution.py:657
  188.6 5.2 %collective-permute-start.6 = (bf16[48,768]{1,0:T(8,128)(2,1)S(1)}, bf16[48,768]{1,0:T(8,128)(2,1)S(1)}, u32[]{:S(2)}, u32[]{:S(2)}) collective-permute-start(bf16[48,768]{1,0:T(8,128)(2,1)S(1)} %reduce_sum.179), channel_id=1, source_target_pairs={{0,16},{16,0},{1,17},{17,1},{2,18},{18,2},{3,19},{19,3},{4,20},{20... | collective-permute-start | bytes 221192 | tf_op jit(solution)/shard_map/ppermute | solution.py:499
  190.8 23.0 %copy-start.2 = (bf16[1,128,768]{2,1,0:T(8,128)(2,1)S(1)}, bf16[1,128,768]{2,1,0:T(8,128)(2,1)}, u32[]{:S(2)}) copy-start(bf16[1,128,768]{2,1,0:T(8,128)(2,1)} %param.11) | copy-start | bytes 589828
  190.8 21.1 %collective-permute-start.5 = (bf16[192,768]{1,0:T(8,128)(2,1)}, bf16[192,768]{1,0:T(8,128)(2,1)S(1)}, u32[]{:S(2)}, u32[]{:S(2)}) collective-permute-start(bf16[192,768]{1,0:T(8,128)(2,1)} %dynamic-slice_bitcast_fusion.1), channel_id=1, source_target_pairs={{0,16},{16,0},{1,17},{17,1},{2,18},{18,2},{3,19},{19,3},{4,20},{20... | collective-permute-start | bytes 884744 | tf_op jit(solution)/shard_map/ppermute | solution.py:482
  214.0 7.6 %copy-start.15 = (bf16[512,768]{1,0:T(8,128)(2,1)S(1)}, bf16[512,768]{1,0:T(8,128)(2,1)}, u32[]{:S(2)}) copy-start(bf16[512,768]{1,0:T(8,128)(2,1)} %copy-done.14) | copy-start | bytes 2359300
  217.3 21.4 %all-to-all-start.4 = ((bf16[4,128,768]{2,1,0:T(8,128)(2,1)}), bf16[4,128,768]{2,1,0:T(8,128)(2,1)}, u32[]{:S(2)}, u32[]{:S(2)}) async-start(bf16[4,128,768]{2,1,0:T(8,128)(2,1)} %bitcast.106), calls=%async_computation.6 | async-start | bytes 1572864 | tf_op jit(solution)/shard_map/all_to_all | solution.py:504
  238.7 18.8 %all-to-all-start.3 = ((bf16[4,128,768]{2,1,0:T(8,128)(2,1)}), bf16[4,128,768]{2,1,0:T(8,128)(2,1)}, u32[]{:S(2)}, u32[]{:S(2)}) async-start(bf16[4,128,768]{2,1,0:T(8,128)(2,1)} %bitcast.29), calls=%async_computation.5 | async-start | bytes 1572864 | tf_op jit(solution)/shard_map/all_to_all | solution.py:504
  292.0 10.6 %copy-start.1 = (bf16[384,2304]{1,0:T(8,128)(2,1)S(1)}, bf16[384,2304]{1,0:T(8,128)(2,1)}, u32[]{:S(2)}) copy-start(bf16[384,2304]{1,0:T(8,128)(2,1)} %param.16) | copy-start | bytes 5308420
Sparse Core Ops, SparseCore 0:
  10.3 49.9 all-gather.4
  111.3 48.0 reduce-scatter.4
  162.2 47.8 reduce-scatter.2
  214.0 77.9 all-gather.6

commit v8 on v7

--- a/solution.py
+++ b/solution.py
@@ -641,7 +641,6 @@
     query_grads, pair_grads, turned, query_turned, gates = attend_back(
         ctx_count, base, query_slot, grad_wide, pairs, prob
     )
-    pair_mine = lax.psum_scatter(pair_grads, "ctx", scatter_dimension=0, tiled=False)
     small = weight_grad(turned, query_turned, gates, score_rows, norm_slot, norm_one, all_in, gain_cols)
     small, out_mine = lax.optimization_barrier((small, out_mine))
     out_came = lax.all_to_all(
@@ -653,7 +652,9 @@
     small_own = jnp.pad(exchange_sum(small_dp, "ctx").astype(bf16), ((0, 0), (0, width - wide)))
     out_own = dp_sum(jnp.sum(out_came.astype(f32), axis=0).astype(bf16))
     gradients = jnp.concatenate([small_own, dp_scatter(mlp_ctx), out_own], axis=0)
-    pair_mine, gradients, active_late = lax.optimization_barrier((pair_mine, gradients, active))
+    pair_grads, gradients, active_late = lax.optimization_barrier((pair_grads, gradients, active))
+    pair_mine = exchange_sum(pair_grads, "ctx").astype(bf16)
+    pair_mine, active_late = lax.optimization_barrier((pair_mine, active_late))
     gathered = lax.all_gather(gradients, ("sp", "ctx"), axis=0, tiled=False).reshape(seg_count, ctx_count, -1, width)
     proj_piece = hidden // (seg_count * dp_count * ctx_count)
 

time: 310 us -> 320 us (1.032)
  waiting for transfers between devices: 120 us -> 129 us
  starting transfers between devices: 30.8 us -> 34.5 us
    all_to_all x3 -> x4, waiting for transfers between devices: 44.6 us -> 91.1 us  [exchange_sum(): came = lax.all_to_all(parts, axis, split_axis=0, concat_axis=0, tiled=True)]
    all_gather x1, waiting for transfers between devices: 32.1 us -> 2 us  [per_device(): lax.all_gather(gradients, ('sp', 'ctx'), axis=0, tiled=False)]
    all_to_all x1, waiting for transfers between devices: 8.24 us -> 0.76 us  [per_device(): lax.all_to_all(out_mine.reshape(ctx_count, -1, width), 'ctx', split_axis=...]
    all_to_all x3 -> x4, starting transfers between devices: 11.9 us -> 15.6 us  [exchange_sum(): came = lax.all_to_all(parts, axis, split_axis=0, concat_axis=0, tiled=True)]
  transfers between devices with their start and end apart: 16 -> 16, of which waited for: 10 -> 11; matrix products, arithmetic and copies ran while one was open for 13% -> 11% of each run, Pallas kernels for 16% -> 16%
where the time goes in v8:
time: 320 us; the launch traced here: 318 us
  waiting for transfers between devices  129 us (40%)
  Pallas kernels  59.5 us (19%)
  starting transfers between devices  34.5 us (11%)
  blocking collectives  29.7 us (9%)
  local copies, waits for them, and re-layouts  21.3 us (7%)
  other arithmetic  15.6 us (5%)
  between operations  14.9 us (5%)
  matrix products  13.9 us (4%)
    all_to_all x4, waiting for transfers between devices, exchange_sum(): came = lax.all_to_all(parts, axis, split_axis=0, concat_axis=0, tiled=True)  91.1 us
    pallas_call x1, Pallas kernels, attend(): pl.pallas_call(functools.partial(attend_kernel, parts, chunk), grid_spec=...  20.3 us
    all_to_all x4, starting transfers between devices, exchange_sum(): came = lax.all_to_all(parts, axis, split_axis=0, concat_axis=0, tiled=True)  15.6 us
    all_gather x1, blocking collectives, per_device(): cot_group = lax.all_gather(cot_own, 'sp', axis=0, tiled=True)  12.2 us
    ppermute x3, waiting for transfers between devices, dp_send(): return lax.ppermute(mine, 'dp', [(0, 1), (1, 0)])  11.2 us
    pallas_call x1, Pallas kernels, attend_back(): pl.pallas_call(functools.partial(attend_back_kernel, parts, chunk), grid_...  11.1 us
    all_gather x1, blocking collectives, per_device(): attended_all = lax.all_gather(attended, 'sp', axis=0, tiled=True)  9.26 us
    pallas_call x1, Pallas kernels, unpack(): pl.pallas_call(functools.partial(unpack_kernel, groups, heads, piece, par...  9.2 us
  transfers between devices with their start and end apart: 16, of which 11 were waited for; matrix products, arithmetic and copies ran while one was open for 11% of the time, Pallas kernels for 16%

profile of v8, /device:TPU:0, one launch (start us, length us, event | category | flops | bytes accessed | tf_op | source)
XLA Modules:
  0.0 318.4 jit_solution(3329256142070131599)
XLA Ops:
  12.5 2.1 arrange.1
  14.6 3.0 collective-permute-start
  22.9 6.5 %collective-permute-done = bf16[400,640]{1,0:T(8,128)(2,1)S(1)} collective-permute-done((bf16[400,640]{1,0:T(8,128)(2,1)}, bf16[400,640]{1,0:T(8,128)(2,1)S(1)}, u32[]{:S(2)}, u32[]{:S(2)}) %collective-permute-start) | collective-permute-done | bytes 512032 | tf_op jit(solution)/shard_map/ppermute | solution.py:547
  30.8 1.7 collective-permute-start.1
  33.4 1.7 collective-permute-start.3
  35.7 12.2 %all_gather.19 = bf16[512,768]{1,0:T(8,128)(2,1)} all-gather(bf16[128,768]{1,0:T(8,128)(2,1)S(1)} %bitcast.107), channel_id=1, replica_groups=mesh['dp'=2,'sp'=4,'ctx'=4] {'sp'}, dimensions={0}, use_global_device_ids=true | all-gather | bytes 983040 | tf_op jit(solution)/shard_map/all_gather | solution.py:572
  48.4 11.2 %collective-permute-done.2 = bf16[384,768]{1,0:T(8,128)(2,1)S(1)} collective-permute-done((bf16[384,768]{1,0:T(8,128)(2,1)S(1)}, bf16[384,768]{1,0:T(8,128)(2,1)S(1)}, u32[]{:S(2)}, u32[]{:S(2)}) %collective-permute-start.2) | collective-permute-done | bytes 589856 | tf_op jit(solution)/shard_map/ppermute | solution.py:465
  61.1 7.2 %project.1 = (bf16[2048,768]{1,0:T(8,128)(2,1)}, bf16[2048,384]{1,0:T(8,128)(2,1)}, bf16[2048,384]{1,0:T(8,128)(2,1)}, bf16[3,1,2048]{2,1,0:T(2,128)(2,1)}) custom-call(bf16[2048,768]{1,0:T(8,128)(2,1)} %bitcast.99, f32[1,768]{1,0:T(1,128)} %maximum_convert_fusion.gain_ref, bf16[768,640]{1,0:T(8,128)(2,1)} %pad_maximum_fusion.1.in_ref), custom_call_target="tpu_custom_call" | custom-call | tf_op jit(solution)/shard_map/project/pallas_call | solution.py:73
  68.3 20.3 %attend.1 = (bf16[3,64,512]{2,1,0:T(8,128)(2,1)}, bf16[3,4,128,2048]{3,2,1,0:T(8,128)(2,1)}) custom-call(s32[2]{0:T(128)} %pad_add_fusion.base_ref, s32[3,4,128,64]{3,2,1,0:T(8,128)} %bitcast.104, bf16[2048,384]{1,0:T(8,128)(2,1)} %get-tuple-element.66.refs_1_.q_ref, bf16[2048,384]{1,0:T(8,128)(2,1)} %get-tuple-element.67.refs_2_.kv_ref, ...), custom_call_target="tpu_custom_call" | custom-call | tf_op jit(solution)/shard_map/attend/pallas_call | solution.py:205
  88.6 9.3 %all_gather.20 = bf16[768,512]{1,0:T(8,128)(2,1)S(1)} all-gather(bf16[192,512]{1,0:T(8,128)(2,1)} %bitcast.112), channel_id=1, replica_groups=mesh['dp'=2,'sp'=4,'ctx'=4] {'sp'}, dimensions={0}, use_global_device_ids=true | all-gather | bytes 983040 | tf_op jit(solution)/shard_map/all_gather | solution.py:595
  102.6 3.0 fusion.6
  112.9 3.5 %all-to-all-start = ((bf16[4,128,768]{2,1,0:T(8,128)(2,1)}), bf16[4,128,768]{2,1,0:T(8,128)(2,1)S(1)}, u32[]{:S(2)}, u32[]{:S(2)}) async-start(bf16[4,128,768]{2,1,0:T(8,128)(2,1)} %bitcast.10), calls=%async_computation | async-start | bytes 1572864 | tf_op jit(solution)/shard_map/all_to_all | solution.py:621
  117.8 2.1 constant_dynamic-slice_fusion.1
  119.9 8.1 %all-to-all-done = bf16[4,128,768]{2,1,0:T(8,128)(2,1)S(1)} async-done(((bf16[4,128,768]{2,1,0:T(8,128)(2,1)}), bf16[4,128,768]{2,1,0:T(8,128)(2,1)S(1)}, u32[]{:S(2)}, u32[]{:S(2)}) %all-to-all-start) | async-done | bytes 786464 | tf_op jit(solution)/shard_map/all_to_all | solution.py:621
  129.6 8.2 %all_gather.21 = bf16[512,768]{1,0:T(8,128)(2,1)S(1)} all-gather(bf16[128,768]{1,0:T(8,128)(2,1)S(1)} %fusion.19), channel_id=1, replica_groups=mesh['dp'=2,'sp'=4,'ctx'=4] {'sp'}, dimensions={0}, use_global_device_ids=true | all-gather | bytes 983040 | tf_op jit(solution)/shard_map/all_gather | solution.py:633
  141.1 11.1 %attend_back.1 = (bf16[512,384]{1,0:T(8,128)(2,1)}, bf16[4,528,384]{2,1,0:T(8,128)(2,1)}, bf16[3,128,2048]{2,1,0:T(8,128)(2,1)}, bf16[3,64,512]{2,1,0:T(8,128)(2,1)}, f32[3,8,2048]{2,1,0:T(8,128)}) custom-call(s32[2]{0:T(128)} %pad_add_fusion.base_ref, bf16[2048,384]{1,0:T(8,128)(2,1)} %get-tuple-element.66.refs_1_.q_ref, ...), custom_call_target="tpu_custom_call" | custom-call | tf_op jit(solution)/shard_map/attend_back/pallas_call | solution.py:272
  152.3 6.3 %weight_grad.1 = bf16[768,640]{1,0:T(8,128)(2,1)} custom-call(bf16[3,128,2048]{2,1,0:T(8,128)(2,1)} %get-tuple-element.83.turned_ref, bf16[3,64,512]{2,1,0:T(8,128)(2,1)} %get-tuple-element.84.dq_ref, f32[3,8,2048]{2,1,0:T(8,128)} %get-tuple-element.85.gates_ref, bf16[3,2048]{1,0:T(4,128)(2,1)} %bitcast.117, bf16[2048,768]{1,0:T(8,128)(2,1)} %get-tuple-element.77.slot_ref, ...), custom_call_target="tpu_custom_call" | custom-call | tf_op jit(solution)/shard_map/weight_grad/pallas_call | solution.py:331
  161.3 4.9 %all-to-all-start.1 = ((bf16[4,48,768]{2,1,0:T(8,128)(2,1)}), bf16[4,48,768]{2,1,0:T(8,128)(2,1)S(1)}, u32[]{:S(2)}, u32[]{:S(2)}) async-start(bf16[4,48,768]{2,1,0:T(8,128)(2,1)} %bitcast.20), calls=%async_computation.1 | async-start | bytes 589824 | tf_op jit(solution)/shard_map/all_to_all | solution.py:646
  166.2 7.2 %collective-permute-done.4 = bf16[4,96,640]{2,1,0:T(8,128)(2,1)} collective-permute-done((bf16[4,96,640]{2,1,0:T(8,128)(2,1)S(1)}, bf16[4,96,640]{2,1,0:T(8,128)(2,1)}, u32[]{:S(2)}, u32[]{:S(2)}) %collective-permute-start.4) | collective-permute-done | bytes 491552 | tf_op jit(solution)/shard_map/ppermute | solution.py:482
  173.4 1.9 fusion.8
  176.1 4.2 %all-to-all-start.2 = ((bf16[4,96,640]{2,1,0:T(8,128)(2,1)}), bf16[4,96,640]{2,1,0:T(8,128)(2,1)S(1)}, u32[]{:S(2)}, u32[]{:S(2)}) async-start(bf16[4,96,640]{2,1,0:T(8,128)(2,1)} %fusion.8), calls=%async_computation.2 | async-start | bytes 983040 | tf_op jit(solution)/shard_map/all_to_all | solution.py:504
  184.9 8.8 %all-to-all-done.2 = bf16[4,96,640]{2,1,0:T(8,128)(2,1)S(1)} async-done(((bf16[4,96,640]{2,1,0:T(8,128)(2,1)}), bf16[4,96,640]{2,1,0:T(8,128)(2,1)S(1)}, u32[]{:S(2)}, u32[]{:S(2)}) %all-to-all-start.2) | async-done | bytes 491552 | tf_op jit(solution)/shard_map/all_to_all | solution.py:504
  194.8 3.7 %all-to-all-start.3 = ((bf16[4,528,384]{2,1,0:T(8,128)(2,1)}), bf16[4,528,384]{2,1,0:T(8,128)(2,1)S(1)}, u32[]{:S(2)}, u32[]{:S(2)}) async-start(bf16[4,528,384]{2,1,0:T(8,128)(2,1)} %get-tuple-element.96), calls=%async_computation.4 | async-start | bytes 3244032 | tf_op jit(solution)/shard_map/all_to_all | solution.py:504
  198.6 54.0 %all-to-all-done.3 = bf16[4,528,384]{2,1,0:T(8,128)(2,1)S(1)} async-done(((bf16[4,528,384]{2,1,0:T(8,128)(2,1)}), bf16[4,528,384]{2,1,0:T(8,128)(2,1)S(1)}, u32[]{:S(2)}, u32[]{:S(2)}) %all-to-all-start.3) | async-done | bytes 1622048 | tf_op jit(solution)/shard_map/all_to_all | solution.py:504
  253.7 3.3 %finish.1 = bf16[512,768]{1,0:T(8,128)(2,1)} custom-call(bf16[528,384]{1,0:T(8,128)(2,1)} %reduce_sum.192.pair_ref, bf16[512,384]{1,0:T(8,128)(2,1)} %get-tuple-element.100.dq_ref, bf16[3,512]{1,0:T(4,128)(2,1)} %bitcast.118, bf16[768,640]{1,0:T(8,128)(2,1)} %pad_maximum_fusion.1.in_ref), custom_call_target="tpu_custom_call" | custom-call | tf_op jit(solution)/shard_map/finish/pallas_call | solution.py:364
  257.0 3.5 %all-to-all-start.5 = ((bf16[4,128,768]{2,1,0:T(8,128)(2,1)}), bf16[4,128,768]{2,1,0:T(8,128)(2,1)S(1)}, u32[]{:S(2)}, u32[]{:S(2)}) async-start(bf16[4,128,768]{2,1,0:T(8,128)(2,1)} %bitcast.105), calls=%async_computation.6 | async-start | bytes 1572864 | tf_op jit(solution)/shard_map/all_to_all | solution.py:504
  260.6 3.2 %convolution_convert_fusion.2 = bf16[512,768]{1,0:T(8,128)(2,1)} fusion(bf16[512,768]{1,0:T(8,128)(2,1)} %copy-done.25, bf16[384,768]{1,0:T(8,128)(2,1)} %collective-permute-done.3, bf16[384,768]{1,0:T(8,128)(2,1)S(1)} %copy-done.15, pred[]{:T(512)S(6)} %eq.5), kind=kOutput, calls=%fused_computation.19 | convolution fusion | flops 609681408 | bytes 2752513 | tf_op jit(solution)/shard_map/dot_general | solution.py:663
  263.8 17.2 %all-to-all-done.5 = bf16[4,128,768]{2,1,0:T(8,128)(2,1)S(1)} async-done(((bf16[4,128,768]{2,1,0:T(8,128)(2,1)}), bf16[4,128,768]{2,1,0:T(8,128)(2,1)S(1)}, u32[]{:S(2)}, u32[]{:S(2)}) %all-to-all-start.5) | async-done | bytes 786464 | tf_op jit(solution)/shard_map/all_to_all | solution.py:504
  281.0 4.2 %all-to-all-start.4 = ((bf16[4,128,768]{2,1,0:T(8,128)(2,1)}), bf16[4,128,768]{2,1,0:T(8,128)(2,1)}, u32[]{:S(2)}, u32[]{:S(2)}) async-start(bf16[4,128,768]{2,1,0:T(8,128)(2,1)} %bitcast.28), calls=%async_computation.5 | async-start | bytes 1572864 | tf_op jit(solution)/shard_map/all_to_all | solution.py:504
  285.9 11.0 %all-to-all-done.4 = bf16[4,128,768]{2,1,0:T(8,128)(2,1)} async-done(((bf16[4,128,768]{2,1,0:T(8,128)(2,1)}), bf16[4,128,768]{2,1,0:T(8,128)(2,1)}, u32[]{:S(2)}, u32[]{:S(2)}) %all-to-all-start.4) | async-done | bytes 786464 | tf_op jit(solution)/shard_map/all_to_all | solution.py:504
  299.2 2.0 all-gather.7.cloned.1.call-done
  301.2 9.2 %unpack.1 = (f32[384,2304]{1,0:T(8,128)}, f32[12,384]{1,0:T(8,128)}, f32[8,384]{1,0:T(8,128)}, f32[384,3072]{1,0:T(8,128)}, f32[4,4,96,768]{3,2,1,0:T(8,128)}, /*index=5*/f32[2,4,48,768]{3,2,1,0:T(8,128)}) custom-call(s32[1]{0:T(128)} %bitcast.33.dp_ref, bf16[4,4,336,768]{3,2,1,0:T(8,128)(2,1)} %bitcast.98), custom_call_target="tpu_custom_call" | custom-call | tf_op jit(solution)/shard_map/unpack/pallas_call | solution.py:426
  (144 shorter events, 47.4 us)
Async XLA Ops:
  7.2 11.0 %copy-start.17 = (s32[1,4,128,3,64]{2,4,3,1,0:T(8,128)S(1)}, s32[1,4,128,3,64]{2,4,3,1,0:T(8,128)}, u32[]{:S(2)}) copy-start(s32[1,4,128,3,64]{2,4,3,1,0:T(8,128)} %param.14) | copy-start | bytes 1179652
  7.2 53.9 %all-gather.5.cloned.1.call-start = ((), (), s32[]{:S(2)}) async-start(), calls=%async_computation.8 | async-start | bytes 3342336 | tf_op jit(solution)/shard_map/all_gather | solution.py:553
  7.9 173.9 %reduce-scatter.2.cloned.1.call-start = ((), (), s32[]{:S(2)}) async-start(), calls=%async_computation.7 | async-start | bytes 2949120 | tf_op jit(solution)/shard_map/reduce_scatter | solution.py:618
  14.6 14.8 %collective-permute-start = (bf16[400,640]{1,0:T(8,128)(2,1)}, bf16[400,640]{1,0:T(8,128)(2,1)S(1)}, u32[]{:S(2)}, u32[]{:S(2)}) collective-permute-start(bf16[400,640]{1,0:T(8,128)(2,1)} %arrange.1), channel_id=1, source_target_pairs={{0,16},{16,0},{1,17},{17,1},{2,18},{18,2},{3,19},{19,3},{4,20},{20... | collective-permute-start | bytes 1536008 | tf_op jit(solution)/shard_map/ppermute | solution.py:547
  20.5 8.9 %copy-start.6 = (bf16[400,640]{1,0:T(8,128)(2,1)S(1)}, bf16[400,640]{1,0:T(8,128)(2,1)}, u32[]{:S(2)}) copy-start(bf16[400,640]{1,0:T(8,128)(2,1)} %arrange.1) | copy-start | bytes 1536004
  22.9 79.7 %copy-start.14 = (bf16[384,768]{1,0:T(8,128)(2,1)}, bf16[384,768]{1,0:T(8,128)(2,1)S(1)}, u32[]{:S(2)}) copy-start(bf16[384,768]{1,0:T(8,128)(2,1)S(1)} %get-tuple-element.70) | copy-start | bytes 1769476
  30.8 17.2 %collective-permute-start.1 = (bf16[384,768]{1,0:T(8,128)(2,1)S(1)}, bf16[384,768]{1,0:T(8,128)(2,1)S(1)}, u32[]{:S(2)}, u32[]{:S(2)}) collective-permute-start(bf16[384,768]{1,0:T(8,128)(2,1)S(1)} %copy-done.13), channel_id=1, source_target_pairs={{0,16},{16,0},{1,17},{17,1},{2,18},{18,2},{3,19},{19,3},{4,20},{20... | collective-permute-start | bytes 1769480 | tf_op jit(solution)/shard_map/ppermute | solution.py:465
  33.1 26.5 %collective-permute-start.2 = (bf16[384,768]{1,0:T(8,128)(2,1)S(1)}, bf16[384,768]{1,0:T(8,128)(2,1)S(1)}, u32[]{:S(2)}, u32[]{:S(2)}) collective-permute-start(bf16[384,768]{1,0:T(8,128)(2,1)S(1)} %get-tuple-element.62), channel_id=1, source_target_pairs={{0,16},{16,0},{1,17},{17,1},{2,18},{18,2},{3,19},{19,3},{4,20},{20... | collective-permute-start | bytes 1769480 | tf_op jit(solution)/shard_map/ppermute | solution.py:465
  33.4 55.2 %collective-permute-start.3 = (bf16[384,768]{1,0:T(8,128)(2,1)S(1)}, bf16[384,768]{1,0:T(8,128)(2,1)}, u32[]{:S(2)}, u32[]{:S(2)}) collective-permute-start(bf16[384,768]{1,0:T(8,128)(2,1)S(1)} %get-tuple-element.70), channel_id=1, source_target_pairs={{0,16},{16,0},{1,17},{17,1},{2,18},{18,2},{3,19},{19,3},{4,20},{20... | collective-permute-start | bytes 1769480 | tf_op jit(solution)/shard_map/ppermute | solution.py:465
  48.4 50.6 %copy-start.7 = (bf16[768,768]{1,0:T(8,128)(2,1)}, bf16[768,768]{1,0:T(8,128)(2,1)S(1)}, u32[]{:S(2)}) copy-start(bf16[768,768]{1,0:T(8,128)(2,1)S(1)} %maximum_select_fusion) | copy-start | bytes 3538948
  110.9 17.8 %copy-start.20 = (pred[128]{0:T(512)(128)(4,1)}, pred[128]{0:T(512)(128)(4,1)S(1)}, u32[]{:S(2)}) copy-start(pred[128]{0:T(512)(128)(4,1)S(1)} %add_compare_fusion) | copy-start | bytes 388
  112.9 15.1 %all-to-all-start = ((bf16[4,128,768]{2,1,0:T(8,128)(2,1)}), bf16[4,128,768]{2,1,0:T(8,128)(2,1)S(1)}, u32[]{:S(2)}, u32[]{:S(2)}) async-start(bf16[4,128,768]{2,1,0:T(8,128)(2,1)} %bitcast.10), calls=%async_computation | async-start | bytes 1572864 | tf_op jit(solution)/shard_map/all_to_all | solution.py:621
  128.4 9.4 %copy-start.12 = (bf16[3,64,512]{2,1,0:T(8,128)(2,1)S(1)}, bf16[3,64,512]{2,1,0:T(8,128)(2,1)}, u32[]{:S(2)}) copy-start(bf16[3,64,512]{2,1,0:T(8,128)(2,1)} %get-tuple-element.71) | copy-start | bytes 589828
  128.6 11.5 %copy-start.22 = (f32[128]{0:T(128)}, f32[128]{0:T(128)S(1)}, u32[]{:S(2)}) copy-start(f32[128]{0:T(128)S(1)} %negate_multiply_fusion.1) | copy-start | bytes 1540
  158.6 14.8 %copy-start.3 = (bf16[768,640]{1,0:T(8,128)(2,1)S(1)}, bf16[768,640]{1,0:T(8,128)(2,1)}, u32[]{:S(2)}) copy-start(bf16[768,640]{1,0:T(8,128)(2,1)} %weight_grad.1) | copy-start | bytes 2949124
  159.7 13.7 %collective-permute-start.4 = (bf16[4,96,640]{2,1,0:T(8,128)(2,1)S(1)}, bf16[4,96,640]{2,1,0:T(8,128)(2,1)}, u32[]{:S(2)}, u32[]{:S(2)}) collective-permute-start(bf16[4,96,640]{2,1,0:T(8,128)(2,1)S(1)} %dynamic-slice_bitcast_fusion), channel_id=1, source_target_pairs={{0,16},{16,0},{1,17},{17,1},{2,18},{18,2},{3,19},{19,3},{4,20},{20... | collective-permute-start | bytes 1474568 | tf_op jit(solution)/shard_map/ppermute | solution.py:482
  161.3 14.8 %all-to-all-start.1 = ((bf16[4,48,768]{2,1,0:T(8,128)(2,1)}), bf16[4,48,768]{2,1,0:T(8,128)(2,1)S(1)}, u32[]{:S(2)}, u32[]{:S(2)}) async-start(bf16[4,48,768]{2,1,0:T(8,128)(2,1)} %bitcast.20), calls=%async_computation.1 | async-start | bytes 589824 | tf_op jit(solution)/shard_map/all_to_all | solution.py:646
  176.1 17.7 %all-to-all-start.2 = ((bf16[4,96,640]{2,1,0:T(8,128)(2,1)}), bf16[4,96,640]{2,1,0:T(8,128)(2,1)S(1)}, u32[]{:S(2)}, u32[]{:S(2)}) async-start(bf16[4,96,640]{2,1,0:T(8,128)(2,1)} %fusion.8), calls=%async_computation.2 | async-start | bytes 983040 | tf_op jit(solution)/shard_map/all_to_all | solution.py:504
  180.2 121.0 %all-gather.7.cloned.1.call-start = ((), (), s32[]{:S(2)}) async-start(), calls=%async_computation.9 | async-start | bytes 8773632 | tf_op jit(solution)/shard_map/all_gather | solution.py:658
  180.3 4.6 %collective-permute-start.6 = (bf16[48,768]{1,0:T(8,128)(2,1)S(1)}, bf16[48,768]{1,0:T(8,128)(2,1)S(1)}, u32[]{:S(2)}, u32[]{:S(2)}) collective-permute-start(bf16[48,768]{1,0:T(8,128)(2,1)S(1)} %reduce_sum.191), channel_id=1, source_target_pairs={{0,16},{16,0},{1,17},{17,1},{2,18},{18,2},{3,19},{19,3},{4,20},{20... | collective-permute-start | bytes 221192 | tf_op jit(solution)/shard_map/ppermute | solution.py:499
  181.8 12.0 %copy-start.16 = (bf16[1,384,768]{2,1,0:T(8,128)(2,1)S(1)}, bf16[1,384,768]{2,1,0:T(8,128)(2,1)}, u32[]{:S(2)}) copy-start(bf16[1,384,768]{2,1,0:T(8,128)(2,1)} %reduce-scatter.2.cloned.1.call-done) | copy-start | bytes 1769476
  182.9 10.9 %collective-permute-start.5 = (bf16[192,768]{1,0:T(8,128)(2,1)S(1)}, bf16[192,768]{1,0:T(8,128)(2,1)S(1)}, u32[]{:S(2)}, u32[]{:S(2)}) collective-permute-start(bf16[192,768]{1,0:T(8,128)(2,1)S(1)} %dynamic-slice_bitcast_fusion.1), channel_id=1, source_target_pairs={{0,16},{16,0},{1,17},{17,1},{2,18},{18,2},{3,19},{19,3},{4,20},{20... | collective-permute-start | bytes 884744 | tf_op jit(solution)/shard_map/ppermute | solution.py:482
  194.8 57.8 %all-to-all-start.3 = ((bf16[4,528,384]{2,1,0:T(8,128)(2,1)}), bf16[4,528,384]{2,1,0:T(8,128)(2,1)S(1)}, u32[]{:S(2)}, u32[]{:S(2)}) async-start(bf16[4,528,384]{2,1,0:T(8,128)(2,1)} %get-tuple-element.96), calls=%async_computation.4 | async-start | bytes 3244032 | tf_op jit(solution)/shard_map/all_to_all | solution.py:504
  253.7 6.8 %copy-start.19 = (bf16[384]{0:T(512)(128)(2,1)S(1)}, bf16[384]{0:T(512)(128)(2,1)}, u32[]{:S(2)}) copy-start(bf16[384]{0:T(512)(128)(2,1)} %get-tuple-element.140) | copy-start | bytes 2308
  253.7 6.9 %copy-start.15 = (bf16[384,768]{1,0:T(8,128)(2,1)S(1)}, bf16[384,768]{1,0:T(8,128)(2,1)}, u32[]{:S(2)}) copy-start(bf16[384,768]{1,0:T(8,128)(2,1)} %copy-done.14) | copy-start | bytes 1769476
  257.0 23.9 %all-to-all-start.5 = ((bf16[4,128,768]{2,1,0:T(8,128)(2,1)}), bf16[4,128,768]{2,1,0:T(8,128)(2,1)S(1)}, u32[]{:S(2)}, u32[]{:S(2)}) async-start(bf16[4,128,768]{2,1,0:T(8,128)(2,1)} %bitcast.105), calls=%async_computation.6 | async-start | bytes 1572864 | tf_op jit(solution)/shard_map/all_to_all | solution.py:504
  281.0 15.9 %all-to-all-start.4 = ((bf16[4,128,768]{2,1,0:T(8,128)(2,1)}), bf16[4,128,768]{2,1,0:T(8,128)(2,1)}, u32[]{:S(2)}, u32[]{:S(2)}) async-start(bf16[4,128,768]{2,1,0:T(8,128)(2,1)} %bitcast.28), calls=%async_computation.5 | async-start | bytes 1572864 | tf_op jit(solution)/shard_map/all_to_all | solution.py:504
  285.2 13.0 %copy-start.5 = (f32[128,768]{1,0:T(8,128)S(1)}, f32[128,768]{1,0:T(8,128)}, u32[]{:S(2)}) copy-start(f32[128,768]{1,0:T(8,128)} %copy-done.4) | copy-start | bytes 1179652
  285.2 13.0 %copy-start.9 = (bf16[1,128,768]{2,1,0:T(8,128)(2,1)S(1)}, bf16[1,128,768]{2,1,0:T(8,128)(2,1)}, u32[]{:S(2)}) copy-start(bf16[1,128,768]{2,1,0:T(8,128)(2,1)} %param.12) | copy-start | bytes 589828
  285.2 13.0 %copy-start.21 = (pred[128]{0:T(512)(128)(4,1)S(1)}, pred[128]{0:T(512)(128)(4,1)}, u32[]{:S(2)}) copy-start(pred[128]{0:T(512)(128)(4,1)} %copy-done.20) | copy-start | bytes 388
  285.3 13.0 %copy-start.23 = (f32[128]{0:T(128)S(1)}, f32[128]{0:T(128)}, u32[]{:S(2)}) copy-start(f32[128]{0:T(128)} %copy-done.22) | copy-start | bytes 1540
  301.2 10.6 %copy-start.1 = (bf16[384,2304]{1,0:T(8,128)(2,1)S(1)}, bf16[384,2304]{1,0:T(8,128)(2,1)}, u32[]{:S(2)}) copy-start(bf16[384,2304]{1,0:T(8,128)(2,1)} %param.16) | copy-start | bytes 5308420
  (10 other events, 25.3 us)
Sparse Core Ops, SparseCore 0:
  10.3 50.4 all-gather.4
  111.0 48.0 reduce-scatter.1
  194.9 106.3 all-gather.6
